TPU v7x, 32 devices: a whole 2x2x4 slice. The times are simulated.
32 devices in a mesh: seq: 2 (over core), fsdp: 16 (over z, y, x).
Axes of the slice: x: 2, y: 2, z: 4, core: 2. Of those that a mesh axis runs over, the one named last changes fastest.
Arguments:
- byte_inputs: bfloat16 [16, 2048, 768], P('fsdp', 'seq'), may hold values from -6 to 6
- segment_ids: int32 [16, 256], P('fsdp'), may hold values from 0 to 31, never falling along the last dimension, each value on 1 to 128 neighbouring positions
- cotangent: bfloat16 [16, 2048, 768], P('fsdp', 'seq'), may hold values from -6 to 6
- patch_weight: bfloat16 [6144, 768], P('fsdp'), may hold values from -0.078125 to 0.078125
- coarse_first_gain: bfloat16 [768], P('fsdp'), may hold values from 0.25 to 1.75
- coarse_first_bias: bfloat16 [768], P('fsdp'), may hold values from -3 to 3
- coarse_project: bfloat16 [768, 2304], P('fsdp'), may hold values from -0.21875 to 0.21875
- coarse_output: bfloat16 [768, 768], P(None, 'fsdp'), may hold values from -0.875 to 0.875
- coarse_second_gain: bfloat16 [768], P('fsdp'), may hold values from 0.25 to 1.75
- coarse_second_bias: bfloat16 [768], P('fsdp'), may hold values from -3 to 3
- coarse_expand: bfloat16 [768, 3072], P('fsdp'), may hold values from -0.21875 to 0.21875
- coarse_narrow: bfloat16 [3072, 768], P(None, 'fsdp'), may hold values from -0.15625 to 0.15625
- fine_first_gain: bfloat16 [768], P('fsdp'), may hold values from 0.25 to 1.75
- fine_first_bias: bfloat16 [768], P('fsdp'), may hold values from -3 to 3
- fine_project: bfloat16 [768, 2304], P('fsdp'), may hold values from -0.21875 to 0.21875
- fine_output: bfloat16 [768, 768], P(None, 'fsdp'), may hold values from -0.4375 to 0.4375
- fine_second_gain: bfloat16 [768], P('fsdp'), may hold values from 0.25 to 1.75
- fine_second_bias: bfloat16 [768], P('fsdp'), may hold values from -3 to 3
- fine_expand: bfloat16 [768, 3072], P('fsdp'), may hold values from -0.21875 to 0.21875
- fine_narrow: bfloat16 [3072, 768], P(None, 'fsdp'), may hold values from -0.15625 to 0.15625
Outputs:
- layer_output: bfloat16 [16, 2048, 768], P('fsdp', 'seq')
- input_gradient: bfloat16 [16, 2048, 768], P('fsdp', 'seq')
- gradient_patch_weight: float32 [6144, 768], P('fsdp')
- gradient_coarse_first_gain: float32 [768], P('fsdp')
- gradient_coarse_first_bias: float32 [768], P('fsdp')
- gradient_coarse_project: float32 [768, 2304], P('fsdp')
- gradient_coarse_output: float32 [768, 768], P(None, 'fsdp')
- gradient_coarse_second_gain: float32 [768], P('fsdp')
- gradient_coarse_second_bias: float32 [768], P('fsdp')
- gradient_coarse_expand: float32 [768, 3072], P('fsdp')
- gradient_coarse_narrow: float32 [3072, 768], P(None, 'fsdp')
- gradient_fine_first_gain: float32 [768], P('fsdp')
- gradient_fine_first_bias: float32 [768], P('fsdp')
- gradient_fine_project: float32 [768, 2304], P('fsdp')
- gradient_fine_output: float32 [768, 768], P(None, 'fsdp')
- gradient_fine_second_gain: float32 [768], P('fsdp')
- gradient_fine_second_bias: float32 [768], P('fsdp')
- gradient_fine_expand: float32 [768, 3072], P('fsdp')
- gradient_fine_narrow: float32 [3072, 768], P(None, 'fsdp')
Inputs may be any that keep to these rules, and one draw needn't show every extreme that they name: `segment_ids`: along each sequence the document number never falls from one patch to the next, starting at 0; a document covers at most 128 patches.
All inputs are finite; a program needn't handle non-finite values.
Results may differ from a plain program's by a relative error of at most 0.018.
Values may be sent and summed in bfloat16 or wider, within the bound.
A program may use at most 256 MiB of HBM per device.

v0:
```python
import math

import jax
import jax.numpy as jnp
from jax import lax
from jax.sharding import PartitionSpec as P

D = 768
HEAD_DIM = 64
PATCH = 8


epsilon = 1e-05


def shifted(block, axis, distance):
    devices = range(lax.axis_size(axis))
    route = [(i - distance, i) for i in devices if i - distance in devices]
    return lax.ppermute(block, axis, route)


def layer_norm(values, norm_gain, norm_bias):
    center = jnp.mean(values, -1, keepdims=True)
    centred = values - center
    spread = jnp.mean(centred * centred, -1, keepdims=True)
    return centred * lax.rsqrt(spread + epsilon) * norm_gain + norm_bias


def smooth_gate(values):
    return jax.nn.gelu(values, approximate=True)


def product(left_side, right_side):
    return jnp.dot(left_side, right_side, preferred_element_type=jnp.float32)


def left_product(left_side, right_side):
    return lax.dot_general(
        left_side, right_side, (((0,), (0,)), ((), ())), preferred_element_type=jnp.float32
    )


def right_product(left_side, right_side):
    return lax.dot_general(
        left_side, right_side, (((1,), (1,)), ((), ())), preferred_element_type=jnp.float32
    )


def attend_forward(queries, key_part, value_part, allowed):
    factor = 1.0 / math.sqrt(HEAD_DIM)
    scores = (
        jnp.einsum("bqhd,bkhd->bhqk", queries, key_part, preferred_element_type=jnp.float32)
        * factor
    )
    scores = jnp.where(allowed[:, None], scores, -1e30)
    highest = jnp.max(scores, -1, keepdims=True)
    log_total = highest + jnp.log(jnp.sum(jnp.exp(scores - highest), -1, keepdims=True))
    rounded = jnp.exp(scores - log_total).astype(jnp.bfloat16)
    mixture = jnp.einsum("bhqk,bkhd->bqhd", rounded, value_part, preferred_element_type=jnp.float32)
    return (mixture, log_total)


def attend_backward(queries, key_part, value_part, allowed, log_total, grad_mixture):
    factor = 1.0 / math.sqrt(HEAD_DIM)
    scores = (
        jnp.einsum("bqhd,bkhd->bhqk", queries, key_part, preferred_element_type=jnp.float32)
        * factor
    )
    scores = jnp.where(allowed[:, None], scores, -1e30)
    chances = jnp.exp(scores - log_total)
    rounded = chances.astype(jnp.bfloat16)
    grad_values = jnp.einsum(
        "bhqk,bqhd->bkhd", rounded, grad_mixture, preferred_element_type=jnp.float32
    )
    grad_chances = jnp.einsum(
        "bqhd,bkhd->bhqk", grad_mixture, value_part, preferred_element_type=jnp.float32
    )
    grad_scores = (
        chances * (grad_chances - jnp.sum(grad_chances * chances, -1, keepdims=True))
    ).astype(jnp.bfloat16)
    grad_queries = (
        jnp.einsum("bhqk,bkhd->bqhd", grad_scores, key_part, preferred_element_type=jnp.float32)
        * factor
    )
    grad_keys = (
        jnp.einsum("bhqk,bqhd->bkhd", grad_scores, queries, preferred_element_type=jnp.float32)
        * factor
    )
    return (grad_queries, grad_keys, grad_values)


def block_forward(inputs, weights, attend):
    first_gain, first_bias, project, output, second_gain, second_bias, expand, narrow = weights
    normed = layer_norm(
        inputs, first_gain.astype(jnp.float32), first_bias.astype(jnp.float32)
    ).astype(jnp.bfloat16)
    triple = product(normed, project).astype(jnp.bfloat16)
    mixture, attend_stored = attend(triple)
    middle = inputs + product(mixture, output)
    second = layer_norm(
        middle, second_gain.astype(jnp.float32), second_bias.astype(jnp.float32)
    ).astype(jnp.bfloat16)
    lifted = product(second, expand)
    hidden = smooth_gate(lifted).astype(jnp.bfloat16)
    result = middle + product(hidden, narrow)
    stored = (inputs, normed, attend_stored, mixture, middle, second, lifted, hidden)
    return (result, stored)


def block_backward(grad_result, weights, stored, attend_back):
    first_gain, first_bias, project, output, second_gain, second_bias, expand, narrow = weights
    inputs, normed, attend_stored, mixture, middle, second, lifted, hidden = stored
    grad_branch = grad_result.astype(jnp.bfloat16)
    grad_narrow = left_product(hidden, grad_branch)
    grad_hidden = right_product(grad_branch, narrow)
    grad_lifted = jax.vjp(smooth_gate, lifted)[1](grad_hidden)[0].astype(jnp.bfloat16)
    grad_expand = left_product(second, grad_lifted)
    grad_second = right_product(grad_lifted, expand)
    pullback = jax.vjp(
        layer_norm, middle, second_gain.astype(jnp.float32), second_bias.astype(jnp.float32)
    )[1]
    grad_middle, grad_gain_two, grad_bias_two = pullback(grad_second)
    grad_middle = grad_middle + grad_result
    grad_attended = grad_middle.astype(jnp.bfloat16)
    grad_output = left_product(mixture, grad_attended)
    grad_mixture = right_product(grad_attended, output).astype(jnp.bfloat16)
    grad_triple = attend_back(grad_mixture, attend_stored)
    grad_project = left_product(normed, grad_triple)
    grad_normed = right_product(grad_triple, project)
    pullback = jax.vjp(
        layer_norm, inputs, first_gain.astype(jnp.float32), first_bias.astype(jnp.float32)
    )[1]
    grad_inputs, grad_gain_one, grad_bias_one = pullback(grad_normed)
    grad_inputs = grad_inputs + grad_middle
    return (
        grad_inputs,
        (
            grad_gain_one,
            grad_bias_one,
            grad_project,
            grad_output,
            grad_gain_two,
            grad_bias_two,
            grad_expand,
            grad_narrow,
        ),
    )


def body(
    byte_inputs,
    segment_ids,
    cotangent,
    patch_weight,
    coarse_first_gain,
    coarse_first_bias,
    coarse_project,
    coarse_output,
    coarse_second_gain,
    coarse_second_bias,
    coarse_expand,
    coarse_narrow,
    fine_first_gain,
    fine_first_bias,
    fine_project,
    fine_output,
    fine_second_gain,
    fine_second_bias,
    fine_expand,
    fine_narrow,
):
    coarse_full = (
        lax.all_gather(patch_weight, "fsdp", axis=0, tiled=True),
        lax.all_gather(coarse_first_gain, "fsdp", axis=0, tiled=True),
        lax.all_gather(coarse_first_bias, "fsdp", axis=0, tiled=True),
        lax.all_gather(coarse_project, "fsdp", axis=0, tiled=True),
        lax.all_gather(coarse_output, "fsdp", axis=1, tiled=True),
        lax.all_gather(coarse_second_gain, "fsdp", axis=0, tiled=True),
        lax.all_gather(coarse_second_bias, "fsdp", axis=0, tiled=True),
        lax.all_gather(coarse_expand, "fsdp", axis=0, tiled=True),
        lax.all_gather(coarse_narrow, "fsdp", axis=1, tiled=True),
    )
    fine_full = (
        lax.all_gather(fine_first_gain, "fsdp", axis=0, tiled=True),
        lax.all_gather(fine_first_bias, "fsdp", axis=0, tiled=True),
        lax.all_gather(fine_project, "fsdp", axis=0, tiled=True),
        lax.all_gather(fine_output, "fsdp", axis=1, tiled=True),
        lax.all_gather(fine_second_gain, "fsdp", axis=0, tiled=True),
        lax.all_gather(fine_second_bias, "fsdp", axis=0, tiled=True),
        lax.all_gather(fine_expand, "fsdp", axis=0, tiled=True),
        lax.all_gather(fine_narrow, "fsdp", axis=1, tiled=True),
    )
    byte_rows = byte_inputs[0]
    bytes_here = byte_rows.shape[0]
    patches = bytes_here // PATCH
    segment_row = segment_ids[0]
    all_patches = segment_row.shape[0]
    places = jnp.arange(all_patches)
    coarse_allowed = (
        (places[:, None] >= places[None, :]) & (segment_row[:, None] == segment_row[None, :])
    )[None]
    inner = jnp.arange(PATCH)
    fine_allowed = (inner[:, None] >= inner[None, :])[None]

    def coarse_attend(triple):
        head_block = lax.all_to_all(
            triple.reshape(patches, 3, D), "seq", split_axis=2, concat_axis=0, tiled=True
        )
        all_rows = head_block.shape[0]
        columns = head_block.shape[2]
        local_heads = columns // HEAD_DIM
        queries = head_block[:, 0].reshape(1, all_rows, local_heads, HEAD_DIM)
        key_part = head_block[:, 1].reshape(1, all_rows, local_heads, HEAD_DIM)
        value_part = head_block[:, 2].reshape(1, all_rows, local_heads, HEAD_DIM)
        mixture, log_total = attend_forward(queries, key_part, value_part, coarse_allowed)
        merged = mixture.reshape(all_rows, columns).astype(jnp.bfloat16)
        back_rows = lax.all_to_all(merged, "seq", split_axis=0, concat_axis=1, tiled=True)
        return (back_rows, (queries, key_part, value_part, log_total))

    def coarse_back(grad_mixture, stored):
        queries, key_part, value_part, log_total = stored
        head_grad = lax.all_to_all(grad_mixture, "seq", split_axis=1, concat_axis=0, tiled=True)
        all_rows = head_grad.shape[0]
        columns = head_grad.shape[1]
        grad_queries, grad_keys, grad_values = attend_backward(
            queries,
            key_part,
            value_part,
            coarse_allowed,
            log_total,
            head_grad.reshape(1, all_rows, columns // HEAD_DIM, HEAD_DIM),
        )
        stacked = jnp.stack(
            [
                grad_queries.reshape(all_rows, columns),
                grad_keys.reshape(all_rows, columns),
                grad_values.reshape(all_rows, columns),
            ],
            1,
        ).astype(jnp.bfloat16)
        back_rows = lax.all_to_all(stacked, "seq", split_axis=0, concat_axis=2, tiled=True)
        return back_rows.reshape(back_rows.shape[0], 3 * D)

    def fine_attend(triple):
        grouped = triple.reshape(patches, PATCH, 3, D // HEAD_DIM, HEAD_DIM)
        queries = grouped[:, :, 0]
        key_part = grouped[:, :, 1]
        value_part = grouped[:, :, 2]
        mixture, log_total = attend_forward(queries, key_part, value_part, fine_allowed)
        return (
            mixture.reshape(bytes_here, D).astype(jnp.bfloat16),
            (queries, key_part, value_part, log_total),
        )

    def fine_back(grad_mixture, stored):
        queries, key_part, value_part, log_total = stored
        grad_queries, grad_keys, grad_values = attend_backward(
            queries,
            key_part,
            value_part,
            fine_allowed,
            log_total,
            grad_mixture.reshape(patches, PATCH, D // HEAD_DIM, HEAD_DIM),
        )
        stacked = jnp.stack([grad_queries, grad_keys, grad_values], 2).astype(jnp.bfloat16)
        return stacked.reshape(bytes_here, 3 * D)

    grouped_bytes = byte_rows.reshape(patches, PATCH * D)
    embedded = product(grouped_bytes, coarse_full[0])
    coarse_out, coarse_stored = block_forward(embedded, coarse_full[1:], coarse_attend)
    coarse_low = coarse_out.astype(jnp.bfloat16)
    arrived = shifted(coarse_low[-1:], "seq", 1)
    offset = lax.axis_index("seq") * patches
    padded = jnp.concatenate([segment_row[:1] - 1, segment_row])
    before = lax.dynamic_slice_in_dim(padded, offset, patches)
    current = lax.dynamic_slice_in_dim(segment_row, offset, patches)
    joined = (before == current).astype(jnp.float32)[:, None]
    previous = jnp.concatenate([arrived, coarse_low[:-1]]).astype(jnp.float32) * joined
    fine_in = (
        byte_rows.astype(jnp.float32).reshape(patches, PATCH, D) + previous[:, None, :]
    ).reshape(bytes_here, D)
    layer_rows, fine_stored = block_forward(fine_in, fine_full, fine_attend)
    fine_weights_back = (
        lax.all_gather(fine_first_gain, "fsdp", axis=0, tiled=True),
        lax.all_gather(fine_first_bias, "fsdp", axis=0, tiled=True),
        lax.all_gather(fine_project, "fsdp", axis=0, tiled=True),
        lax.all_gather(fine_output, "fsdp", axis=1, tiled=True),
        lax.all_gather(fine_second_gain, "fsdp", axis=0, tiled=True),
        lax.all_gather(fine_second_bias, "fsdp", axis=0, tiled=True),
        lax.all_gather(fine_expand, "fsdp", axis=0, tiled=True),
        lax.all_gather(fine_narrow, "fsdp", axis=1, tiled=True),
    )
    grad_fine_in, fine_grads = block_backward(
        cotangent[0].astype(jnp.float32), fine_weights_back, fine_stored, fine_back
    )
    grad_previous = jnp.sum(grad_fine_in.reshape(patches, PATCH, D), 1) * joined
    arrived_back = shifted(grad_previous[:1], "seq", -1)
    grad_coarse_out = jnp.concatenate([grad_previous[1:], arrived_back])
    coarse_weights_back = (
        lax.all_gather(patch_weight, "fsdp", axis=0, tiled=True),
        lax.all_gather(coarse_first_gain, "fsdp", axis=0, tiled=True),
        lax.all_gather(coarse_first_bias, "fsdp", axis=0, tiled=True),
        lax.all_gather(coarse_project, "fsdp", axis=0, tiled=True),
        lax.all_gather(coarse_output, "fsdp", axis=1, tiled=True),
        lax.all_gather(coarse_second_gain, "fsdp", axis=0, tiled=True),
        lax.all_gather(coarse_second_bias, "fsdp", axis=0, tiled=True),
        lax.all_gather(coarse_expand, "fsdp", axis=0, tiled=True),
        lax.all_gather(coarse_narrow, "fsdp", axis=1, tiled=True),
    )
    grad_embedded, coarse_grads = block_backward(
        grad_coarse_out, coarse_weights_back[1:], coarse_stored, coarse_back
    )
    grad_embed_low = grad_embedded.astype(jnp.bfloat16)
    grad_patch = left_product(grouped_bytes, grad_embed_low)
    grad_grouped = right_product(grad_embed_low, coarse_weights_back[0])
    input_gradient = (grad_fine_in + grad_grouped.reshape(bytes_here, D)).astype(jnp.bfloat16)
    shards = (
        lax.psum_scatter(grad_patch, "fsdp", scatter_dimension=0, tiled=True),
        lax.psum_scatter(coarse_grads[0], "fsdp", scatter_dimension=0, tiled=True),
        lax.psum_scatter(coarse_grads[1], "fsdp", scatter_dimension=0, tiled=True),
        lax.psum_scatter(coarse_grads[2], "fsdp", scatter_dimension=0, tiled=True),
        lax.psum_scatter(coarse_grads[3], "fsdp", scatter_dimension=1, tiled=True),
        lax.psum_scatter(coarse_grads[4], "fsdp", scatter_dimension=0, tiled=True),
        lax.psum_scatter(coarse_grads[5], "fsdp", scatter_dimension=0, tiled=True),
        lax.psum_scatter(coarse_grads[6], "fsdp", scatter_dimension=0, tiled=True),
        lax.psum_scatter(coarse_grads[7], "fsdp", scatter_dimension=1, tiled=True),
        lax.psum_scatter(fine_grads[0], "fsdp", scatter_dimension=0, tiled=True),
        lax.psum_scatter(fine_grads[1], "fsdp", scatter_dimension=0, tiled=True),
        lax.psum_scatter(fine_grads[2], "fsdp", scatter_dimension=0, tiled=True),
        lax.psum_scatter(fine_grads[3], "fsdp", scatter_dimension=1, tiled=True),
        lax.psum_scatter(fine_grads[4], "fsdp", scatter_dimension=0, tiled=True),
        lax.psum_scatter(fine_grads[5], "fsdp", scatter_dimension=0, tiled=True),
        lax.psum_scatter(fine_grads[6], "fsdp", scatter_dimension=0, tiled=True),
        lax.psum_scatter(fine_grads[7], "fsdp", scatter_dimension=1, tiled=True),
    )
    totals = (
        lax.psum(shards[0].astype(jnp.bfloat16), "seq").astype(jnp.float32),
        lax.psum(shards[1].astype(jnp.bfloat16), "seq").astype(jnp.float32),
        lax.psum(shards[2].astype(jnp.bfloat16), "seq").astype(jnp.float32),
        lax.psum(shards[3].astype(jnp.bfloat16), "seq").astype(jnp.float32),
        lax.psum(shards[4].astype(jnp.bfloat16), "seq").astype(jnp.float32),
        lax.psum(shards[5].astype(jnp.bfloat16), "seq").astype(jnp.float32),
        lax.psum(shards[6].astype(jnp.bfloat16), "seq").astype(jnp.float32),
        lax.psum(shards[7].astype(jnp.bfloat16), "seq").astype(jnp.float32),
        lax.psum(shards[8].astype(jnp.bfloat16), "seq").astype(jnp.float32),
        lax.psum(shards[9].astype(jnp.bfloat16), "seq").astype(jnp.float32),
        lax.psum(shards[10].astype(jnp.bfloat16), "seq").astype(jnp.float32),
        lax.psum(shards[11].astype(jnp.bfloat16), "seq").astype(jnp.float32),
        lax.psum(shards[12].astype(jnp.bfloat16), "seq").astype(jnp.float32),
        lax.psum(shards[13].astype(jnp.bfloat16), "seq").astype(jnp.float32),
        lax.psum(shards[14].astype(jnp.bfloat16), "seq").astype(jnp.float32),
        lax.psum(shards[15].astype(jnp.bfloat16), "seq").astype(jnp.float32),
        lax.psum(shards[16].astype(jnp.bfloat16), "seq").astype(jnp.float32),
    )
    layer_output = layer_rows.astype(jnp.bfloat16)[None]
    return (
        layer_output,
        input_gradient[None],
        totals[0],
        totals[1],
        totals[2],
        totals[3],
        totals[4],
        totals[5],
        totals[6],
        totals[7],
        totals[8],
        totals[9],
        totals[10],
        totals[11],
        totals[12],
        totals[13],
        totals[14],
        totals[15],
        totals[16],
    )


def solution(mesh):
    return jax.shard_map(
        body,
        mesh=mesh,
        in_specs=(
            P("fsdp", "seq", None),
            P("fsdp", None),
            P("fsdp", "seq", None),
            P("fsdp", None),
            P("fsdp"),
            P("fsdp"),
            P("fsdp", None),
            P(None, "fsdp"),
            P("fsdp"),
            P("fsdp"),
            P("fsdp", None),
            P(None, "fsdp"),
            P("fsdp"),
            P("fsdp"),
            P("fsdp", None),
            P(None, "fsdp"),
            P("fsdp"),
            P("fsdp"),
            P("fsdp", None),
            P(None, "fsdp"),
        ),
        out_specs=(
            P("fsdp", "seq", None),
            P("fsdp", "seq", None),
            P("fsdp", None),
            P("fsdp"),
            P("fsdp"),
            P("fsdp", None),
            P(None, "fsdp"),
            P("fsdp"),
            P("fsdp"),
            P("fsdp", None),
            P(None, "fsdp"),
            P("fsdp"),
            P("fsdp"),
            P("fsdp", None),
            P(None, "fsdp"),
            P("fsdp"),
            P("fsdp"),
            P("fsdp", None),
            P(None, "fsdp"),
        ),
        check_vma=False,
    )
```

profile of v0, /device:TPU:0, one launch (start us, length us, event | category | flops | bytes accessed | tf_op | source)
XLA Modules:
  0.0 2491.6 jit_solution(15751886596229776372)
XLA Ops:
  27.3 81.9 %all-reduce.17 = (bf16[768]{0:T(1024)(128)(2,1)S(1)}, bf16[768]{0:T(1024)(128)(2,1)S(1)}, bf16[768]{0:T(1024)(128)(2,1)S(1)}, bf16[768]{0:T(1024)(128)(2,1)S(1)}...) all-reduce(bf16[768]{0:T(1024)(128)(2,1)S(1)} %dynamic-update-slice, ...), channel_id=1, replica_groups=mesh['seq'=2,'fsdp'=16] {'fsdp'}, use_global_device_ids=true, to_apply=%add.1 | all-reduce | flops 6144 | bytes 24576
  110.0 26.6 %all-gather.10.cloned.1.call-done = bf16[6144,768]{1,0:T(8,128)(2,1)} async-done(((bf16[384,768]{1,0:T(8,128)(2,1)}), bf16[6144,768]{1,0:T(8,128)(2,1)}) %all-gather.10.cloned.1.call-update) | async-done | bytes 9437200 | tf_op jit(solution)/shard_map/all_gather | solution.py:173
  142.5 66.0 %all-gather.12.cloned.1.call-done = bf16[768,2304]{1,0:T(8,128)(2,1)} async-done(((bf16[48,2304]{1,0:T(8,128)(2,1)}), bf16[768,2304]{1,0:T(8,128)(2,1)}) %all-gather.12.cloned.1.call-update) | async-done | bytes 3538960 | tf_op jit(solution)/shard_map/all_gather | solution.py:176
  223.7 42.0 %all-gather.14.cloned.1.call-done = bf16[768,768]{0,1:T(8,128)(2,1)} async-done(((bf16[768,48]{0,1:T(8,128)(2,1)}), bf16[768,768]{0,1:T(8,128)(2,1)}) %all-gather.14.cloned.1.call-update) | async-done | bytes 1179664 | tf_op jit(solution)/shard_map/all_gather | solution.py:177
  268.0 78.8 %all-gather.16.cloned.1.call-done = bf16[768,3072]{1,0:T(8,128)(2,1)} async-done(((bf16[48,3072]{1,0:T(8,128)(2,1)}), bf16[768,3072]{1,0:T(8,128)(2,1)}) %all-gather.16.cloned.1.call-update) | async-done | bytes 4718608 | tf_op jit(solution)/shard_map/all_gather | solution.py:180
  351.3 76.6 %all-gather.18.cloned.1.call-done = bf16[3072,768]{0,1:T(8,128)(2,1)} async-done(((bf16[3072,48]{0,1:T(8,128)(2,1)}), bf16[3072,768]{0,1:T(8,128)(2,1)}) %all-gather.18.cloned.1.call-update) | async-done | bytes 4718608 | tf_op jit(solution)/shard_map/all_gather | solution.py:181
  435.8 64.0 %all-gather.20.cloned.1.call-done = bf16[768,2304]{1,0:T(8,128)(2,1)} async-done(((bf16[48,2304]{1,0:T(8,128)(2,1)}), bf16[768,2304]{1,0:T(8,128)(2,1)}) %all-gather.20.cloned.1.call-update) | async-done | bytes 3538960 | tf_op jit(solution)/shard_map/all_gather | solution.py:186
  508.0 15.1 reshape.527
  562.7 75.7 %all-gather.24.cloned.1.call-done = bf16[768,3072]{1,0:T(8,128)(2,1)} async-done(((bf16[48,3072]{1,0:T(8,128)(2,1)}), bf16[768,3072]{1,0:T(8,128)(2,1)}) %all-gather.24.cloned.1.call-update) | async-done | bytes 4718608 | tf_op jit(solution)/shard_map/all_gather | solution.py:190
  649.4 70.1 %all-gather.26.cloned.1.call-done = bf16[3072,768]{0,1:T(8,128)(2,1)} async-done(((bf16[3072,48]{0,1:T(8,128)(2,1)}), bf16[3072,768]{0,1:T(8,128)(2,1)}) %all-gather.26.cloned.1.call-update) | async-done | bytes 4718608 | tf_op jit(solution)/shard_map/all_gather | solution.py:191
  719.6 15.5 fusion.6
  766.8 12.5 multiply_reduce_fusion
  819.6 18.3 copy.145
  837.9 15.7 convert_element_type.329
  962.7 92.8 %reduce-scatter.14.cloned.1.call-done = f32[768,48]{0,1:T(8,128)} async-done(((f32[768,768]{0,1:T(8,128)}), f32[768,48]{0,1:T(8,128)}) %reduce-scatter.14.cloned.1.call-update) | async-done | bytes 147472 | tf_op jit(solution)/shard_map/reduce_scatter | solution.py:322
  1057.1 154.4 %reduce-scatter.20.cloned.1.call-done = f32[48,2304]{1,0:T(8,128)} async-done(((f32[768,2304]{1,0:T(8,128)}), f32[48,2304]{1,0:T(8,128)}) %reduce-scatter.20.cloned.1.call-update) | async-done | bytes 442384 | tf_op jit(solution)/shard_map/reduce_scatter | solution.py:329
  1213.2 155.0 %reduce-scatter.12.cloned.1.call-done = f32[48,2304]{1,0:T(8,128)} async-done(((f32[768,2304]{1,0:T(8,128)}), f32[48,2304]{1,0:T(8,128)}) %reduce-scatter.12.cloned.1.call-update) | async-done | bytes 442384 | tf_op jit(solution)/shard_map/reduce_scatter | solution.py:321
  1369.9 175.1 %reduce-scatter.24.cloned.1.call-done = f32[48,3072]{1,0:T(8,128)} async-done(((f32[768,3072]{1,0:T(8,128)}), f32[48,3072]{1,0:T(8,128)}) %reduce-scatter.24.cloned.1.call-update) | async-done | bytes 589840 | tf_op jit(solution)/shard_map/reduce_scatter | solution.py:333
  1546.8 174.5 %reduce-scatter.26.cloned.1.call-done = f32[3072,48]{0,1:T(8,128)} async-done(((f32[3072,768]{0,1:T(8,128)}), f32[3072,48]{0,1:T(8,128)}) %reduce-scatter.26.cloned.1.call-update) | async-done | bytes 589840 | tf_op jit(solution)/shard_map/reduce_scatter | solution.py:334
  1723.1 174.4 %reduce-scatter.18.cloned.1.call-done = f32[3072,48]{0,1:T(8,128)} async-done(((f32[3072,768]{0,1:T(8,128)}), f32[3072,48]{0,1:T(8,128)}) %reduce-scatter.18.cloned.1.call-update) | async-done | bytes 589840 | tf_op jit(solution)/shard_map/reduce_scatter | solution.py:326
  1899.4 174.1 %reduce-scatter.16.cloned.1.call-done = f32[48,3072]{1,0:T(8,128)} async-done(((f32[768,3072]{1,0:T(8,128)}), f32[48,3072]{1,0:T(8,128)}) %reduce-scatter.16.cloned.1.call-update) | async-done | bytes 589840 | tf_op jit(solution)/shard_map/reduce_scatter | solution.py:325
  2075.3 288.1 %reduce-scatter.10.cloned.1.call-done = f32[384,768]{0,1:T(8,128)} async-done(((f32[6144,768]{0,1:T(8,128)}), f32[384,768]{0,1:T(8,128)}) %reduce-scatter.10.cloned.1.call-update) | async-done | bytes 1179664 | tf_op jit(solution)/shard_map/reduce_scatter | solution.py:318
  2365.6 13.3 fusion.64
  2386.7 75.0 %all-reduce.16 = (bf16[768]{0:T(1024)(128)(2,1)S(1)}, bf16[768]{0:T(1024)(128)(2,1)S(1)}, bf16[768]{0:T(1024)(128)(2,1)S(1)}, bf16[768]{0:T(1024)(128)(2,1)S(1)}...) all-reduce(f32[768]{0:T(1024)S(1)} %get-tuple-element.123, ...), channel_id=3, replica_groups=mesh['seq'=2,'fsdp'=16] {'fsdp'}, use_global_device_ids=true, to_apply=%region_26.27.clone | all-reduce | flops 6144 | bytes 36864
  (432 shorter events, 338.2 us)
Async XLA Ops:
  7.2 129.4 %all-gather.10.cloned.1.call-start = ((), (), s32[]{:S(2)}) async-start(), calls=%async_computation.13 | async-start | bytes 10027008 | tf_op jit(solution)/shard_map/all_gather | solution.py:173
  7.9 200.6 %all-gather.12.cloned.1.call-start = ((), (), s32[]{:S(2)}) async-start(), calls=%async_computation.14 | async-start | bytes 3760128 | tf_op jit(solution)/shard_map/all_gather | solution.py:176
  8.7 257.1 %all-gather.14.cloned.1.call-start = ((), (), s32[]{:S(2)}) async-start(), calls=%async_computation.15 | async-start | bytes 1253376 | tf_op jit(solution)/shard_map/all_gather | solution.py:177
  9.4 337.4 %all-gather.16.cloned.1.call-start = ((), (), s32[]{:S(2)}) async-start(), calls=%async_computation.16 | async-start | bytes 5013504 | tf_op jit(solution)/shard_map/all_gather | solution.py:180
  10.0 417.9 %all-gather.18.cloned.1.call-start = ((), (), s32[]{:S(2)}) async-start(), calls=%async_computation.17 | async-start | bytes 5013504 | tf_op jit(solution)/shard_map/all_gather | solution.py:181
  10.6 489.3 %all-gather.20.cloned.1.call-start = ((), (), s32[]{:S(2)}) async-start(), calls=%async_computation.18 | async-start | bytes 3760128 | tf_op jit(solution)/shard_map/all_gather | solution.py:186
  11.2 546.0 %all-gather.22.cloned.1.call-start = ((), (), s32[]{:S(2)}) async-start(), calls=%async_computation.19 | async-start | bytes 1253376 | tf_op jit(solution)/shard_map/all_gather | solution.py:187
  11.9 626.4 %all-gather.24.cloned.1.call-start = ((), (), s32[]{:S(2)}) async-start(), calls=%async_computation.20 | async-start | bytes 5013504 | tf_op jit(solution)/shard_map/all_gather | solution.py:190
  12.7 706.9 %all-gather.26.cloned.1.call-start = ((), (), s32[]{:S(2)}) async-start(), calls=%async_computation.21 | async-start | bytes 5013504 | tf_op jit(solution)/shard_map/all_gather | solution.py:191
  220.2 45.5 %all-to-all-start.1 = ((bf16[2,128,384]{1,2,0:T(8,128)(2,1)}), bf16[2,128,384]{1,2,0:T(8,128)(2,1)S(1)}, u32[]{:S(2)}, u32[]{:S(2)}) async-start(bf16[2,128,384]{1,2,0:T(8,128)(2,1)} %copy.132), calls=%async_computation.1 | async-start | bytes 393216 | tf_op jit(solution)/shard_map/all_to_all | solution.py:217
  223.7 737.5 %reduce-scatter.22.cloned.1.call-start = ((), (), s32[]{:S(2)}) async-start(), calls=%async_computation.28 | async-start | bytes 2506752 | tf_op jit(solution)/shard_map/reduce_scatter | solution.py:330
  432.5 2.2 collective-permute-start
  434.6 306.7 %copy-start.61 = (f32[768]{0:T(1024)}, f32[768]{0:T(1024)S(1)}, u32[]{:S(2)}) copy-start(f32[768]{0:T(1024)S(1)} %convert_element_type.318) | copy-start | bytes 9220
  793.8 261.7 %reduce-scatter.14.cloned.1.call-start = ((), (), s32[]{:S(2)}) async-start(), calls=%async_computation.24 | async-start | bytes 2506752 | tf_op jit(solution)/shard_map/reduce_scatter | solution.py:322
  869.1 3.1 collective-permute-start.1
  881.2 330.2 %reduce-scatter.20.cloned.1.call-start = ((), (), s32[]{:S(2)}) async-start(), calls=%async_computation.27 | async-start | bytes 7520256 | tf_op jit(solution)/shard_map/reduce_scatter | solution.py:329
  890.1 478.1 %reduce-scatter.12.cloned.1.call-start = ((), (), s32[]{:S(2)}) async-start(), calls=%async_computation.23 | async-start | bytes 7520256 | tf_op jit(solution)/shard_map/reduce_scatter | solution.py:321
  909.7 635.3 %reduce-scatter.24.cloned.1.call-start = ((), (), s32[]{:S(2)}) async-start(), calls=%async_computation.29 | async-start | bytes 10027008 | tf_op jit(solution)/shard_map/reduce_scatter | solution.py:333
  922.2 799.0 %reduce-scatter.26.cloned.1.call-start = ((), (), s32[]{:S(2)}) async-start(), calls=%async_computation.30 | async-start | bytes 10027008 | tf_op jit(solution)/shard_map/reduce_scatter | solution.py:334
  934.5 963.0 %reduce-scatter.18.cloned.1.call-start = ((), (), s32[]{:S(2)}) async-start(), calls=%async_computation.26 | async-start | bytes 10027008 | tf_op jit(solution)/shard_map/reduce_scatter | solution.py:326
  941.1 1132.5 %reduce-scatter.16.cloned.1.call-start = ((), (), s32[]{:S(2)}) async-start(), calls=%async_computation.25 | async-start | bytes 10027008 | tf_op jit(solution)/shard_map/reduce_scatter | solution.py:325
  947.4 1416.0 %reduce-scatter.10.cloned.1.call-start = ((), (), s32[]{:S(2)}) async-start(), calls=%async_computation.22 | async-start | bytes 20054016 | tf_op jit(solution)/shard_map/reduce_scatter | solution.py:318
  960.2 1512.0 %all-reduce.22.cloned.1.call-start = ((), (), s32[]{:S(2)}) async-start(), calls=%async_computation.31 | async-start | bytes 4718592 | tf_op jit(solution)/shard_map/psum | solution.py:337
  1897.5 481.4 %slice-start = ((s8[9437184]{0:T(1024)(128)(4,1)}), s8[1048576]{0:T(1024)(128)(4,1)S(1)}, s32[]{:S(2)}) async-start(s8[9437184]{0:T(1024)(128)(4,1)} %bitcast.245), calls=%async_computation.32 | async-start | bytes 2097152
  (101 other events, 2685.0 us)
Sparse Core Ops, SparseCore 0:
  10.8 125.7 all-gather.9
  139.4 69.0 all-gather.11
  211.3 54.4 all-gather.13
  268.4 78.3 all-gather.15
  349.5 78.3 all-gather.17
  430.5 69.2 all-gather.19
  502.6 54.4 all-gather.21
  559.9 78.3 all-gather.23
  641.2 78.3 all-gather.25
  793.9 128.1 reduce-scatter.21
  927.1 128.3 reduce-scatter.13
  1060.7 150.7 reduce-scatter.19
  1216.8 151.3 reduce-scatter.11
  1373.7 171.2 reduce-scatter.23
  1550.5 170.7 reduce-scatter.25
  1726.8 170.6 reduce-scatter.17
  1903.0 170.4 reduce-scatter.15
  2079.1 284.2 reduce-scatter.9
  2368.1 22.1 all-reduce.21
where the time goes:
time: 2500 us; the launch traced here: 2490 us
  waiting for transfers between devices  1900 us (76%)
  matrix products  200 us (8%)
  blocking collectives  172 us (7%)
  local copies, waits for them, and re-layouts  129 us (5%)
  other arithmetic  67.7 us (3%)
    reduce_scatter x1, waiting for transfers between devices, body(): lax.psum_scatter(grad_patch, 'fsdp', scatter_dimension=0, tiled=True)  288 us
    reduce_scatter x1, waiting for transfers between devices, body(): lax.psum_scatter(fine_grads[6], 'fsdp', scatter_dimension=0, tiled=True)  175 us
    reduce_scatter x1, waiting for transfers between devices, body(): lax.psum_scatter(fine_grads[7], 'fsdp', scatter_dimension=1, tiled=True)  174 us
    reduce_scatter x1, waiting for transfers between devices, body(): lax.psum_scatter(coarse_grads[7], 'fsdp', scatter_dimension=1, tiled=True)  174 us
    reduce_scatter x1, waiting for transfers between devices, body(): lax.psum_scatter(coarse_grads[6], 'fsdp', scatter_dimension=0, tiled=True)  174 us
    unnamed x2, blocking collectives  157 us
    reduce_scatter x1, waiting for transfers between devices, body(): lax.psum_scatter(coarse_grads[2], 'fsdp', scatter_dimension=0, tiled=True)  155 us
    reduce_scatter x1, waiting for transfers between devices, body(): lax.psum_scatter(fine_grads[2], 'fsdp', scatter_dimension=0, tiled=True)  154 us
  transfers between devices with their start and end apart: 22, of which 18 were waited for; matrix products, arithmetic and copies ran while one was open for 12% of the time, Pallas kernels for 0%

commit v1 on v0

--- a/solution.py
+++ b/solution.py
@@ -1,9 +1,13 @@
+import functools
 import math
 
 import jax
 import jax.numpy as jnp
 from jax import lax
+from jax.experimental import pallas as pl
+from jax.experimental.pallas import tpu as pltpu
 from jax.sharding import PartitionSpec as P
+
 
 D = 768
 HEAD_DIM = 64
@@ -376,9 +380,597 @@
     )
 
 
+MESH = pl.DeviceIdType.MESH
+HBM = pltpu.MemorySpace.HBM
+VMEM = pltpu.MemorySpace.VMEM
+
+
+class Place:
+    def __init__(self):
+        self.core = lax.axis_index("seq")
+        self.at = lax.axis_index("fsdp")
+        self.z = self.at // 4
+        self.plane = self.at % 4
+        self.near = 1 + self.core
+        self.far = 2 - self.core
+
+    def flip(self, mask):
+        return self.at ^ mask
+
+    def across(self, mask):
+        return (self.core, self.at ^ mask)
+
+    def partner(self):
+        return (1 - self.core, self.at)
+
+
+def enter(place, masks, partner=True):
+    barrier = pltpu.get_barrier_semaphore()
+    for mask in masks:
+        pl.semaphore_signal(barrier, inc=1, device_id=place.across(mask), device_id_type=MESH)
+    if partner:
+        pl.semaphore_signal(barrier, inc=1, device_id=place.partner(), device_id_type=MESH)
+    pl.semaphore_wait(barrier, len(masks) + (1 if partner else 0))
+
+
+MASKS = (1, 2, 4, 8, 12)
+
+
+class Gather:
+    EVENTS = 12
+
+    def __init__(self, place, source, buffer, rows, column, width, z_first, sends, receives, local):
+        self.p, self.source, self.buffer, self.rows = place, source, buffer, rows
+        self.z_first, self.sends, self.receives, self.local = z_first, sends, receives, local
+        self.half = width // 2
+        self.column, self.width = column, width
+        self.mine = pl.ds(pl.multiple_of(column + place.core * self.half, 128), self.half)
+        self.theirs = pl.ds(pl.multiple_of(column + (1 - place.core) * self.half, 128), self.half)
+        self.started = []
+
+    def group(self, plane, columns=None):
+        return self.buffer.at[:, plane, self.rows, self.mine if columns is None else columns]
+
+    def block(self, z, plane):
+        return self.buffer.at[z, plane, self.rows, self.mine]
+
+    def send(self, event, view, device, source=None):
+        copy = pltpu.make_async_remote_copy(
+            src_ref=view if source is None else source,
+            dst_ref=view,
+            send_sem=self.sends.at[event],
+            recv_sem=self.receives.at[event],
+            device_id=device,
+            device_id_type=MESH,
+        )
+        copy.start()
+        self.started.append(copy)
+
+    def arrived(self, event, view):
+        pltpu.make_async_remote_copy(
+            src_ref=view,
+            dst_ref=view,
+            send_sem=self.sends.at[event],
+            recv_sem=self.receives.at[event],
+            device_id=self.p.partner(),
+            device_id_type=MESH,
+        ).wait_recv()
+
+    def start(self):
+        p = self.p
+        own = self.source.at[self.rows, pl.ds(pl.multiple_of(p.core * self.half, 128), self.half)]
+        self.copy = pltpu.make_async_copy(own, self.block(p.z, p.plane), self.local)
+        self.copy.start()
+        if not self.z_first:
+            self.send(6, self.block(p.z, p.plane), p.across(p.near), own)
+        for j in (1, 2, 3):
+            self.send(j - 1, self.block(p.z, p.plane), p.across(4 * j), own)
+
+    def one(self):
+        p = self.p
+        self.copy.wait()
+        if self.z_first:
+            for j in (1, 2, 3):
+                self.arrived(j - 1, self.block(p.z ^ j, p.plane))
+            self.send(6, self.group(p.plane), p.across(p.near))
+            self.send(7, self.group(p.plane), p.across(p.far))
+            self.send(9, self.group(p.plane), p.partner())
+        else:
+            self.arrived(6, self.block(p.z, p.plane ^ p.near))
+            for j in (1, 2, 3):
+                self.send(2 + j, self.block(p.z, p.plane ^ p.near), p.across(4 * j))
+
+    def two(self):
+        p = self.p
+        if self.z_first:
+            self.arrived(6, self.group(p.plane ^ p.near))
+        else:
+            for j in (1, 2, 3):
+                self.arrived(j - 1, self.block(p.z ^ j, p.plane))
+            self.send(7, self.group(p.plane), p.across(p.far))
+            self.send(9, self.group(p.plane), p.partner())
+            for j in (1, 2, 3):
+                self.arrived(2 + j, self.block(p.z ^ j, p.plane ^ p.near))
+        self.send(8, self.group(p.plane ^ p.near), p.across(p.far))
+        self.send(10, self.group(p.plane ^ p.near), p.partner())
+
+    def three(self):
+        p = self.p
+        self.arrived(7, self.group(p.plane ^ p.far))
+        self.send(11, self.group(p.plane ^ p.far), p.partner())
+        self.arrived(8, self.group(p.plane ^ 3))
+        self.send(12, self.group(p.plane ^ 3), p.partner())
+
+    def four(self):
+        p = self.p
+        self.arrived(9, self.group(p.plane, self.theirs))
+        self.arrived(10, self.group(p.plane ^ p.far, self.theirs))
+        self.arrived(11, self.group(p.plane ^ p.near, self.theirs))
+        self.arrived(12, self.group(p.plane ^ 3, self.theirs))
+
+    def drain(self):
+        for copy in self.started:
+            copy.wait_send()
+
+
+def run_gathers(gathers, ahead, tick):
+    n = len(gathers)
+    for k in range(min(ahead, n)):
+        gathers[k].start()
+    for t in range(n + 3):
+        if t < n:
+            gathers[t].one()
+            if t + ahead < n:
+                gathers[t + ahead].start()
+        if 0 <= t - 1 < n:
+            gathers[t - 1].two()
+        if 0 <= t - 2 < n:
+            gathers[t - 2].three()
+        if 0 <= t - 3 < n:
+            gathers[t - 3].four()
+        tick()
+    for g in gathers:
+        g.drain()
+
+
+def gather_kernel(plan, ahead, *refs):
+    sources, small, rows, rest = refs[:9], refs[9], refs[10], refs[11:]
+    buffers, small_out, all_rows = rest[:3], rest[3], rest[4]
+    sends, receives, local, value, arriving, small_sends, small_receives, row_sems = rest[5:]
+    place = Place()
+    enter(place, MASKS)
+    value[0] = small[...]
+    total = Total(place, (1, 2, 4, 8), value, arriving, small_sends, small_receives, small_out)
+    stay = pltpu.make_async_copy(rows, all_rows.at[place.core], row_sems.at[0])
+    stay.start()
+    cross = pltpu.make_async_remote_copy(
+        src_ref=rows, dst_ref=all_rows.at[place.core], send_sem=row_sems.at[1], recv_sem=row_sems.at[2],
+        device_id=place.partner(), device_id_type=MESH,
+    )
+    cross.start()
+    gathers = []
+    for k, (source, buffer, first, rows, column, width, z_first) in enumerate(plan):
+        gathers.append(
+            Gather(place, sources[source], buffers[buffer], pl.ds(first, rows), column, width, z_first,
+                   sends.at[k], receives.at[k], local.at[k])
+        )
+    run_gathers(gathers, ahead, total.advance)
+    stay.wait()
+    cross.wait()
+
+
+PLAN = (
+    (0, 0, 0, 192, 0, 768, True),
+    (0, 0, 192, 192, 0, 768, False),
+    (1, 1, 0, 48, 0, 2304, True),
+    (2, 1, 0, 48, 2304, 768, True),
+    (3, 1, 0, 48, 3072, 3072, True),
+    (4, 1, 0, 48, 6144, 3072, False),
+    (5, 2, 0, 48, 0, 2304, True),
+    (6, 2, 0, 48, 2304, 768, True),
+    (7, 2, 0, 48, 3072, 3072, False),
+    (8, 2, 0, 48, 6144, 3072, True),
+)
+
+
+def gather_all(sources, small, rows, ahead=2, plan=PLAN):
+    n = len(plan)
+    bf = jnp.bfloat16
+    return pl.pallas_call(
+        functools.partial(gather_kernel, plan, ahead),
+        out_shape=(
+            jax.ShapeDtypeStruct((4, 4, 384, 768), bf),
+            jax.ShapeDtypeStruct((4, 4, 48, 9216), bf),
+            jax.ShapeDtypeStruct((4, 4, 48, 9216), bf),
+            jax.ShapeDtypeStruct((8, 768), jnp.float32),
+            jax.ShapeDtypeStruct((2,) + rows.shape, bf),
+        ),
+        in_specs=[pl.BlockSpec(memory_space=VMEM)] * 10 + [pl.BlockSpec(memory_space=HBM)],
+        out_specs=[pl.BlockSpec(memory_space=HBM)] * 3 + [pl.BlockSpec(memory_space=VMEM), pl.BlockSpec(memory_space=HBM)],
+        scratch_shapes=[
+            pltpu.SemaphoreType.DMA((n, 13)),
+            pltpu.SemaphoreType.DMA((n, 13)),
+            pltpu.SemaphoreType.DMA((n,)),
+            pltpu.VMEM((5, 8, 768), jnp.float32),
+            pltpu.VMEM((4, 8, 768), jnp.float32),
+            pltpu.SemaphoreType.DMA((4,)),
+            pltpu.SemaphoreType.DMA((4,)),
+            pltpu.SemaphoreType.DMA((3,)),
+        ],
+        compiler_params=pltpu.CompilerParams(collective_id=0, has_side_effects=True),
+        name="gather_all",
+    )(*sources, small, rows)
+
+
+class Total:
+    def __init__(self, place, masks, value, arriving, sends, receives, result):
+        self.p, self.masks, self.value, self.arriving = place, masks, value, arriving
+        self.sends, self.receives, self.result = sends, receives, result
+        self.step, self.copy = 0, None
+
+    def advance(self):
+        if self.step > len(self.masks):
+            return
+        if self.copy is not None:
+            self.copy.wait()
+            i = self.step - 1
+            self.value[i + 1] = self.value[i] + self.arriving[i]
+        if self.step < len(self.masks):
+            i = self.step
+            mask = self.masks[i]
+            self.copy = pltpu.make_async_remote_copy(
+                src_ref=self.value.at[i],
+                dst_ref=self.arriving.at[i],
+                send_sem=self.sends.at[i],
+                recv_sem=self.receives.at[i],
+                device_id=self.p.across(mask) if mask else self.p.partner(),
+                device_id_type=MESH,
+            )
+            self.copy.start()
+        else:
+            self.result[...] = self.value[len(self.masks)]
+        self.step += 1
+
+
+def add(left, right):
+    return left.astype(jnp.float32) + right.astype(jnp.float32)
+
+
+class Reduce:
+    def __init__(self, place, held, paired, far, near, line, out, rows, column, width, z_last, sends, receives):
+        self.p, self.held, self.from_partner, self.from_far = place, held, paired, far
+        self.from_near, self.from_line, self.out, self.rows = near, line, out, rows
+        self.z_last, self.sends, self.receives = z_last, sends, receives
+        self.half = width // 2
+        self.mine = pl.ds(pl.multiple_of(column + place.core * self.half, 128), self.half)
+        self.theirs = pl.ds(pl.multiple_of(column + (1 - place.core) * self.half, 128), self.half)
+        self.started = []
+
+    def send(self, event, source, target, device):
+        copy = pltpu.make_async_remote_copy(
+            src_ref=source, dst_ref=target, send_sem=self.sends.at[event], recv_sem=self.receives.at[event],
+            device_id=device, device_id_type=MESH,
+        )
+        copy.start()
+        self.started.append(copy)
+
+    def arrived(self, event, target):
+        pltpu.make_async_remote_copy(
+            src_ref=target, dst_ref=target, send_sem=self.sends.at[event], recv_sem=self.receives.at[event],
+            device_id=self.p.partner(), device_id_type=MESH,
+        ).wait_recv()
+
+    def pair(self, theirs):
+        self.send(0, theirs, self.from_partner, self.p.partner())
+
+    def fold(self, plane, others):
+        def step(z, _):
+            self.held[z, plane] = add(self.held[z, plane], others[z]).astype(jnp.bfloat16)
+            return 0
+
+        lax.fori_loop(0, 4, step, 0)
+
+    def one(self):
+        p = self.p
+        if self.from_partner is not None:
+            self.arrived(0, self.from_partner)
+            self.fold(p.plane ^ p.far, self.from_partner.at[:, p.plane ^ p.far])
+        self.send(1, self.held.at[:, p.plane ^ p.far], self.from_far.at[0], p.across(p.far))
+        if self.from_partner is not None:
+            self.fold(p.plane ^ 3, self.from_partner.at[:, p.plane ^ 3])
+        self.send(2, self.held.at[:, p.plane ^ 3], self.from_far.at[1], p.across(p.far))
+        if self.from_partner is not None:
+            self.fold(p.plane, self.from_partner.at[:, p.plane])
+            self.fold(p.plane ^ p.near, self.from_partner.at[:, p.plane ^ p.near])
+
+    def two(self):
+        p = self.p
+        self.arrived(2, self.from_far.at[1])
+        self.fold(p.plane ^ p.near, self.from_far.at[1])
+        if self.z_last:
+            self.send(3, self.held.at[:, p.plane ^ p.near], self.from_near, p.across(p.near))
+        else:
+            for j in (1, 2, 3):
+                self.send(6 + j, self.held.at[p.z ^ j, p.plane ^ p.near], self.from_line.at[2 + j], p.across(4 * j))
+        self.arrived(1, self.from_far.at[0])
+        self.fold(p.plane, self.from_far.at[0])
+        if not self.z_last:
+            for j in (1, 2, 3):
+                self.send(3 + j, self.held.at[p.z ^ j, p.plane], self.from_line.at[j - 1], p.across(4 * j))
+
+    def three(self):
+        p = self.p
+        if self.z_last:
+            self.arrived(3, self.from_near)
+            self.fold(p.plane, self.from_near)
+            for j in (1, 2, 3):
+                self.send(3 + j, self.held.at[p.z ^ j, p.plane], self.from_line.at[j - 1], p.across(4 * j))
+        else:
+            for j in (1, 2, 3):
+                self.arrived(6 + j, self.from_line.at[2 + j])
+            near = (add(self.held[p.z, p.plane ^ p.near], self.from_line[3]) + add(self.from_line[4], self.from_line[5]))
+            self.held[p.z, p.plane ^ p.near] = near.astype(jnp.bfloat16)
+            self.send(3, self.held.at[p.z, p.plane ^ p.near], self.from_near.at[0], p.across(p.near))
+
+    def four(self):
+        p = self.p
+        for j in (1, 2, 3):
+            self.arrived(3 + j, self.from_line.at[j - 1])
+        total = add(self.held[p.z, p.plane], self.from_line[0]) + add(self.from_line[1], self.from_line[2])
+        if not self.z_last:
+            self.arrived(3, self.from_near.at[0])
+            total = total + self.from_near[0].astype(jnp.float32)
+        self.out[self.rows, self.mine] = total
+        view = self.out.at[self.rows, self.mine]
+        self.send(10, view, view, p.partner())
+
+    def drain(self):
+        for copy in self.started:
+            copy.wait_send()
+        self.started = []
+
+    def five(self):
+        self.arrived(10, self.out.at[self.rows, self.theirs])
+
+
+BACK_PLAN = (
+    (2, 0, 48, 6144, 3072, True),
+    (2, 0, 48, 3072, 3072, False),
+    (2, 0, 48, 2304, 768, True),
+    (2, 0, 48, 0, 2304, True),
+    (1, 0, 48, 6144, 3072, True),
+    (1, 0, 48, 3072, 3072, False),
+    (1, 0, 48, 2304, 768, True),
+    (1, 0, 48, 0, 2304, True),
+    (0, 0, 192, 0, 768, False),
+    (0, 192, 192, 0, 768, True),
+)
+SLOTS = 3
+
+
+def reduce_kernel(plan, grads, small, outs, small_out, slots, pairs, fars, nears, lines, sends, receives, loads,
+                  value, arriving, small_sends, small_receives):
+    place = Place()
+    enter(place, MASKS)
+    n = len(plan)
+    value[0] = small[...]
+    total = Total(place, (0, 1, 2, 4, 8), value, arriving, small_sends, small_receives, small_out)
+    used = [0, 0]
+    reduces, copies = [], []
+    for k, (array, first, rows, column, width, z_last) in enumerate(plan):
+        kind = 0 if array == 0 else 1
+        slot = used[kind] % SLOTS if kind else used[kind]
+        used[kind] += 1
+        half = width // 2
+        cut = (lambda ref, kind=kind, half=half: ref if not kind or half == 1536 else ref.at[..., pl.ds(0, half)])
+        reduces.append(
+            Reduce(place, cut(slots[kind].at[slot]), cut(pairs.at[used[kind] - 1]) if array == 2 else None, cut(fars[kind].at[used[kind] - 1]),
+                   cut(nears[kind].at[used[kind] - 1]), cut(lines[kind].at[used[kind] - 1]), outs[array],
+                   pl.ds(first, rows), column, width, z_last, sends.at[k], receives.at[k])
+        )
+
+    def load(k):
+        array, first, rows, column, width, z_last = plan[k]
+        r = reduces[k]
+        if k - SLOTS >= 0:
+            reduces[k - SLOTS].drain()
+        copy = pltpu.make_async_copy(grads[array].at[:, :, r.rows, r.mine], r.held, loads.at[k])
+        copy.start()
+        copies.append(copy)
+        if array == 2:
+            r.pair(grads[array].at[:, :, r.rows, r.theirs])
+
+    for t in range(n + 4):
+        if t - 4 >= 0:
+            reduces[t - 4].five()
+        if 0 <= t - 3 < n:
+            reduces[t - 3].four()
+        if t < n:
+            load(t)
+        if 0 <= t - 2 < n:
+            reduces[t - 2].three()
+        if 0 <= t - 1 < n:
+            reduces[t - 1].two()
+        if t < n:
+            copies[t].wait()
+            reduces[t].one()
+        total.advance()
+    for r in reduces:
+        r.drain()
+
+
+def reduce_all(grads, small, plan=BACK_PLAN):
+    n = len(plan)
+    bf = jnp.bfloat16
+    shapes = ((2, 192, 384), (8, 48, 1536))
+
+    def kernel(*refs):
+        grads, small, outs, small_out = refs[:3], refs[3], refs[4:7], refs[7]
+        pairs = refs[8]
+        slots, fars, nears, lines = (refs[9 + 2 * i : 11 + 2 * i] for i in range(4))
+        reduce_kernel(plan, grads, small, outs, small_out, slots, pairs, fars, nears, lines, *refs[17:])
+
+    scratch = [pltpu.VMEM((4, 4, 4, 48, 1536), bf)]
+    for lead in (((2, 4, 4), (SLOTS, 4, 4)), ((2, 2, 4), (8, 2, 4)), ((2, 4), (8, 4)), ((2, 6), (8, 6))):
+        scratch += [pltpu.VMEM(lead[i] + shapes[i][1:], bf) for i in (0, 1)]
+    scratch += [
+        pltpu.SemaphoreType.DMA((n, 11)),
+        pltpu.SemaphoreType.DMA((n, 11)),
+        pltpu.SemaphoreType.DMA((n,)),
+        pltpu.VMEM((6, 8, 768), jnp.float32),
+        pltpu.VMEM((5, 8, 768), jnp.float32),
+        pltpu.SemaphoreType.DMA((5,)),
+        pltpu.SemaphoreType.DMA((5,)),
+    ]
+    return pl.pallas_call(
+        kernel,
+        out_shape=(
+            jax.ShapeDtypeStruct((384, 768), jnp.float32),
+            jax.ShapeDtypeStruct((48, 9216), jnp.float32),
+            jax.ShapeDtypeStruct((48, 9216), jnp.float32),
+            jax.ShapeDtypeStruct((8, 768), jnp.float32),
+        ),
+        in_specs=[pl.BlockSpec(memory_space=HBM)] * 3 + [pl.BlockSpec(memory_space=VMEM)],
+        out_specs=[pl.BlockSpec(memory_space=VMEM)] * 4,
+        scratch_shapes=scratch,
+        compiler_params=pltpu.CompilerParams(collective_id=1, has_side_effects=True, vmem_limit_bytes=66_000_000),
+        name="reduce_all",
+    )(*grads, small)
+
+
+def fast_body(byte_inputs, segment_ids, cotangent, patch_weight, *weights):
+    coarse, fine = weights[:8], weights[8:]
+    core, at = lax.axis_index("seq"), lax.axis_index("fsdp")
+    vectors = jnp.stack([w[i] for w in (coarse, fine) for i in (0, 1, 4, 5)]).astype(jnp.float32)
+    small = lax.dynamic_update_slice(jnp.zeros((8, D), jnp.float32), vectors, (0, at * vectors.shape[1]))
+    sources = [patch_weight]
+    for w in (coarse, fine):
+        sources += [w[2], w[3].T, w[6], w[7].T]
+    byte_rows = byte_inputs[0]
+    bytes_here = byte_rows.shape[0]
+    patches = bytes_here // PATCH
+    patch_full, coarse_full, fine_full, small, all_rows = gather_all(sources, small, byte_rows)
+    patch_full = patch_full.reshape(-1, D)
+
+    def unpack(full, first):
+        full = full.reshape(D, -1)
+        return (small[first], small[first + 1], full[:, : 3 * D], full[:, 3 * D : 4 * D], small[first + 2], small[first + 3],
+                full[:, 4 * D : 8 * D], full[:, 8 * D :])
+
+    coarse_w, fine_w = unpack(coarse_full, 0), unpack(fine_full, 4)
+    segment_row = segment_ids[0]
+    all_patches = segment_row.shape[0]
+    places = jnp.arange(all_patches)
+    coarse_allowed = (
+        (places[:, None] >= places[None, :]) & (segment_row[:, None] == segment_row[None, :])
+    )[None]
+    inner = jnp.arange(PATCH)
+    fine_allowed = (inner[:, None] >= inner[None, :])[None]
+
+    def attend(shape, allowed):
+        rows = shape[0] * shape[1]
+
+        def forward(triple):
+            grouped = triple.reshape(shape + (3, D // HEAD_DIM, HEAD_DIM))
+            parts = grouped[:, :, 0], grouped[:, :, 1], grouped[:, :, 2]
+            mixture, log_total = attend_forward(*parts, allowed)
+            return (mixture.reshape(rows, D).astype(jnp.bfloat16), parts + (log_total,))
+
+        def backward(grad_mixture, stored):
+            queries, key_part, value_part, log_total = stored
+            grads = attend_backward(
+                queries, key_part, value_part, allowed, log_total,
+                grad_mixture.reshape(shape + (D // HEAD_DIM, HEAD_DIM)),
+            )
+            return jnp.stack(grads, 2).astype(jnp.bfloat16).reshape(rows, 3 * D)
+
+        return forward, backward
+
+    coarse_attend, coarse_back = attend((1, all_patches), coarse_allowed)
+    fine_attend, fine_back = attend((patches, PATCH), fine_allowed)
+    grouped_bytes = all_rows.reshape(all_patches, PATCH * D)
+    embedded = product(grouped_bytes, patch_full)
+    coarse_out, coarse_stored = block_forward_t(embedded, coarse_w, coarse_attend)
+    coarse_low = coarse_out.astype(jnp.bfloat16)
+    joined = jnp.concatenate([jnp.zeros((1,), bool), segment_row[1:] == segment_row[:-1]]).astype(jnp.float32)[:, None]
+    previous = jnp.concatenate([jnp.zeros((1, D), jnp.bfloat16), coarse_low[:-1]]).astype(jnp.float32) * joined
+    previous = lax.dynamic_slice_in_dim(previous, core * patches, patches)
+    fine_in = (
+        byte_rows.astype(jnp.float32).reshape(patches, PATCH, D) + previous[:, None, :]
+    ).reshape(bytes_here, D)
+    layer_rows, fine_stored = block_forward_t(fine_in, fine_w, fine_attend)
+    grad_fine_in, fine_grads = block_backward_t(cotangent[0].astype(jnp.float32), fine_w, fine_stored, fine_back)
+    grad_previous = jnp.sum(grad_fine_in.reshape(patches, PATCH, D), 1)
+    grad_previous = lax.all_gather(grad_previous, "seq", axis=0, tiled=True) * joined
+    grad_coarse_out = jnp.concatenate([grad_previous[1:], jnp.zeros((1, D), jnp.float32)])
+    grad_embedded, coarse_grads = block_backward_t(grad_coarse_out, coarse_w, coarse_stored, coarse_back)
+    grad_embed_low = grad_embedded.astype(jnp.bfloat16)
+    grad_patch = left_product(grouped_bytes, grad_embed_low)
+    grad_here = lax.dynamic_slice_in_dim(grad_embed_low, core * patches, patches)
+    grad_grouped = right_product(grad_here, patch_full)
+    input_gradient = (grad_fine_in + grad_grouped.reshape(bytes_here, D)).astype(jnp.bfloat16)
+
+    def pack(grads):
+        return jnp.concatenate([grads[2], grads[3], grads[6], grads[7]], 1).astype(jnp.bfloat16).reshape(4, 4, 48, 12 * D)
+
+    once = (core == 0).astype(jnp.float32)
+    small = jnp.stack([coarse_grads[i] * once for i in (0, 1, 4, 5)] + [fine_grads[i] for i in (0, 1, 4, 5)])
+    patch_shard, coarse_shard, fine_shard, small = reduce_all(
+        (grad_patch.astype(jnp.bfloat16).reshape(4, 4, 384, D), pack(coarse_grads), pack(fine_grads)), small
+    )
+    small = lax.dynamic_slice_in_dim(small, at * vectors.shape[1], vectors.shape[1], 1)
+
+    def shards(full, first):
+        return (small[first], small[first + 1], full[:, : 3 * D], full[:, 3 * D : 4 * D].T, small[first + 2],
+                small[first + 3], full[:, 4 * D : 8 * D], full[:, 8 * D :].T)
+
+    return (layer_rows.astype(jnp.bfloat16)[None], input_gradient[None], patch_shard) + shards(coarse_shard, 0) + shards(fine_shard, 4)
+
+
+def block_forward_t(inputs, weights, attend):
+    first_gain, first_bias, project, output_t, second_gain, second_bias, expand, narrow_t = weights
+    normed = layer_norm(inputs, first_gain, first_bias).astype(jnp.bfloat16)
+    triple = product(normed, project).astype(jnp.bfloat16)
+    mixture, attend_stored = attend(triple)
+    middle = inputs + right_product(mixture, output_t)
+    second = layer_norm(middle, second_gain, second_bias).astype(jnp.bfloat16)
+    lifted = product(second, expand)
+    hidden = smooth_gate(lifted).astype(jnp.bfloat16)
+    result = middle + right_product(hidden, narrow_t)
+    stored = (inputs, normed, attend_stored, mixture, middle, second, lifted, hidden)
+    return (result, stored)
+
+
+def block_backward_t(grad_result, weights, stored, attend_back):
+    first_gain, first_bias, project, output_t, second_gain, second_bias, expand, narrow_t = weights
+    inputs, normed, attend_stored, mixture, middle, second, lifted, hidden = stored
+    grad_branch = grad_result.astype(jnp.bfloat16)
+    grad_narrow_t = left_product(grad_branch, hidden)
+    grad_hidden = product(grad_branch, narrow_t)
+    grad_lifted = jax.vjp(smooth_gate, lifted)[1](grad_hidden)[0].astype(jnp.bfloat16)
+    grad_expand = left_product(second, grad_lifted)
+    grad_second = right_product(grad_lifted, expand)
+    pullback = jax.vjp(layer_norm, middle, second_gain, second_bias)[1]
+    grad_middle, grad_gain_two, grad_bias_two = pullback(grad_second)
+    grad_middle = grad_middle + grad_result
+    grad_attended = grad_middle.astype(jnp.bfloat16)
+    grad_output_t = left_product(grad_attended, mixture)
+    grad_mixture = product(grad_attended, output_t).astype(jnp.bfloat16)
+    grad_triple = attend_back(grad_mixture, attend_stored)
+    grad_project = left_product(normed, grad_triple)
+    grad_normed = right_product(grad_triple, project)
+    pullback = jax.vjp(layer_norm, inputs, first_gain, first_bias)[1]
+    grad_inputs, grad_gain_one, grad_bias_one = pullback(grad_normed)
+    grad_inputs = grad_inputs + grad_middle
+    return (
+        grad_inputs,
+        (grad_gain_one, grad_bias_one, grad_project, grad_output_t, grad_gain_two, grad_bias_two, grad_expand, grad_narrow_t),
+    )
+
+
 def solution(mesh):
     return jax.shard_map(
-        body,
+        fast_body if (mesh.shape["seq"], mesh.shape["fsdp"]) == (2, 16) else body,
         mesh=mesh,
         in_specs=(
             P("fsdp", "seq", None),

time: 2500 us -> 831 us (0.33)
  waiting for transfers between devices: 1900 us -> 0 us
  Pallas kernels: 0 us -> 404 us
  blocking collectives: 172 us -> 2.53 us
  local copies, waits for them, and re-layouts: 129 us -> 154 us
    reduce_scatter x9 -> x0, waiting for transfers between devices: 1390 us -> none  [the longest x1 288 us: body(): lax.psum_scatter(grad_patch, 'fsdp', scatter_dimension=0, tiled=True)]
    all_gather x9 -> x0, waiting for transfers between devices: 501 us -> none  [the longest x1 78.8 us: body(): lax.all_gather(coarse_expand, 'fsdp', axis=0, tiled=True)]
    pallas_call x0 -> x2, Pallas kernels: none -> 404 us  [the longest x1 231 us: reduce_all(): pl.pallas_call(kernel, out_shape=(jax.ShapeDtypeStruct((384, 768), jnp.fl...]
    unnamed x2 -> x0, blocking collectives: 157 us -> none
    convert_element_type x37 -> x7, other arithmetic: 34 us -> 4.52 us  [the longest x2 2.63 us: backward(): return jnp.stack(grads, 2).astype(jnp.bfloat16).reshape(rows, 3 * D)]
    convert_element_type x7 -> x8, local copies, waits for them, and re-layouts: 44.9 us -> 67.2 us  [the longest x3 49.7 us: backward(): return jnp.stack(grads, 2).astype(jnp.bfloat16).reshape(rows, 3 * D)]
  transfers between devices with their start and end apart: 22 -> 0, of which waited for: 18 -> 0; matrix products, arithmetic and copies ran while one was open for 12% -> 0% of each run, Pallas kernels for 0% -> 0%
where the time goes in v1:
time: 831 us; the launch traced here: 823 us
  Pallas kernels  404 us (49%)
  matrix products  200 us (24%)
  local copies, waits for them, and re-layouts  154 us (19%)
  other arithmetic  60.2 us (7%)
    pallas_call x1, Pallas kernels, reduce_all(): pl.pallas_call(kernel, out_shape=(jax.ShapeDtypeStruct((384, 768), jnp.fl...  231 us
    pallas_call x1, Pallas kernels, gather_all(): pl.pallas_call(functools.partial(gather_kernel, plan, ahead), out_shape=(...  173 us
    dot_general x9, matrix products, product(): return jnp.dot(left_side, right_side, preferred_element_type=jnp.float32)  54.9 us
    dot_general x9, matrix products, right_product(): lax.dot_general(left_side, right_side, (((1,), (1,)), ((), ())), preferre...  54.5 us
    convert_element_type x3, local copies, waits for them, and re-layouts, backward(): return jnp.stack(grads, 2).astype(jnp.bfloat16).reshape(rows, 3 * D)  49.7 us
    dot_general x9, matrix products, left_product(): lax.dot_general(left_side, right_side, (((0,), (0,)), ((), ())), preferre...  44.5 us
    concatenate x2, other arithmetic, pack(): jnp.concatenate([grads[2], grads[3], grads[6], grads[7]], 1)  21.6 us

profile of v1, /device:TPU:0, one launch (start us, length us, event | category | flops | bytes accessed | tf_op | source)
XLA Modules:
  0.0 823.4 jit_solution(16655459713909514325)
XLA Ops:
  4.3 173.2 %gather_all.1 = (bf16[4,4,384,768]{3,2,1,0:T(8,128)(2,1)}, bf16[4,4,48,9216]{3,2,1,0:T(8,128)(2,1)}, bf16[4,4,48,9216]{3,2,1,0:T(8,128)(2,1)}, f32[8,768]{1,0:T(8,128)}, bf16[2,1024,768]{2,1,0:T(8,128)(2,1)}) custom-call(bf16[384,768]{1,0:T(8,128)(2,1)} %refs_0_.1, bf16[48,2304]{1,0:T(8,128)(2,1)} %refs_1_.1, bf16[48,768]{1,0:T(8,128)(2,1)} %bitcast.281, ...), custom_call_target="tpu_custom_call" | custom-call | tf_op jit(solution)/shard_map/gather_all/pallas_call | solution.py:579
  181.9 7.3 fusion.109
  211.5 8.1 convolution_convert_fusion.1
  219.6 14.9 %reshape.539 = bf16[128,8,3,12,64]{4,3,2,1,0:T(8,128)(2,1)} reshape(bf16[1024,2304]{1,0:T(8,128)(2,1)} %convolution_convert_fusion.1) | data formatting | bytes 9437184 | tf_op jit(solution)/shard_map/reshape | solution.py:874
  234.6 9.5 %fusion.108 = (bf16[128,8,1,12,64]{4,3,2,1,0:T(8,128)(2,1)S(1)}, bf16[128,8,1,12,64]{4,3,2,1,0:T(8,128)(2,1)}, bf16[128,8,1,12,64]{4,3,2,1,0:T(8,128)(2,1)}) fusion(bf16[128,8,3,12,64]{4,3,2,1,0:T(8,128)(2,1)} %reshape.539), kind=kLoop, calls=%fused_computation.224 | loop fusion | bytes 9437184 | tf_op jit(solution)/shard_map/slice | solution.py:875
  276.9 7.7 fusion.18
  284.6 14.6 %fusion.70 = bf16[1,1024,768]{2,1,0:T(8,128)(2,1)} fusion(f32[1024,768]{1,0:T(8,128)S(1)} %get-tuple-element.94, bf16[768,9216]{1,0:T(8,128)(2,1)} %bitcast.295, f32[1024,3072]{1,0:T(8,128)S(1)} %fusion.18), kind=kOutput, calls=%fused_computation.118 | convolution fusion | flops 4861722624 | bytes 22020096 | tf_op jit(solution)/shard_map/dot_general | solution.py:48
  299.2 7.5 convolution_convert_fusion.2
  306.7 15.0 %fusion.6 = bf16[1024,3072]{1,0:T(8,128)(2,1)S(1)} fusion(f32[1024,3072]{1,0:T(8,128)} %copy-done.81, bf16[768,9216]{1,0:T(8,128)(2,1)} %bitcast.296, bf16[1,1024,768]{2,1,0:T(8,128)(2,1)S(1)} %copy-done.21), kind=kOutput, calls=%fused_computation.10 | convolution fusion | flops 4894752768 | bytes 25165824 | tf_op jit(solution)/shard_map/dot_general | solution.py:38
  321.7 8.0 multiply_reduce_fusion.1
  329.7 8.1 convolution_convert_fusion.3
  358.3 8.0 fusion.55
  372.0 12.4 %multiply_reduce_fusion = (f32[128,12,8]{2,1,0:T(8,128)}, f32[128,12,8,8]{2,3,1,0:T(8,128)}) fusion(f32[128,12,8,8]{2,3,1,0:T(8,128)} %copy-done, f32[128,12,8]{2,1,0:T(8,128)S(1)} %log_add_fusion, pred[8,8]{0,1:T(8,128)(4,1)S(1)} %iota_compare_fusion.1, bf16[128,8,1,12,64]{4,3,2,1,0:T(8,128)(2,1)} %get-tuple-element.70, bf16[128,8,12,64]{3,2,1,0:T(8,128)(2,1)} %reshape.540), kind=kOutput, calls=%fused_computation.20 | convolution fusion | flops 13062144 | bytes 4030528 | tf_op jit(solution)/shard_map/bqhd,bkhd->bhqk/dot_general | solution.py:79
  396.6 6.7 copy.98
  409.2 6.7 copy.97
  422.3 18.5 %copy.102 = bf16[128,8,3,12,64]{4,3,2,1,0:T(8,128)(2,1)} copy(bf16[128,8,3,12,64]{0,4,3,2,1:T(8,128)(2,1)} %maximum_convert_fusion) | data formatting | bytes 9437184 | tf_op jit(solution)/shard_map/convert_element_type | solution.py:885
  440.8 15.6 %reshape.551 = bf16[1024,2304,1,1]{1,0,2,3:T(8,128)(2,1)} reshape(bf16[128,8,3,12,64]{4,3,2,1,0:T(8,128)(2,1)} %copy.102) | data formatting | bytes 9437184 | tf_op jit(solution)/shard_map/convert_element_type | solution.py:885
  456.4 15.6 %convert_element_type.204 = bf16[1024,2304]{1,0:T(8,128)(2,1)} reshape(bf16[128,8,3,12,64]{4,3,2,1,0:T(8,128)(2,1)} %copy.102) | data formatting | bytes 9437184 | tf_op jit(solution)/shard_map/convert_element_type | solution.py:885
  472.1 7.3 fusion.104
  516.0 6.7 convolution_convert_fusion.4
  522.8 10.7 %pad_maximum_fusion.1.refs_2_ = bf16[4,4,48,9216]{3,2,1,0:T(8,128)(2,1)} fusion(bf16[4,4,48,3072]{3,2,1,0:T(8,128)(2,1)} %bitcast.251, bf16[4,4,48,3072]{3,2,1,0:T(8,128)(2,1)} %bitcast.252, bf16[4,4,48,768]{3,2,1,0:T(8,128)(2,1)S(1)} %copy-done.33, bf16[4,4,48,2304]{3,2,1,0:T(8,128)(2,1)S(1)} %convolution_convert_fusion.4), kind=kLoop, calls=%fused_computation.3 | loop fusion | flops 56623104 | bytes 28311552 | tf_op jit(solution)/shard_map/concatenate | solution.py:914
  546.4 8.4 %fusion.83 = f32[128,6144]{1,0:T(8,128)} fusion(bf16[6144,768]{1,0:T(8,128)(2,1)} %bitcast.247, bf16[256,768]{1,0:T(8,128)(2,1)S(1)} %add_convert_fusion.4, s32[]{:T(128)S(6)} %select_n.21), kind=kOutput, calls=%fused_computation.159 | convolution fusion | flops 1207959552 | bytes 12779524 | tf_op jit(solution)/shard_map/dot_general | solution.py:48
  564.6 10.9 %pad_maximum_fusion.refs_1_ = bf16[4,4,48,9216]{3,2,1,0:T(8,128)(2,1)} fusion(bf16[4,4,48,3072]{3,2,1,0:T(8,128)(2,1)} %bitcast.253, bf16[4,4,48,3072]{3,2,1,0:T(8,128)(2,1)} %bitcast.248, bf16[4,4,48,768]{3,2,1,0:T(8,128)(2,1)S(1)} %copy-done.23, bf16[4,4,48,2304]{3,2,1,0:T(8,128)(2,1)S(1)} %convolution_convert_fusion.7), kind=kLoop, calls=%fused_computation.2 | loop fusion | flops 56623104 | bytes 28311552 | tf_op jit(solution)/shard_map/concatenate | solution.py:914
  580.6 230.5 %reduce_all.1 = (f32[384,768]{1,0:T(8,128)}, f32[48,9216]{1,0:T(8,128)}, f32[48,9216]{1,0:T(8,128)}, f32[8,768]{1,0:T(8,128)}) custom-call(bf16[4,4,384,768]{3,2,1,0:T(8,128)(2,1)} %bitcast.244, bf16[4,4,48,9216]{3,2,1,0:T(8,128)(2,1)} %pad_maximum_fusion.refs_1_, bf16[4,4,48,9216]{3,2,1,0:T(8,128)(2,1)} %pad_maximum_fusion.1.refs_2_, f32[8,768]{1,0:T(8,128)} %stack.79.refs_3_), custom_call_target="tpu_custom_call" | custom-call | tf_op jit(solution)/shard_map/reduce_all/pallas_call | solution.py:825
  (288 shorter events, 188.7 us)
Async XLA Ops:
  4.3 191.3 %copy-start.35 = (pred[256,256]{0,1:T(8,128)(4,1)}, pred[256,256]{0,1:T(8,128)(4,1)S(1)}, u32[]{:S(2)}) copy-start(pred[256,256]{0,1:T(8,128)(4,1)S(1)} %fusion.82) | copy-start | bytes 196612
  181.9 17.4 %copy-start.38 = (f32[768]{0:T(1024)}, f32[768]{0:T(1024)S(1)}, u32[]{:S(2)}) copy-start(f32[768]{0:T(1024)S(1)} %get-tuple-element.55) | copy-start | bytes 9220
  181.9 17.4 %copy-start.42 = (f32[768]{0:T(1024)}, f32[768]{0:T(1024)S(1)}, u32[]{:S(2)}) copy-start(f32[768]{0:T(1024)S(1)} %get-tuple-element.54) | copy-start | bytes 9220
  181.9 29.6 %copy-start.49 = (f32[768]{0:T(1024)}, f32[768]{0:T(1024)S(1)}, u32[]{:S(2)}) copy-start(f32[768]{0:T(1024)S(1)} %get-tuple-element.53) | copy-start | bytes 9220
  181.9 29.6 %copy-start.60 = (f32[768]{0:T(1024)}, f32[768]{0:T(1024)S(1)}, u32[]{:S(2)}) copy-start(f32[768]{0:T(1024)S(1)} %get-tuple-element.52) | copy-start | bytes 9220
  199.0 10.0 %copy-start.10 = (f32[256,768]{1,0:T(8,128)}, f32[256,768]{1,0:T(8,128)S(1)}, u32[]{:S(2)}) copy-start(f32[256,768]{1,0:T(8,128)S(1)} %get-tuple-element.90) | copy-start | bytes 2359300
  210.8 8.8 %copy-start.45 = (f32[1024]{0:T(1024)}, f32[1024]{0:T(1024)S(1)}, u32[]{:S(2)}) copy-start(f32[1024]{0:T(1024)S(1)} %broadcast_multiply_fusion.5) | copy-start | bytes 12292
  211.5 8.1 copy-start.47
  211.5 8.1 copy-start.51
  284.6 14.6 %copy-start.81 = (f32[1024,3072]{1,0:T(8,128)}, f32[1024,3072]{1,0:T(8,128)S(1)}, u32[]{:S(2)}) copy-start(f32[1024,3072]{1,0:T(8,128)S(1)} %fusion.18) | copy-start | bytes 37748740
  284.6 14.6 %copy-start.21 = (bf16[1,1024,768]{2,1,0:T(8,128)(2,1)S(1)}, bf16[1,1024,768]{2,1,0:T(8,128)(2,1)}, u32[]{:S(2)}) copy-start(bf16[1,1024,768]{2,1,0:T(8,128)(2,1)} %param.22) | copy-start | bytes 4718596
  456.4 15.6 %copy-start.46 = (f32[1024]{0:T(1024)S(1)}, f32[1024]{0:T(1024)}, u32[]{:S(2)}) copy-start(f32[1024]{0:T(1024)} %copy-done.45) | copy-start | bytes 12292
  456.4 15.6 %copy-start.50 = (f32[768]{0:T(1024)S(1)}, f32[768]{0:T(1024)}, u32[]{:S(2)}) copy-start(f32[768]{0:T(1024)} %copy-done.49) | copy-start | bytes 9220
  472.0 8.0 copy-start.48
  472.0 8.0 copy-start.52
  472.0 8.0 copy-start.61
  472.0 19.4 %slice-start = ((s8[14155776]{0:T(1024)(128)(4,1)}), s8[4194304]{0:T(1024)(128)(4,1)S(1)}, s32[]{:S(2)}) async-start(s8[14155776]{0:T(1024)(128)(4,1)} %bitcast.275), calls=%async_computation | async-start | bytes 8388608
  472.1 19.4 %slice-start.1 = ((s8[14155776]{0:T(1024)(128)(4,1)}), s8[4194304]{0:T(1024)(128)(4,1)S(1)}, s32[]{:S(2)}) async-start(s8[14155776]{0:T(1024)(128)(4,1)} %bitcast.275), calls=%async_computation.1 | async-start | bytes 8388608
  472.1 19.4 %slice-start.2 = ((s8[14155776]{0:T(1024)(128)(4,1)}), s8[4194304]{0:T(1024)(128)(4,1)S(1)}, s32[]{:S(2)}) async-start(s8[14155776]{0:T(1024)(128)(4,1)} %bitcast.275), calls=%async_computation.2 | async-start | bytes 8388608
  522.8 10.8 %copy-start.12 = (f32[256,768]{1,0:T(8,128)S(1)}, f32[256,768]{1,0:T(8,128)}, u32[]{:S(2)}) copy-start(f32[256,768]{1,0:T(8,128)} %copy-done.10) | copy-start | bytes 2359300
  522.8 10.8 %copy-start.31 = (bf16[256,3072]{1,0:T(8,128)(2,1)S(1)}, bf16[256,3072]{1,0:T(8,128)(2,1)}, u32[]{:S(2)}) copy-start(bf16[256,3072]{1,0:T(8,128)(2,1)} %copy-done.30) | copy-start | bytes 4718596
  522.8 10.8 %copy-start.43 = (f32[768]{0:T(1024)S(1)}, f32[768]{0:T(1024)}, u32[]{:S(2)}) copy-start(f32[768]{0:T(1024)} %copy-done.42) | copy-start | bytes 9220
  564.6 10.9 %copy-start.14 = (bf16[256,6144]{1,0:T(8,128)(2,1)S(1)}, bf16[256,6144]{1,0:T(8,128)(2,1)}, u32[]{:S(2)}) copy-start(bf16[256,6144]{1,0:T(8,128)(2,1)} %copy-done.13) | copy-start | bytes 9437188
  811.1 8.9 %copy-start.29 = (f32[48,9216]{1,0:T(8,128)S(1)}, f32[48,9216]{1,0:T(8,128)}, u32[]{:S(2)}) copy-start(f32[48,9216]{1,0:T(8,128)} %get-tuple-element.36) | copy-start | bytes 5308420
  (62 other events, 235.9 us)

commit v2 on v1

--- a/solution.py
+++ b/solution.py
@@ -734,18 +734,19 @@
 
 
 BACK_PLAN = (
-    (2, 0, 48, 6144, 3072, True),
-    (2, 0, 48, 3072, 3072, False),
-    (2, 0, 48, 2304, 768, True),
-    (2, 0, 48, 0, 2304, True),
-    (1, 0, 48, 6144, 3072, True),
-    (1, 0, 48, 3072, 3072, False),
-    (1, 0, 48, 2304, 768, True),
-    (1, 0, 48, 0, 2304, True),
-    (0, 0, 192, 0, 768, False),
-    (0, 192, 192, 0, 768, True),
+    (8, 0, 48, 3072, True),
+    (7, 0, 48, 3072, False),
+    (6, 0, 48, 768, True),
+    (5, 0, 48, 2304, True),
+    (4, 0, 48, 3072, True),
+    (3, 0, 48, 3072, False),
+    (2, 0, 48, 768, True),
+    (1, 0, 48, 2304, True),
+    (0, 0, 192, 768, False),
+    (0, 192, 192, 768, True),
 )
 SLOTS = 3
+ARRAYS = 9
 
 
 def reduce_kernel(plan, grads, small, outs, small_out, slots, pairs, fars, nears, lines, sends, receives, loads,
@@ -757,27 +758,27 @@
     total = Total(place, (0, 1, 2, 4, 8), value, arriving, small_sends, small_receives, small_out)
     used = [0, 0]
     reduces, copies = [], []
-    for k, (array, first, rows, column, width, z_last) in enumerate(plan):
+    for k, (array, first, rows, width, z_last) in enumerate(plan):
         kind = 0 if array == 0 else 1
         slot = used[kind] % SLOTS if kind else used[kind]
         used[kind] += 1
         half = width // 2
         cut = (lambda ref, kind=kind, half=half: ref if not kind or half == 1536 else ref.at[..., pl.ds(0, half)])
         reduces.append(
-            Reduce(place, cut(slots[kind].at[slot]), cut(pairs.at[used[kind] - 1]) if array == 2 else None, cut(fars[kind].at[used[kind] - 1]),
+            Reduce(place, cut(slots[kind].at[slot]), cut(pairs.at[used[kind] - 1]) if array > 4 else None, cut(fars[kind].at[used[kind] - 1]),
                    cut(nears[kind].at[used[kind] - 1]), cut(lines[kind].at[used[kind] - 1]), outs[array],
-                   pl.ds(first, rows), column, width, z_last, sends.at[k], receives.at[k])
+                   pl.ds(first, rows), 0, width, z_last, sends.at[k], receives.at[k])
         )
 
     def load(k):
-        array, first, rows, column, width, z_last = plan[k]
+        array = plan[k][0]
         r = reduces[k]
         if k - SLOTS >= 0:
             reduces[k - SLOTS].drain()
         copy = pltpu.make_async_copy(grads[array].at[:, :, r.rows, r.mine], r.held, loads.at[k])
         copy.start()
         copies.append(copy)
-        if array == 2:
+        if array > 4:
             r.pair(grads[array].at[:, :, r.rows, r.theirs])
 
     for t in range(n + 4):
@@ -805,10 +806,10 @@
     shapes = ((2, 192, 384), (8, 48, 1536))
 
     def kernel(*refs):
-        grads, small, outs, small_out = refs[:3], refs[3], refs[4:7], refs[7]
-        pairs = refs[8]
-        slots, fars, nears, lines = (refs[9 + 2 * i : 11 + 2 * i] for i in range(4))
-        reduce_kernel(plan, grads, small, outs, small_out, slots, pairs, fars, nears, lines, *refs[17:])
+        grads, small, outs, small_out = refs[:ARRAYS], refs[ARRAYS], refs[ARRAYS + 1 : 2 * ARRAYS + 1], refs[2 * ARRAYS + 1]
+        pairs, rest = refs[2 * ARRAYS + 2], refs[2 * ARRAYS + 3 :]
+        slots, fars, nears, lines = (rest[2 * i : 2 * i + 2] for i in range(4))
+        reduce_kernel(plan, grads, small, outs, small_out, slots, pairs, fars, nears, lines, *rest[8:])
 
     scratch = [pltpu.VMEM((4, 4, 4, 48, 1536), bf)]
     for lead in (((2, 4, 4), (SLOTS, 4, 4)), ((2, 2, 4), (8, 2, 4)), ((2, 4), (8, 4)), ((2, 6), (8, 6))):
@@ -822,16 +823,12 @@
         pltpu.SemaphoreType.DMA((5,)),
         pltpu.SemaphoreType.DMA((5,)),
     ]
+    grads = [g.reshape(4, 4, g.shape[0] // 16, g.shape[1]) for g in grads]
     return pl.pallas_call(
         kernel,
-        out_shape=(
-            jax.ShapeDtypeStruct((384, 768), jnp.float32),
-            jax.ShapeDtypeStruct((48, 9216), jnp.float32),
-            jax.ShapeDtypeStruct((48, 9216), jnp.float32),
-            jax.ShapeDtypeStruct((8, 768), jnp.float32),
-        ),
-        in_specs=[pl.BlockSpec(memory_space=HBM)] * 3 + [pl.BlockSpec(memory_space=VMEM)],
-        out_specs=[pl.BlockSpec(memory_space=VMEM)] * 4,
+        out_shape=[jax.ShapeDtypeStruct(g.shape[2:], jnp.float32) for g in grads] + [jax.ShapeDtypeStruct((8, 768), jnp.float32)],
+        in_specs=[pl.BlockSpec(memory_space=HBM)] * ARRAYS + [pl.BlockSpec(memory_space=VMEM)],
+        out_specs=[pl.BlockSpec(memory_space=VMEM)] * (ARRAYS + 1),
         scratch_shapes=scratch,
         compiler_params=pltpu.CompilerParams(collective_id=1, has_side_effects=True, vmem_limit_bytes=66_000_000),
         name="reduce_all",
@@ -857,15 +854,13 @@
         return (small[first], small[first + 1], full[:, : 3 * D], full[:, 3 * D : 4 * D], small[first + 2], small[first + 3],
                 full[:, 4 * D : 8 * D], full[:, 8 * D :])
 
-    coarse_w, fine_w = unpack(coarse_full, 0), unpack(fine_full, 4)
+    coarse_w = unpack(coarse_full, 0)
     segment_row = segment_ids[0]
     all_patches = segment_row.shape[0]
     places = jnp.arange(all_patches)
     coarse_allowed = (
         (places[:, None] >= places[None, :]) & (segment_row[:, None] == segment_row[None, :])
     )[None]
-    inner = jnp.arange(PATCH)
-    fine_allowed = (inner[:, None] >= inner[None, :])[None]
 
     def attend(shape, allowed):
         rows = shape[0] * shape[1]
@@ -887,7 +882,6 @@
         return forward, backward
 
     coarse_attend, coarse_back = attend((1, all_patches), coarse_allowed)
-    fine_attend, fine_back = attend((patches, PATCH), fine_allowed)
     grouped_bytes = all_rows.reshape(all_patches, PATCH * D)
     embedded = product(grouped_bytes, patch_full)
     coarse_out, coarse_stored = block_forward_t(embedded, coarse_w, coarse_attend)
@@ -895,36 +889,31 @@
     joined = jnp.concatenate([jnp.zeros((1,), bool), segment_row[1:] == segment_row[:-1]]).astype(jnp.float32)[:, None]
     previous = jnp.concatenate([jnp.zeros((1, D), jnp.bfloat16), coarse_low[:-1]]).astype(jnp.float32) * joined
     previous = lax.dynamic_slice_in_dim(previous, core * patches, patches)
-    fine_in = (
-        byte_rows.astype(jnp.float32).reshape(patches, PATCH, D) + previous[:, None, :]
-    ).reshape(bytes_here, D)
-    layer_rows, fine_stored = block_forward_t(fine_in, fine_w, fine_attend)
-    grad_fine_in, fine_grads = block_backward_t(cotangent[0].astype(jnp.float32), fine_w, fine_stored, fine_back)
-    grad_previous = jnp.sum(grad_fine_in.reshape(patches, PATCH, D), 1)
+    (layer_rows, grad_fine_in, grad_previous, fine_vectors, normed, mixture, second, hidden, grad_middle, grad_lifted,
+     grad_triple) = fine_block(byte_rows, previous, cotangent[0], small, fine_full.reshape(D, -1))
+    fine_grads = [
+        left_product(*pair).astype(jnp.bfloat16)
+        for pair in ((normed, grad_triple), (grad_middle, mixture), (second, grad_lifted), (cotangent[0], hidden))
+    ]
     grad_previous = lax.all_gather(grad_previous, "seq", axis=0, tiled=True) * joined
     grad_coarse_out = jnp.concatenate([grad_previous[1:], jnp.zeros((1, D), jnp.float32)])
     grad_embedded, coarse_grads = block_backward_t(grad_coarse_out, coarse_w, coarse_stored, coarse_back)
     grad_embed_low = grad_embedded.astype(jnp.bfloat16)
-    grad_patch = left_product(grouped_bytes, grad_embed_low)
+    grad_patch = left_product(grouped_bytes, grad_embed_low).astype(jnp.bfloat16)
     grad_here = lax.dynamic_slice_in_dim(grad_embed_low, core * patches, patches)
     grad_grouped = right_product(grad_here, patch_full)
     input_gradient = (grad_fine_in + grad_grouped.reshape(bytes_here, D)).astype(jnp.bfloat16)
-
-    def pack(grads):
-        return jnp.concatenate([grads[2], grads[3], grads[6], grads[7]], 1).astype(jnp.bfloat16).reshape(4, 4, 48, 12 * D)
-
     once = (core == 0).astype(jnp.float32)
-    small = jnp.stack([coarse_grads[i] * once for i in (0, 1, 4, 5)] + [fine_grads[i] for i in (0, 1, 4, 5)])
-    patch_shard, coarse_shard, fine_shard, small = reduce_all(
-        (grad_patch.astype(jnp.bfloat16).reshape(4, 4, 384, D), pack(coarse_grads), pack(fine_grads)), small
+    small = jnp.concatenate([jnp.stack([coarse_grads[i] * once for i in (0, 1, 4, 5)]), fine_vectors[4:]])
+    *shards, small = reduce_all(
+        [grad_patch] + [coarse_grads[i].astype(jnp.bfloat16) for i in (2, 3, 6, 7)] + fine_grads, small
     )
     small = lax.dynamic_slice_in_dim(small, at * vectors.shape[1], vectors.shape[1], 1)
 
-    def shards(full, first):
-        return (small[first], small[first + 1], full[:, : 3 * D], full[:, 3 * D : 4 * D].T, small[first + 2],
-                small[first + 3], full[:, 4 * D : 8 * D], full[:, 8 * D :].T)
-
-    return (layer_rows.astype(jnp.bfloat16)[None], input_gradient[None], patch_shard) + shards(coarse_shard, 0) + shards(fine_shard, 4)
+    def gradients(parts, first):
+        return (small[first], small[first + 1], parts[0], parts[1].T, small[first + 2], small[first + 3], parts[2], parts[3].T)
+
+    return (layer_rows[None], input_gradient[None], shards[0]) + gradients(shards[1:5], 0) + gradients(shards[5:], 4)
 
 
 def block_forward_t(inputs, weights, attend):
@@ -968,6 +957,184 @@
     )
 
 
+def normalize(values):
+    centred = values - jnp.mean(values, -1, keepdims=True)
+    scale = lax.rsqrt(jnp.mean(centred * centred, -1, keepdims=True) + epsilon)
+    return centred * scale, scale
+
+
+def normalize_back(grad, unit, scale, norm_gain):
+    scaled = grad * norm_gain
+    return scale * (
+        scaled - jnp.mean(scaled, -1, keepdims=True) - unit * jnp.mean(scaled * unit, -1, keepdims=True)
+    )
+
+
+def gate_both(values):
+    root = math.sqrt(2.0 / math.pi)
+    square = values * values
+    bend = jnp.tanh(root * values * (1.0 + 0.044715 * square))
+    half = 0.5 + 0.5 * bend
+    slope = half + 0.5 * values * (1.0 - bend * bend) * (root * (1.0 + 3.0 * 0.044715 * square))
+    return values * half, slope
+
+
+def head_lanes(pair):
+    lane = lax.broadcasted_iota(jnp.int32, pair.shape, 1)
+    zero = jnp.zeros_like(pair)
+    return jnp.where(lane < HEAD_DIM, pair, zero), jnp.where(lane < HEAD_DIM, zero, pair)
+
+
+def chances_of(queries, keys, allowed):
+    scores = right_product(queries, keys) * (1.0 / math.sqrt(HEAD_DIM))
+    scores = jnp.where(allowed, scores, -1e30)
+    powers = jnp.exp(scores - jnp.max(scores, -1, keepdims=True))
+    return powers * (1.0 / jnp.sum(powers, -1, keepdims=True))
+
+
+TILE = 128
+PAIRS = 6
+
+
+def fine_kernel(byte_ref, previous_ref, cotangent_ref, small_ref, w_ref,
+                out_ref, grad_in_ref, patch_grad_ref, vectors_ref,
+                normed_ref, mixture_ref, second_ref, hidden_ref, low_ref, lifted_grad_ref, triple_grad_ref,
+                triple, chances, result, grad_second):
+    rows = byte_ref.shape[0]
+    bf = jnp.bfloat16
+    first_gain, first_bias, second_gain, second_bias = (small_ref[i : i + 1] for i in (4, 5, 6, 7))
+    previous = previous_ref[...]
+    inputs = (
+        byte_ref[...].astype(jnp.float32).reshape(rows // PATCH, PATCH, D) + previous[:, None, :]
+    ).reshape(rows, D)
+    unit_one, scale_one = normalize(inputs)
+    normed = (unit_one * first_gain + first_bias).astype(bf)
+    normed_ref[...] = normed
+    triple[...] = product(normed, w_ref[:, : 3 * D]).astype(bf)
+    row = lax.broadcasted_iota(jnp.int32, (TILE, TILE), 0)
+    column = lax.broadcasted_iota(jnp.int32, (TILE, TILE), 1)
+    allowed = (row // PATCH == column // PATCH) & (column <= row)
+    tiles = rows // TILE
+
+    def attend(pair, _):
+        lanes = [pl.ds(pl.multiple_of(i * D + pair * 128, 128), 128) for i in range(3)]
+        for tile in range(tiles):
+            here = slice(tile * TILE, tile * TILE + TILE)
+            queries = head_lanes(triple[here, lanes[0]])
+            keys = triple[here, lanes[1]]
+            values = head_lanes(triple[here, lanes[2]])
+            mixed = None
+            for head in range(2):
+                found = chances_of(queries[head], keys, allowed)
+                chances[pair * 2 + head, here] = found
+                term = product(found.astype(bf), values[head])
+                mixed = term if mixed is None else mixed + term
+            mixture_ref[here, lanes[0]] = mixed.astype(bf)
+        return 0
+
+    lax.fori_loop(0, PAIRS, attend, 0)
+    middle = inputs + right_product(mixture_ref[...], w_ref[:, 3 * D : 4 * D])
+    unit_two, scale_two = normalize(middle)
+    second = (unit_two * second_gain + second_bias).astype(bf)
+    second_ref[...] = second
+    grad_low = cotangent_ref[...]
+    result[...] = middle
+    for j in range(4):
+        here = slice(j * D, j * D + D)
+        expand = w_ref[:, 4 * D + j * D : 5 * D + j * D]
+        narrow_t = w_ref[:, 8 * D + j * D : 9 * D + j * D]
+        hidden, slope = gate_both(product(second, expand))
+        hidden = hidden.astype(bf)
+        hidden_ref[:, here] = hidden
+        lifted_grad = (product(grad_low, narrow_t) * slope).astype(bf)
+        lifted_grad_ref[:, here] = lifted_grad
+        result[...] += right_product(hidden, narrow_t)
+        term = right_product(lifted_grad, expand)
+        if j:
+            grad_second[...] += term
+        else:
+            grad_second[...] = term
+    out_ref[...] = result[...].astype(bf)
+    grad_two = grad_second[...]
+    grad_middle = grad_low.astype(jnp.float32) + normalize_back(grad_two, unit_two, scale_two, second_gain)
+    low = grad_middle.astype(bf)
+    low_ref[...] = low
+    grad_second[...] = grad_middle
+    grad_mixture = product(low, w_ref[:, 3 * D : 4 * D]).astype(bf)
+    result[...] = grad_mixture.astype(jnp.float32)
+
+    def attend_back(pair, _):
+        lanes = [pl.ds(pl.multiple_of(i * D + pair * 128, 128), 128) for i in range(3)]
+        factor = 1.0 / math.sqrt(HEAD_DIM)
+        for tile in range(tiles):
+            here = slice(tile * TILE, tile * TILE + TILE)
+            queries = head_lanes(triple[here, lanes[0]])
+            keys = head_lanes(triple[here, lanes[1]])
+            values = triple[here, lanes[2]]
+            mixed = head_lanes(result[here, lanes[0]].astype(bf))
+            sums = [None, None, None]
+            for head in range(2):
+                found = chances[pair * 2 + head, here]
+                grad = right_product(mixed[head], values)
+                scores = (found * (grad - jnp.sum(grad * found, -1, keepdims=True))).astype(bf)
+                terms = (
+                    product(scores, keys[head]),
+                    left_product(scores, queries[head]),
+                    left_product(found.astype(bf), mixed[head]),
+                )
+                sums = [t if s is None else s + t for s, t in zip(sums, terms)]
+            triple_grad_ref[here, lanes[0]] = (sums[0] * factor).astype(bf)
+            triple_grad_ref[here, lanes[1]] = (sums[1] * factor).astype(bf)
+            triple_grad_ref[here, lanes[2]] = sums[2].astype(bf)
+        return 0
+
+    lax.fori_loop(0, PAIRS, attend_back, 0)
+    grad_one = right_product(triple_grad_ref[...], w_ref[:, : 3 * D])
+    grad_in = grad_second[...] + normalize_back(grad_one, unit_one, scale_one, first_gain)
+    grad_in_ref[...] = grad_in
+    patch_grad_ref[...] = jnp.sum(grad_in.reshape(rows // PATCH, PATCH, D), 1)
+    terms = [jnp.sum(t, 0, keepdims=True) for t in (grad_one * unit_one, grad_one, grad_two * unit_two, grad_two)]
+
+    @pl.when(pl.program_id(0) == 0)
+    def _():
+        vectors_ref[...] = jnp.zeros_like(vectors_ref)
+
+    for i, term in enumerate(terms):
+        vectors_ref[4 + i : 5 + i] += term
+
+
+def fine_block(byte_rows, previous, cotangent, small, full, rows=256):
+    count = byte_rows.shape[0]
+    bf, f32 = jnp.bfloat16, jnp.float32
+
+    def spec(height, width):
+        return pl.BlockSpec((height, width), lambda i: (i, 0))
+
+    def whole(shape):
+        return pl.BlockSpec(shape, lambda i: (0, 0), pipeline_mode=pl.Buffered(1))
+
+    outs = [(rows, D, bf), (rows, D, f32), (rows // PATCH, D, f32), None]
+    outs += [(rows, D, bf)] * 3 + [(rows, 4 * D, bf), (rows, D, bf), (rows, 4 * D, bf), (rows, 3 * D, bf)]
+    steps = count // rows
+    return pl.pallas_call(
+        fine_kernel,
+        grid=(steps,),
+        out_shape=[
+            jax.ShapeDtypeStruct((o[0] * steps, o[1]), o[2]) if o else jax.ShapeDtypeStruct((8, D), f32) for o in outs
+        ],
+        in_specs=[spec(rows, D), spec(rows // PATCH, D), spec(rows, D), whole((8, D)), whole(full.shape)],
+        out_specs=[spec(o[0], o[1]) if o else pl.BlockSpec((8, D), lambda i: (0, 0)) for o in outs],
+        scratch_shapes=[
+            pltpu.VMEM((rows, 3 * D), bf),
+            pltpu.VMEM((2 * PAIRS, rows, TILE), f32),
+            pltpu.VMEM((rows, D), f32),
+            pltpu.VMEM((rows, D), f32),
+        ],
+        compiler_params=pltpu.CompilerParams(dimension_semantics=("arbitrary",), vmem_limit_bytes=64_000_000),
+        name="fine_block",
+    )(byte_rows, previous, cotangent, small, full)
+
+
 def solution(mesh):
     return jax.shard_map(
         fast_body if (mesh.shape["seq"], mesh.shape["fsdp"]) == (2, 16) else body,

time: 831 us -> 645 us (0.78)
  local copies, waits for them, and re-layouts: 154 us -> 28.4 us
  matrix products: 200 us -> 92 us
  Pallas kernels: 404 us -> 492 us
  other arithmetic: 60.2 us -> 10.4 us
  blocking collectives: 2.53 us -> 14.9 us
    pallas_call x1 -> x2, Pallas kernels: 231 us -> 319 us  [the longest x1 231 us: reduce_all(): pl.pallas_call(kernel, out_shape=[jax.ShapeDtypeStruct(g.shape[2:], jnp.f...]
    convert_element_type x6 -> x0, local copies, waits for them, and re-layouts: 65.2 us -> none  [the longest x3 49.7 us: backward(): return jnp.stack(grads, 2).astype(jnp.bfloat16).reshape(rows, 3 * D)]
    dot_general x9 -> x5, matrix products: 54.5 us -> 20.7 us  [right_product(): lax.dot_general(left_side, right_side, (((1,), (1,)), ((), ())), preferre...]
    dot_general x9 -> x5, matrix products: 54.9 us -> 22 us  [product(): return jnp.dot(left_side, right_side, preferred_element_type=jnp.float32)]
    dot_general x6 -> x0, local copies, waits for them, and re-layouts: 25.4 us -> none  [the longest x1 6.75 us: attend_backward(): jnp.einsum('bhqk,bkhd->bqhd', grad_scores, key_part, preferred_element_ty...]
    reshape x6 -> x0, local copies, waits for them, and re-layouts: 22.7 us -> none  [the longest x1 14.9 us: forward(): grouped = triple.reshape(shape + (3, D // HEAD_DIM, HEAD_DIM))]
    concatenate x2 -> x0, other arithmetic: 21.6 us -> none  [pack(): jnp.concatenate([grads[2], grads[3], grads[6], grads[7]], 1)]
    dot_general x2 -> x1, matrix products: 13.5 us -> 1.07 us  [attend_backward(): jnp.einsum('bqhd,bkhd->bhqk', grad_mixture, value_part, preferred_element...]
where the time goes in v2:
time: 645 us; the launch traced here: 639 us
  Pallas kernels  492 us (76%)
  matrix products  92 us (14%)
  local copies, waits for them, and re-layouts  28.4 us (4%)
  blocking collectives  14.9 us (2%)
  other arithmetic  10.4 us (2%)
    pallas_call x1, Pallas kernels, reduce_all(): pl.pallas_call(kernel, out_shape=[jax.ShapeDtypeStruct(g.shape[2:], jnp.f...  231 us
    pallas_call x1, Pallas kernels, gather_all(): pl.pallas_call(functools.partial(gather_kernel, plan, ahead), out_shape=(...  173 us
    pallas_call x1, Pallas kernels, fine_block(): pl.pallas_call(fine_kernel, grid=(steps,), out_shape=[jax.ShapeDtypeStruc...  87.7 us
    dot_general x9, matrix products, left_product(): lax.dot_general(left_side, right_side, (((0,), (0,)), ((), ())), preferre...  43.8 us
    dot_general x5, matrix products, product(): return jnp.dot(left_side, right_side, preferred_element_type=jnp.float32)  22 us
    dot_general x5, matrix products, right_product(): lax.dot_general(left_side, right_side, (((1,), (1,)), ((), ())), preferre...  20.7 us
    all_gather x1, blocking collectives, fast_body(): lax.all_gather(grad_previous, 'seq', axis=0, tiled=True) * joined  14.9 us

profile of v2, /device:TPU:0, one launch (start us, length us, event | category | flops | bytes accessed | tf_op | source)
XLA Modules:
  0.0 639.4 jit_solution(10451247394864079358)
XLA Ops:
  3.7 173.2 %gather_all.1 = (bf16[4,4,384,768]{3,2,1,0:T(8,128)(2,1)}, bf16[4,4,48,9216]{3,2,1,0:T(8,128)(2,1)}, bf16[4,4,48,9216]{3,2,1,0:T(8,128)(2,1)}, f32[8,768]{1,0:T(8,128)}, bf16[2,1024,768]{2,1,0:T(8,128)(2,1)}) custom-call(bf16[384,768]{1,0:T(8,128)(2,1)} %refs_0_.1, bf16[48,2304]{1,0:T(8,128)(2,1)} %refs_1_.1, bf16[48,768]{1,0:T(8,128)(2,1)} %bitcast.162, ...), custom_call_target="tpu_custom_call" | custom-call | tf_op jit(solution)/shard_map/gather_all/pallas_call | solution.py:579
  177.0 5.7 reshape.339
  182.7 7.3 %fusion.52 = (f32[256]{0:T(256)S(1)}, f32[256,768]{1,0:T(8,128)S(1)}) fusion(bf16[256,6144]{1,0:T(8,128)(2,1)} %reshape.339, bf16[6144,768]{1,0:T(8,128)(2,1)} %bitcast.121), kind=kOutput, calls=%fused_computation.123 | convolution fusion | flops 2416115456 | bytes 13370368 | tf_op jit(solution)/shard_map/dot_general | solution.py:38
  190.3 3.2 convolution_convert_fusion.7
  199.2 3.8 fusion.6
  203.0 5.5 fusion.2
  209.5 87.7 %fine_block.1 = (bf16[1024,768]{1,0:T(8,128)(2,1)}, f32[1024,768]{1,0:T(8,128)}, f32[128,768]{1,0:T(8,128)}, f32[8,768]{1,0:T(8,128)}, bf16[1024,768]{1,0:T(8,12...) custom-call(bf16[1024,768]{1,0:T(8,128)(2,1)} %bitcast.129, ...), custom_call_target="tpu_custom_call" | custom-call | tf_op jit(solution)/shard_map/fine_block/pallas_call | solution.py:1119
  298.6 14.9 %all_gather.3 = f32[256,768]{1,0:T(8,128)S(1)} all-gather(f32[128,768]{1,0:T(8,128)} %get-tuple-element.52), channel_id=1, replica_groups=mesh['seq'=2,'fsdp'=16] {'seq'}, dimensions={0}, use_global_device_ids=true | all-gather | bytes 1179648 | tf_op jit(solution)/shard_map/all_gather | solution.py:898
  313.6 4.7 convolution_convert_fusion.8
  318.3 5.2 fusion.14
  323.5 4.5 multiply_reduce_fusion.1
  329.8 2.5 convolution_convert_fusion.11
  335.7 3.7 convolution_convert_fusion.4
  341.0 3.8 convolution_convert_fusion.5
  348.0 3.9 multiply_reduce_fusion.2
  352.5 4.8 fusion.34
  357.3 4.4 reshape.348
  361.7 4.3 fusion.22
  366.7 3.1 convolution_convert_fusion.6
  369.8 7.8 %convolution_convert_fusion.3 = bf16[768,2304]{1,0:T(8,128)(2,1)} fusion(bf16[1024,768]{1,0:T(8,128)(2,1)S(1)} %copy-done.45, bf16[1024,2304]{1,0:T(8,128)(2,1)} %get-tuple-element.54), kind=kOutput, calls=%fused_computation.3 | convolution fusion | flops 3625648128 | bytes 9830400 | tf_op jit(solution)/shard_map/dot_general | solution.py:42
  377.7 6.9 %convolution_convert_fusion.2 = bf16[768,3072]{1,0:T(8,128)(2,1)} fusion(bf16[1024,768]{1,0:T(8,128)(2,1)S(1)} %copy-done.44, bf16[1024,3072]{1,0:T(8,128)(2,1)S(1)} %bitcast.176), kind=kOutput, calls=%fused_computation.2 | convolution fusion | flops 4834197504 | bytes 12582912 | tf_op jit(solution)/shard_map/dot_general | solution.py:42
  384.6 7.1 %convolution_convert_fusion.1 = bf16[3072,768]{0,1:T(8,128)(2,1)} fusion(bf16[1024,3072]{1,0:T(8,128)(2,1)S(1)} %bitcast.174, bf16[1,1024,768]{2,1,0:T(8,128)(2,1)S(1)} %copy-done.13), kind=kOutput, calls=%fused_computation.1 | convolution fusion | flops 4834197504 | bytes 12582912 | tf_op jit(solution)/shard_map/dot_general | solution.py:42
  391.8 5.1 convolution_convert_fusion
  396.9 230.9 %reduce_all.1 = (f32[384,768]{1,0:T(8,128)}, f32[48,2304]{1,0:T(8,128)}, f32[48,768]{1,0:T(8,128)}, f32[48,3072]{1,0:T(8,128)}, f32[48,3072]{1,0:T(8,128)}, /*in...) custom-call(bf16[4,4,384,768]{3,2,1,0:T(8,128)(2,1)} %bitcast.120, ...), custom_call_target="tpu_custom_call" | custom-call | tf_op jit(solution)/shard_map/reduce_all/pallas_call | solution.py:827
  (175 shorter events, 33.3 us)
Async XLA Ops:
  3.7 192.1 %copy-start.18 = (pred[256,256]{0,1:T(8,128)(4,1)}, pred[256,256]{0,1:T(8,128)(4,1)S(1)}, u32[]{:S(2)}) copy-start(pred[256,256]{0,1:T(8,128)(4,1)S(1)} %fusion.33) | copy-start | bytes 196612
  177.0 5.7 copy-start.30
  190.0 6.8 %copy-start.4 = (f32[256,768]{1,0:T(8,128)}, f32[256,768]{1,0:T(8,128)S(1)}, u32[]{:S(2)}) copy-start(f32[256,768]{1,0:T(8,128)S(1)} %get-tuple-element.94) | copy-start | bytes 2359300
  198.9 129.2 %copy-start.2 = (f32[256,768]{1,0:T(8,128)}, f32[256,768]{1,0:T(8,128)S(1)}, u32[]{:S(2)}) copy-start(f32[256,768]{1,0:T(8,128)S(1)} %get-tuple-element.98) | copy-start | bytes 2359300
  198.9 129.2 %copy-start.34 = (f32[256]{0:T(256)}, f32[256]{0:T(256)S(1)}, u32[]{:S(2)}) copy-start(f32[256]{0:T(256)S(1)} %broadcast_multiply_fusion.4) | copy-start | bytes 3076
  199.2 128.9 %copy-start.38 = (f32[256]{0:T(256)}, f32[256]{0:T(256)S(1)}, u32[]{:S(2)}) copy-start(f32[256]{0:T(256)S(1)} %fusion.40) | copy-start | bytes 3076
  203.0 5.5 copy-start.46
  313.6 14.9 %copy-start.11 = (f32[255,768]{1,0:T(8,128)}, f32[255,768]{1,0:T(8,128)S(1)}, u32[]{:S(2)}) copy-start(f32[255,768]{1,0:T(8,128)S(1)} %slice_multiply_fusion) | copy-start | bytes 2350084
  335.7 5.3 copy-start.35
  346.8 5.7 slice-start
  366.7 11.0 %slice-start.5 = ((s8[6291456]{0:T(1024)(128)(4,1)}), s8[4194304]{0:T(1024)(128)(4,1)S(1)}, s32[]{:S(2)}) async-start(s8[6291456]{0:T(1024)(128)(4,1)} %bitcast.175), calls=%async_computation.5 | async-start | bytes 8388608
  369.8 7.8 %slice-start.6 = ((s8[6291456]{0:T(1024)(128)(4,1)}), s8[2097152]{0:T(1024)(128)(4,1)S(1)}, s32[]{:S(2)}) async-start(s8[6291456]{0:T(1024)(128)(4,1)} %bitcast.175), calls=%async_computation.6 | async-start | bytes 4194304
  369.8 7.8 %copy-start.44 = (bf16[1024,768]{1,0:T(8,128)(2,1)S(1)}, bf16[1024,768]{1,0:T(8,128)(2,1)}, u32[]{:S(2)}) copy-start(bf16[1024,768]{1,0:T(8,128)(2,1)} %get-tuple-element.57) | copy-start | bytes 4718596
  369.8 14.8 %slice-start.3 = ((s8[6291456]{0:T(1024)(128)(4,1)}), s8[4194304]{0:T(1024)(128)(4,1)S(1)}, s32[]{:S(2)}) async-start(s8[6291456]{0:T(1024)(128)(4,1)} %bitcast.173), calls=%async_computation.3 | async-start | bytes 8388608
  377.7 7.0 %copy-start.13 = (bf16[1,1024,768]{2,1,0:T(8,128)(2,1)S(1)}, bf16[1,1024,768]{2,1,0:T(8,128)(2,1)}, u32[]{:S(2)}) copy-start(bf16[1,1024,768]{2,1,0:T(8,128)(2,1)} %param.22) | copy-start | bytes 4718596
  377.7 6.9 %slice-start.4 = ((s8[6291456]{0:T(1024)(128)(4,1)}), s8[2097152]{0:T(1024)(128)(4,1)S(1)}, s32[]{:S(2)}) async-start(s8[6291456]{0:T(1024)(128)(4,1)} %bitcast.173), calls=%async_computation.4 | async-start | bytes 4194304
  384.6 7.1 %copy-start.6 = (bf16[256,6144]{1,0:T(8,128)(2,1)S(1)}, bf16[256,6144]{1,0:T(8,128)(2,1)}, u32[]{:S(2)}) copy-start(bf16[256,6144]{1,0:T(8,128)(2,1)} %reshape.339) | copy-start | bytes 9437188
  627.8 5.8 copy-start.28
  627.8 6.4 %copy-start.23 = (f32[48,3072]{1,0:T(8,128)S(1)}, f32[48,3072]{1,0:T(8,128)}, u32[]{:S(2)}) copy-start(f32[48,3072]{1,0:T(8,128)} %get-tuple-element.135) | copy-start | bytes 1769476
  627.8 7.3 %copy-start.22 = (f32[48,3072]{1,0:T(8,128)S(1)}, f32[48,3072]{1,0:T(8,128)}, u32[]{:S(2)}) copy-start(f32[48,3072]{1,0:T(8,128)} %get-tuple-element.66) | copy-start | bytes 1769476
  627.8 8.1 %copy-start.24 = (f32[48,2304]{1,0:T(8,128)S(1)}, f32[48,2304]{1,0:T(8,128)}, u32[]{:S(2)}) copy-start(f32[48,2304]{1,0:T(8,128)} %get-tuple-element.139) | copy-start | bytes 1327108
  629.3 7.4 %copy-start.27 = (f32[48,768]{1,0:T(8,128)S(1)}, f32[48,768]{1,0:T(8,128)}, u32[]{:S(2)}) copy-start(f32[48,768]{1,0:T(8,128)} %get-tuple-element.68) | copy-start | bytes 442372
  629.3 8.0 %copy-start.21 = (f32[48,3072]{1,0:T(8,128)S(1)}, f32[48,3072]{1,0:T(8,128)}, u32[]{:S(2)}) copy-start(f32[48,3072]{1,0:T(8,128)} %get-tuple-element.143) | copy-start | bytes 1769476
  631.7 6.4 %copy-start.20 = (f32[48,3072]{1,0:T(8,128)S(1)}, f32[48,3072]{1,0:T(8,128)}, u32[]{:S(2)}) copy-start(f32[48,3072]{1,0:T(8,128)} %get-tuple-element.70) | copy-start | bytes 1769476
  (32 other events, 100.4 us)

commit v3 on v2

--- a/solution.py
+++ b/solution.py
@@ -419,8 +419,8 @@
 class Gather:
     EVENTS = 12
 
-    def __init__(self, place, source, buffer, rows, column, width, z_first, sends, receives, local):
-        self.p, self.source, self.buffer, self.rows = place, source, buffer, rows
+    def __init__(self, place, source, buffer, rows, first, column, width, z_first, sends, receives, local):
+        self.p, self.source, self.buffer, self.rows, self.first = place, source, buffer, rows, first
         self.z_first, self.sends, self.receives, self.local = z_first, sends, receives, local
         self.half = width // 2
         self.column, self.width = column, width
@@ -458,7 +458,7 @@
 
     def start(self):
         p = self.p
-        own = self.source.at[self.rows, pl.ds(pl.multiple_of(p.core * self.half, 128), self.half)]
+        own = self.source.at[self.rows, pl.ds(pl.multiple_of(self.first + p.core * self.half, 128), self.half)]
         self.copy = pltpu.make_async_copy(own, self.block(p.z, p.plane), self.local)
         self.copy.start()
         if not self.z_first:
@@ -549,9 +549,9 @@
     )
     cross.start()
     gathers = []
-    for k, (source, buffer, first, rows, column, width, z_first) in enumerate(plan):
+    for k, (source, buffer, first, rows, start, column, width, z_first) in enumerate(plan):
         gathers.append(
-            Gather(place, sources[source], buffers[buffer], pl.ds(first, rows), column, width, z_first,
+            Gather(place, sources[source], buffers[buffer], pl.ds(first, rows), start, column, width, z_first,
                    sends.at[k], receives.at[k], local.at[k])
         )
     run_gathers(gathers, ahead, total.advance)
@@ -559,21 +559,23 @@
     cross.wait()
 
 
-PLAN = (
-    (0, 0, 0, 192, 0, 768, True),
-    (0, 0, 192, 192, 0, 768, False),
-    (1, 1, 0, 48, 0, 2304, True),
-    (2, 1, 0, 48, 2304, 768, True),
-    (3, 1, 0, 48, 3072, 3072, True),
-    (4, 1, 0, 48, 6144, 3072, False),
-    (5, 2, 0, 48, 0, 2304, True),
-    (6, 2, 0, 48, 2304, 768, True),
-    (7, 2, 0, 48, 3072, 3072, False),
-    (8, 2, 0, 48, 6144, 3072, True),
-)
-
-
-def gather_all(sources, small, rows, ahead=2, plan=PLAN):
+def forward_plan(step=1536, patch_rows=96):
+    plan = []
+    for first in range(0, 384, patch_rows):
+        plan.append((0, 0, first, patch_rows, 0, 0, 768))
+    for block in (1, 2):
+        column = 0
+        for i, width in enumerate((2304, 768, 3072, 3072)):
+            for start in range(0, width, step):
+                plan.append((4 * block - 3 + i, block, 0, 48, start, column + start, min(step, width - start)))
+            column += width
+    return tuple(p + (i % 5 != 4,) for i, p in enumerate(plan))
+
+
+PLAN = forward_plan()
+
+
+def gather_all(sources, small, rows, ahead=3, plan=PLAN):
     n = len(plan)
     bf = jnp.bfloat16
     return pl.pallas_call(
@@ -733,19 +735,19 @@
         self.arrived(10, self.out.at[self.rows, self.theirs])
 
 
-BACK_PLAN = (
-    (8, 0, 48, 3072, True),
-    (7, 0, 48, 3072, False),
-    (6, 0, 48, 768, True),
-    (5, 0, 48, 2304, True),
-    (4, 0, 48, 3072, True),
-    (3, 0, 48, 3072, False),
-    (2, 0, 48, 768, True),
-    (1, 0, 48, 2304, True),
-    (0, 0, 192, 768, False),
-    (0, 192, 192, 768, True),
-)
-SLOTS = 3
+def backward_plan(step=1536, patch_rows=96):
+    plan = []
+    for array, width in ((8, 3072), (7, 3072), (6, 768), (5, 2304), (4, 3072), (3, 3072), (2, 768), (1, 2304)):
+        for start in range(0, width, step):
+            plan.append((array, 0, 48, start, min(step, width - start)))
+    for first in range(0, 384, patch_rows):
+        plan.append((0, first, patch_rows, 0, 768))
+    return tuple(p + (i % 5 != 4,) for i, p in enumerate(plan))
+
+
+BACK_PLAN = backward_plan()
+SLOTS = 8
+LAGS = (2, 3, 4, 5)
 ARRAYS = 9
 
 
@@ -758,16 +760,16 @@
     total = Total(place, (0, 1, 2, 4, 8), value, arriving, small_sends, small_receives, small_out)
     used = [0, 0]
     reduces, copies = [], []
-    for k, (array, first, rows, width, z_last) in enumerate(plan):
+    for k, (array, first, rows, column, width, z_last) in enumerate(plan):
         kind = 0 if array == 0 else 1
-        slot = used[kind] % SLOTS if kind else used[kind]
+        slot = used[kind] % SLOTS
         used[kind] += 1
         half = width // 2
-        cut = (lambda ref, kind=kind, half=half: ref if not kind or half == 1536 else ref.at[..., pl.ds(0, half)])
+        cut = (lambda ref, half=half: ref if half == ref.shape[-1] else ref.at[..., pl.ds(0, half)])
         reduces.append(
             Reduce(place, cut(slots[kind].at[slot]), cut(pairs.at[used[kind] - 1]) if array > 4 else None, cut(fars[kind].at[used[kind] - 1]),
                    cut(nears[kind].at[used[kind] - 1]), cut(lines[kind].at[used[kind] - 1]), outs[array],
-                   pl.ds(first, rows), 0, width, z_last, sends.at[k], receives.at[k])
+                   pl.ds(first, rows), column, width, z_last, sends.at[k], receives.at[k])
         )
 
     def load(k):
@@ -781,20 +783,16 @@
         if array > 4:
             r.pair(grads[array].at[:, :, r.rows, r.theirs])
 
-    for t in range(n + 4):
-        if t - 4 >= 0:
-            reduces[t - 4].five()
-        if 0 <= t - 3 < n:
-            reduces[t - 3].four()
-        if t < n:
-            load(t)
-        if 0 <= t - 2 < n:
-            reduces[t - 2].three()
-        if 0 <= t - 1 < n:
-            reduces[t - 1].two()
+    load(0)
+    for t in range(n + LAGS[-1]):
+        if t + 1 < n:
+            load(t + 1)
         if t < n:
             copies[t].wait()
             reduces[t].one()
+        for lag, name in zip(LAGS, ("two", "three", "four", "five")):
+            if 0 <= t - lag < n:
+                getattr(reduces[t - lag], name)()
         total.advance()
     for r in reduces:
         r.drain()
@@ -803,7 +801,8 @@
 def reduce_all(grads, small, plan=BACK_PLAN):
     n = len(plan)
     bf = jnp.bfloat16
-    shapes = ((2, 192, 384), (8, 48, 1536))
+    counts = [sum(p[0] == 0 for p in plan), sum(p[0] > 0 for p in plan), sum(p[0] > 4 for p in plan)]
+    shapes = tuple((max(p[2] for p in plan if c(p[0])), max(p[4] for p in plan if c(p[0])) // 2) for c in (lambda a: a == 0, lambda a: a > 0))
 
     def kernel(*refs):
         grads, small, outs, small_out = refs[:ARRAYS], refs[ARRAYS], refs[ARRAYS + 1 : 2 * ARRAYS + 1], refs[2 * ARRAYS + 1]
@@ -811,9 +810,10 @@
         slots, fars, nears, lines = (rest[2 * i : 2 * i + 2] for i in range(4))
         reduce_kernel(plan, grads, small, outs, small_out, slots, pairs, fars, nears, lines, *rest[8:])
 
-    scratch = [pltpu.VMEM((4, 4, 4, 48, 1536), bf)]
-    for lead in (((2, 4, 4), (SLOTS, 4, 4)), ((2, 2, 4), (8, 2, 4)), ((2, 4), (8, 4)), ((2, 6), (8, 6))):
-        scratch += [pltpu.VMEM(lead[i] + shapes[i][1:], bf) for i in (0, 1)]
+    scratch = [pltpu.VMEM((counts[2], 4, 4) + shapes[1], bf)]
+    scratch += [pltpu.VMEM((min(SLOTS, counts[i]), 4, 4) + shapes[i], bf) for i in (0, 1)]
+    for lead in ((2, 4), (4,), (6,)):
+        scratch += [pltpu.VMEM((counts[i],) + lead + shapes[i], bf) for i in (0, 1)]
     scratch += [
         pltpu.SemaphoreType.DMA((n, 11)),
         pltpu.SemaphoreType.DMA((n, 11)),

time: 645 us -> 577 us (0.89)
  Pallas kernels: 492 us -> 434 us
  blocking collectives: 14.9 us -> 3.26 us
    pallas_call x1, Pallas kernels: 231 us -> 178 us  [reduce_all(): pl.pallas_call(kernel, out_shape=[jax.ShapeDtypeStruct(g.shape[2:], jnp.f...]
    all_gather x1, blocking collectives: 14.9 us -> 3.26 us  [fast_body(): lax.all_gather(grad_previous, 'seq', axis=0, tiled=True) * joined]
where the time goes in v3:
time: 577 us; the launch traced here: 570 us
  Pallas kernels  434 us (75%)
  matrix products  92.2 us (16%)
  local copies, waits for them, and re-layouts  28.5 us (5%)
  other arithmetic  10.4 us (2%)
    pallas_call x1, Pallas kernels, reduce_all(): pl.pallas_call(kernel, out_shape=[jax.ShapeDtypeStruct(g.shape[2:], jnp.f...  178 us
    pallas_call x1, Pallas kernels, gather_all(): pl.pallas_call(functools.partial(gather_kernel, plan, ahead), out_shape=(...  168 us
    pallas_call x1, Pallas kernels, fine_block(): pl.pallas_call(fine_kernel, grid=(steps,), out_shape=[jax.ShapeDtypeStruc...  87.6 us
    dot_general x9, matrix products, left_product(): lax.dot_general(left_side, right_side, (((0,), (0,)), ((), ())), preferre...  43.8 us
    dot_general x5, matrix products, product(): return jnp.dot(left_side, right_side, preferred_element_type=jnp.float32)  22 us
    dot_general x5, matrix products, right_product(): lax.dot_general(left_side, right_side, (((1,), (1,)), ((), ())), preferre...  20.7 us

profile of v3, /device:TPU:0, one launch (start us, length us, event | category | flops | bytes accessed | tf_op | source)
XLA Modules:
  0.0 570.3 jit_solution(11150684193690821353)
XLA Ops:
  3.7 168.5 %gather_all.1 = (bf16[4,4,384,768]{3,2,1,0:T(8,128)(2,1)}, bf16[4,4,48,9216]{3,2,1,0:T(8,128)(2,1)}, bf16[4,4,48,9216]{3,2,1,0:T(8,128)(2,1)}, f32[8,768]{1,0:T(8,128)}, bf16[2,1024,768]{2,1,0:T(8,128)(2,1)}) custom-call(bf16[384,768]{1,0:T(8,128)(2,1)} %refs_0_.1, bf16[48,2304]{1,0:T(8,128)(2,1)} %refs_1_.1, bf16[48,768]{1,0:T(8,128)(2,1)} %bitcast.162, ...), custom_call_target="tpu_custom_call" | custom-call | tf_op jit(solution)/shard_map/gather_all/pallas_call | solution.py:581
  172.2 5.7 %reshape.339 = bf16[256,6144]{1,0:T(8,128)(2,1)} reshape(bf16[2,1024,768]{2,1,0:T(8,128)(2,1)} %get-tuple-element.45) | data formatting | bytes 6291456 | tf_op jit(solution)/shard_map/reshape | solution.py:885
  178.0 7.3 %fusion.52 = (f32[256]{0:T(256)S(1)}, f32[256,768]{1,0:T(8,128)S(1)}) fusion(bf16[256,6144]{1,0:T(8,128)(2,1)} %reshape.339, bf16[6144,768]{1,0:T(8,128)(2,1)} %bitcast.121), kind=kOutput, calls=%fused_computation.123 | convolution fusion | flops 2416115456 | bytes 13370368 | tf_op jit(solution)/shard_map/dot_general | solution.py:38
  185.5 3.2 convolution_convert_fusion.7
  194.7 3.8 fusion.6
  198.6 5.5 fusion.2
  205.1 87.6 %fine_block.1 = (bf16[1024,768]{1,0:T(8,128)(2,1)}, f32[1024,768]{1,0:T(8,128)}, f32[128,768]{1,0:T(8,128)}, f32[8,768]{1,0:T(8,128)}, bf16[1024,768]{1,0:T(8,12...) custom-call(bf16[1024,768]{1,0:T(8,128)(2,1)} %bitcast.129, ...), custom_call_target="tpu_custom_call" | custom-call | tf_op jit(solution)/shard_map/fine_block/pallas_call | solution.py:1119
  294.0 3.3 all_gather.3
  297.4 4.7 convolution_convert_fusion.8
  302.1 5.2 fusion.14
  307.3 4.5 multiply_reduce_fusion.1
  313.6 2.5 convolution_convert_fusion.11
  319.5 3.7 convolution_convert_fusion.4
  324.8 3.8 convolution_convert_fusion.5
  332.0 3.9 multiply_reduce_fusion.2
  336.4 4.8 fusion.34
  341.2 4.2 reshape.348
  345.5 4.3 fusion.22
  350.5 3.1 convolution_convert_fusion.6
  353.6 7.8 %convolution_convert_fusion.3 = bf16[768,2304]{1,0:T(8,128)(2,1)} fusion(bf16[1024,768]{1,0:T(8,128)(2,1)S(1)} %copy-done.45, bf16[1024,2304]{1,0:T(8,128)(2,1)} %get-tuple-element.54), kind=kOutput, calls=%fused_computation.3 | convolution fusion | flops 3625648128 | bytes 9830400 | tf_op jit(solution)/shard_map/dot_general | solution.py:42
  361.5 6.9 %convolution_convert_fusion.2 = bf16[768,3072]{1,0:T(8,128)(2,1)} fusion(bf16[1024,768]{1,0:T(8,128)(2,1)S(1)} %copy-done.44, bf16[1024,3072]{1,0:T(8,128)(2,1)S(1)} %bitcast.176), kind=kOutput, calls=%fused_computation.2 | convolution fusion | flops 4834197504 | bytes 12582912 | tf_op jit(solution)/shard_map/dot_general | solution.py:42
  368.4 7.1 %convolution_convert_fusion.1 = bf16[3072,768]{0,1:T(8,128)(2,1)} fusion(bf16[1024,3072]{1,0:T(8,128)(2,1)S(1)} %bitcast.174, bf16[1,1024,768]{2,1,0:T(8,128)(2,1)S(1)} %copy-done.13), kind=kOutput, calls=%fused_computation.1 | convolution fusion | flops 4834197504 | bytes 12582912 | tf_op jit(solution)/shard_map/dot_general | solution.py:42
  375.5 5.1 convolution_convert_fusion
  380.7 178.2 %reduce_all.1 = (f32[384,768]{1,0:T(8,128)}, f32[48,2304]{1,0:T(8,128)}, f32[48,768]{1,0:T(8,128)}, f32[48,3072]{1,0:T(8,128)}, f32[48,3072]{1,0:T(8,128)}, /*in...) custom-call(bf16[4,4,384,768]{3,2,1,0:T(8,128)(2,1)} %bitcast.120, ...), custom_call_target="tpu_custom_call" | custom-call | tf_op jit(solution)/shard_map/reduce_all/pallas_call | solution.py:827
  (175 shorter events, 33.8 us)
Async XLA Ops:
  3.7 187.6 %copy-start.18 = (pred[256,256]{0,1:T(8,128)(4,1)}, pred[256,256]{0,1:T(8,128)(4,1)S(1)}, u32[]{:S(2)}) copy-start(pred[256,256]{0,1:T(8,128)(4,1)S(1)} %fusion.33) | copy-start | bytes 196612
  172.2 5.7 %copy-start.30 = (f32[8,768]{1,0:T(8,128)S(1)}, f32[8,768]{1,0:T(8,128)}, u32[]{:S(2)}) copy-start(f32[8,768]{1,0:T(8,128)} %get-tuple-element.47.small_ref) | copy-start | bytes 73732
  185.3 7.1 %copy-start.4 = (f32[256,768]{1,0:T(8,128)}, f32[256,768]{1,0:T(8,128)S(1)}, u32[]{:S(2)}) copy-start(f32[256,768]{1,0:T(8,128)S(1)} %get-tuple-element.94) | copy-start | bytes 2359300
  194.4 117.4 %copy-start.2 = (f32[256,768]{1,0:T(8,128)}, f32[256,768]{1,0:T(8,128)S(1)}, u32[]{:S(2)}) copy-start(f32[256,768]{1,0:T(8,128)S(1)} %get-tuple-element.98) | copy-start | bytes 2359300
  194.5 117.4 %copy-start.34 = (f32[256]{0:T(256)}, f32[256]{0:T(256)S(1)}, u32[]{:S(2)}) copy-start(f32[256]{0:T(256)S(1)} %broadcast_multiply_fusion.4) | copy-start | bytes 3076
  194.7 117.2 %copy-start.38 = (f32[256]{0:T(256)}, f32[256]{0:T(256)S(1)}, u32[]{:S(2)}) copy-start(f32[256]{0:T(256)S(1)} %fusion.40) | copy-start | bytes 3076
  198.5 5.5 copy-start.46
  297.4 14.9 %copy-start.11 = (f32[255,768]{1,0:T(8,128)}, f32[255,768]{1,0:T(8,128)S(1)}, u32[]{:S(2)}) copy-start(f32[255,768]{1,0:T(8,128)S(1)} %slice_multiply_fusion) | copy-start | bytes 2350084
  319.5 5.3 copy-start.35
  330.8 5.6 slice-start
  350.5 11.0 %slice-start.5 = ((s8[6291456]{0:T(1024)(128)(4,1)}), s8[4194304]{0:T(1024)(128)(4,1)S(1)}, s32[]{:S(2)}) async-start(s8[6291456]{0:T(1024)(128)(4,1)} %bitcast.175), calls=%async_computation.5 | async-start | bytes 8388608
  353.6 7.8 %slice-start.6 = ((s8[6291456]{0:T(1024)(128)(4,1)}), s8[2097152]{0:T(1024)(128)(4,1)S(1)}, s32[]{:S(2)}) async-start(s8[6291456]{0:T(1024)(128)(4,1)} %bitcast.175), calls=%async_computation.6 | async-start | bytes 4194304
  353.6 7.8 %copy-start.44 = (bf16[1024,768]{1,0:T(8,128)(2,1)S(1)}, bf16[1024,768]{1,0:T(8,128)(2,1)}, u32[]{:S(2)}) copy-start(bf16[1024,768]{1,0:T(8,128)(2,1)} %get-tuple-element.57) | copy-start | bytes 4718596
  353.6 14.8 %slice-start.3 = ((s8[6291456]{0:T(1024)(128)(4,1)}), s8[4194304]{0:T(1024)(128)(4,1)S(1)}, s32[]{:S(2)}) async-start(s8[6291456]{0:T(1024)(128)(4,1)} %bitcast.173), calls=%async_computation.3 | async-start | bytes 8388608
  361.4 7.0 %copy-start.13 = (bf16[1,1024,768]{2,1,0:T(8,128)(2,1)S(1)}, bf16[1,1024,768]{2,1,0:T(8,128)(2,1)}, u32[]{:S(2)}) copy-start(bf16[1,1024,768]{2,1,0:T(8,128)(2,1)} %param.22) | copy-start | bytes 4718596
  361.4 6.9 %slice-start.4 = ((s8[6291456]{0:T(1024)(128)(4,1)}), s8[2097152]{0:T(1024)(128)(4,1)S(1)}, s32[]{:S(2)}) async-start(s8[6291456]{0:T(1024)(128)(4,1)} %bitcast.173), calls=%async_computation.4 | async-start | bytes 4194304
  368.4 7.1 %copy-start.6 = (bf16[256,6144]{1,0:T(8,128)(2,1)S(1)}, bf16[256,6144]{1,0:T(8,128)(2,1)}, u32[]{:S(2)}) copy-start(bf16[256,6144]{1,0:T(8,128)(2,1)} %reshape.339) | copy-start | bytes 9437188
  558.9 5.8 %copy-start.28 = (f32[48,768]{1,0:T(8,128)S(1)}, f32[48,768]{1,0:T(8,128)}, u32[]{:S(2)}) copy-start(f32[48,768]{1,0:T(8,128)} %get-tuple-element.64) | copy-start | bytes 442372
  558.9 6.4 %copy-start.23 = (f32[48,3072]{1,0:T(8,128)S(1)}, f32[48,3072]{1,0:T(8,128)}, u32[]{:S(2)}) copy-start(f32[48,3072]{1,0:T(8,128)} %get-tuple-element.135) | copy-start | bytes 1769476
  558.9 7.3 %copy-start.22 = (f32[48,3072]{1,0:T(8,128)S(1)}, f32[48,3072]{1,0:T(8,128)}, u32[]{:S(2)}) copy-start(f32[48,3072]{1,0:T(8,128)} %get-tuple-element.66) | copy-start | bytes 1769476
  558.9 8.1 %copy-start.24 = (f32[48,2304]{1,0:T(8,128)S(1)}, f32[48,2304]{1,0:T(8,128)}, u32[]{:S(2)}) copy-start(f32[48,2304]{1,0:T(8,128)} %get-tuple-element.139) | copy-start | bytes 1327108
  560.4 7.4 %copy-start.27 = (f32[48,768]{1,0:T(8,128)S(1)}, f32[48,768]{1,0:T(8,128)}, u32[]{:S(2)}) copy-start(f32[48,768]{1,0:T(8,128)} %get-tuple-element.68) | copy-start | bytes 442372
  560.4 8.0 %copy-start.21 = (f32[48,3072]{1,0:T(8,128)S(1)}, f32[48,3072]{1,0:T(8,128)}, u32[]{:S(2)}) copy-start(f32[48,3072]{1,0:T(8,128)} %get-tuple-element.143) | copy-start | bytes 1769476
  562.8 6.4 %copy-start.20 = (f32[48,3072]{1,0:T(8,128)S(1)}, f32[48,3072]{1,0:T(8,128)}, u32[]{:S(2)}) copy-start(f32[48,3072]{1,0:T(8,128)} %get-tuple-element.70) | copy-start | bytes 1769476
  (32 other events, 100.4 us)

commit v4 on v3

--- a/solution.py
+++ b/solution.py
@@ -528,15 +528,81 @@
             gathers[t - 2].three()
         if 0 <= t - 3 < n:
             gathers[t - 3].four()
-        tick()
+        tick(t)
     for g in gathers:
         g.drain()
 
 
+class PatchForward:
+    def __init__(self, small, rows, patch, w, segments, outs):
+        self.small, self.rows, self.patch, self.w, self.segments = small, rows, patch, w, segments
+        self.embedded, self.normed, self.triple, self.chances, self.mixture = outs[:5]
+        self.middle, self.second, self.lifted, self.hidden, self.result = outs[5:]
+
+    def weight(self, column, width):
+        return self.w[:, :, :, column : column + width].reshape(D, width)
+
+    def embed(self, first):
+        def step(z, _):
+            columns = pl.ds(pl.multiple_of(z * 2 * D, 128), 2 * D)
+            rows = self.rows[:, :, columns].reshape(self.embedded.shape[0], 2 * D)
+            term = product(rows, self.patch[z].reshape(2 * D, D))
+            self.embedded[...] += term
+            return 0
+
+        if first == 0:
+            self.embedded[...] = jnp.zeros_like(self.embedded)
+        lax.fori_loop(first, first + 2, step, 0)
+
+    def project(self):
+        unit, _ = normalize(self.embedded[...])
+        self.normed[...] = (unit * self.small[0:1] + self.small[1:2]).astype(jnp.bfloat16)
+        self.triple[...] = product(self.normed[...], self.weight(0, 3 * D)).astype(jnp.bfloat16)
+
+    def attend(self, first):
+        count = self.triple.shape[0]
+        row = lax.broadcasted_iota(jnp.int32, (count, count), 0)
+        column = lax.broadcasted_iota(jnp.int32, (count, count), 1)
+        allowed = (column <= row) & (self.segments[1][...] == self.segments[0][...])
+
+        def step(pair, _):
+            lanes = [pl.ds(pl.multiple_of(i * D + pair * 128, 128), 128) for i in range(3)]
+            queries = head_lanes(self.triple[:, lanes[0]])
+            keys = self.triple[:, lanes[1]]
+            values = head_lanes(self.triple[:, lanes[2]])
+            mixed = None
+            for head in range(2):
+                found = chances_of(queries[head], keys, allowed)
+                self.chances[pair * 2 + head] = found
+                term = product(found.astype(jnp.bfloat16), values[head])
+                mixed = term if mixed is None else mixed + term
+            self.mixture[:, lanes[0]] = mixed.astype(jnp.bfloat16)
+            return 0
+
+        lax.fori_loop(first, first + 3, step, 0)
+
+    def join(self):
+        middle = self.embedded[...] + right_product(self.mixture[...], self.weight(3 * D, D))
+        self.middle[...] = middle
+        self.result[...] = middle
+        unit, _ = normalize(middle)
+        self.second[...] = (unit * self.small[2:3] + self.small[3:4]).astype(jnp.bfloat16)
+
+    def lift(self, half):
+        here = slice(half * 2 * D, half * 2 * D + 2 * D)
+        lifted = product(self.second[...], self.weight(4 * D + half * 2 * D, 2 * D))
+        self.lifted[:, here] = lifted
+        self.hidden[:, here] = smooth_gate(lifted).astype(jnp.bfloat16)
+
+    def lower(self, half):
+        here = slice(half * 2 * D, half * 2 * D + 2 * D)
+        self.result[...] += right_product(self.hidden[:, here], self.weight(8 * D + half * 2 * D, 2 * D))
+
+
 def gather_kernel(plan, ahead, *refs):
-    sources, small, rows, rest = refs[:9], refs[9], refs[10], refs[11:]
-    buffers, small_out, all_rows = rest[:3], rest[3], rest[4]
-    sends, receives, local, value, arriving, small_sends, small_receives, row_sems = rest[5:]
+    sources, small, rows, segments, rest = refs[:9], refs[9], refs[10], refs[11:13], refs[13:]
+    buffers, small_out, all_rows, patch_outs, rest = rest[:3], rest[3], rest[4], rest[5:15], rest[15:]
+    sends, receives, local, value, arriving, small_sends, small_receives, row_sems, patch, w, loads = rest
     place = Place()
     enter(place, MASKS)
     value[0] = small[...]
@@ -549,14 +615,51 @@
     )
     cross.start()
     gathers = []
-    for k, (source, buffer, first, rows, start, column, width, z_first) in enumerate(plan):
+    for k, (source, buffer, first, rows_here, start, column, width, z_first) in enumerate(plan):
         gathers.append(
-            Gather(place, sources[source], buffers[buffer], pl.ds(first, rows), start, column, width, z_first,
+            Gather(place, sources[source], buffers[buffer], pl.ds(first, rows_here), start, column, width, z_first,
                    sends.at[k], receives.at[k], local.at[k])
         )
-    run_gathers(gathers, ahead, total.advance)
-    stay.wait()
-    cross.wait()
+    forward = PatchForward(small_out, all_rows, patch, w, segments, patch_outs)
+    waiting = []
+    patches = sum(p[1] == 0 for p in plan)
+    held = sum(p[1] < 2 for p in plan)
+
+    def fetched():
+        while waiting:
+            waiting.pop().wait()
+
+    def rows_there():
+        stay.wait()
+        cross.wait()
+
+    base = patches + 4
+    pieces = {
+        base: (rows_there, fetched, functools.partial(forward.embed, 0)),
+        base + 1: (functools.partial(forward.embed, 2),),
+        base + 2: (fetched, forward.project),
+        base + 3: (functools.partial(forward.attend, 0),),
+        base + 4: (functools.partial(forward.attend, 3),),
+        base + 5: (fetched, forward.join),
+        base + 6: (functools.partial(forward.lift, 0),),
+        base + 7: (functools.partial(forward.lift, 1),),
+        base + 8: (fetched, functools.partial(forward.lower, 0)),
+        base + 9: (functools.partial(forward.lower, 1),),
+    }
+
+    def tick(t):
+        total.advance()
+        for piece in pieces.get(t, ()):
+            piece()
+        k = t - 3
+        if 0 <= k < held:
+            _, buffer, first, count, _, column, width, _ = plan[k]
+            part = (slice(None), slice(None), pl.ds(first, count), pl.ds(column, width))
+            copy = pltpu.make_async_copy(buffers[buffer].at[part], (patch, w)[buffer].at[part], loads.at[k])
+            copy.start()
+            waiting.append(copy)
+
+    run_gathers(gathers, ahead, tick)
 
 
 def forward_plan(step=1536, patch_rows=96):
@@ -575,20 +678,20 @@
 PLAN = forward_plan()
 
 
-def gather_all(sources, small, rows, ahead=3, plan=PLAN):
+def gather_all(sources, small, rows, segments, ahead=3, plan=PLAN):
     n = len(plan)
-    bf = jnp.bfloat16
+    bf, f32 = jnp.bfloat16, jnp.float32
+    count = 2 * rows.shape[0]
+    outs = [((8, D), f32), ((2,) + rows.shape, bf), ((count, D), f32), ((count, D), bf), ((count, 3 * D), bf),
+            ((D // HEAD_DIM, count, count), f32), ((count, D), bf), ((count, D), f32), ((count, D), bf), ((count, 4 * D), f32),
+            ((count, 4 * D), bf), ((count, D), f32)]
+    shapes = ((4, 4, 384, D), (4, 4, 48, 12 * D))
     return pl.pallas_call(
         functools.partial(gather_kernel, plan, ahead),
-        out_shape=(
-            jax.ShapeDtypeStruct((4, 4, 384, 768), bf),
-            jax.ShapeDtypeStruct((4, 4, 48, 9216), bf),
-            jax.ShapeDtypeStruct((4, 4, 48, 9216), bf),
-            jax.ShapeDtypeStruct((8, 768), jnp.float32),
-            jax.ShapeDtypeStruct((2,) + rows.shape, bf),
-        ),
-        in_specs=[pl.BlockSpec(memory_space=VMEM)] * 10 + [pl.BlockSpec(memory_space=HBM)],
-        out_specs=[pl.BlockSpec(memory_space=HBM)] * 3 + [pl.BlockSpec(memory_space=VMEM), pl.BlockSpec(memory_space=HBM)],
+        out_shape=[jax.ShapeDtypeStruct(shape, bf) for shape in shapes + shapes[1:]]
+        + [jax.ShapeDtypeStruct(*out) for out in outs],
+        in_specs=[pl.BlockSpec(memory_space=VMEM)] * 10 + [pl.BlockSpec(memory_space=HBM)] + [pl.BlockSpec(memory_space=VMEM)] * 2,
+        out_specs=[pl.BlockSpec(memory_space=HBM)] * 3 + [pl.BlockSpec(memory_space=VMEM)] * len(outs),
         scratch_shapes=[
             pltpu.SemaphoreType.DMA((n, 13)),
             pltpu.SemaphoreType.DMA((n, 13)),
@@ -598,10 +701,13 @@
             pltpu.SemaphoreType.DMA((4,)),
             pltpu.SemaphoreType.DMA((4,)),
             pltpu.SemaphoreType.DMA((3,)),
+            pltpu.VMEM(shapes[0], bf),
+            pltpu.VMEM(shapes[1], bf),
+            pltpu.SemaphoreType.DMA((n,)),
         ],
-        compiler_params=pltpu.CompilerParams(collective_id=0, has_side_effects=True),
+        compiler_params=pltpu.CompilerParams(collective_id=0, has_side_effects=True, vmem_limit_bytes=64_000_000),
         name="gather_all",
-    )(*sources, small, rows)
+    )(*sources, small, rows, *segments)
 
 
 class Total:
@@ -644,8 +750,10 @@
         self.from_near, self.from_line, self.out, self.rows = near, line, out, rows
         self.z_last, self.sends, self.receives = z_last, sends, receives
         self.half = width // 2
-        self.mine = pl.ds(pl.multiple_of(column + place.core * self.half, 128), self.half)
-        self.theirs = pl.ds(pl.multiple_of(column + (1 - place.core) * self.half, 128), self.half)
+        whole = out.shape[1] // 2
+        self.own = pl.ds(column // 2, self.half)
+        self.mine = pl.ds(pl.multiple_of(column // 2 + place.core * whole, 128), self.half)
+        self.theirs = pl.ds(pl.multiple_of(column // 2 + (1 - place.core) * whole, 128), self.half)
         self.started = []
 
     def send(self, event, source, target, device):
@@ -777,7 +885,7 @@
         r = reduces[k]
         if k - SLOTS >= 0:
             reduces[k - SLOTS].drain()
-        copy = pltpu.make_async_copy(grads[array].at[:, :, r.rows, r.mine], r.held, loads.at[k])
+        copy = pltpu.make_async_copy(grads[array].at[:, :, r.rows, r.mine if array > 4 else r.own], r.held, loads.at[k])
         copy.start()
         copies.append(copy)
         if array > 4:
@@ -826,7 +934,9 @@
     grads = [g.reshape(4, 4, g.shape[0] // 16, g.shape[1]) for g in grads]
     return pl.pallas_call(
         kernel,
-        out_shape=[jax.ShapeDtypeStruct(g.shape[2:], jnp.float32) for g in grads] + [jax.ShapeDtypeStruct((8, 768), jnp.float32)],
+        out_shape=[
+            jax.ShapeDtypeStruct((g.shape[2], g.shape[3] if i > 4 else 2 * g.shape[3]), jnp.float32) for i, g in enumerate(grads)
+        ] + [jax.ShapeDtypeStruct((8, 768), jnp.float32)],
         in_specs=[pl.BlockSpec(memory_space=HBM)] * ARRAYS + [pl.BlockSpec(memory_space=VMEM)],
         out_specs=[pl.BlockSpec(memory_space=VMEM)] * (ARRAYS + 1),
         scratch_shapes=scratch,
@@ -846,7 +956,11 @@
     byte_rows = byte_inputs[0]
     bytes_here = byte_rows.shape[0]
     patches = bytes_here // PATCH
-    patch_full, coarse_full, fine_full, small, all_rows = gather_all(sources, small, byte_rows)
+    segment_row = segment_ids[0]
+    all_patches = segment_row.shape[0]
+    patch_full, coarse_full, fine_full, small, all_rows, *stored, coarse_out = gather_all(
+        sources, small, byte_rows.reshape(patches, PATCH * D), (segment_row[None], segment_row[:, None])
+    )
     patch_full = patch_full.reshape(-1, D)
 
     def unpack(full, first):
@@ -854,37 +968,22 @@
         return (small[first], small[first + 1], full[:, : 3 * D], full[:, 3 * D : 4 * D], small[first + 2], small[first + 3],
                 full[:, 4 * D : 8 * D], full[:, 8 * D :])
 
+    def mine(values):
+        width = values.shape[1] // 2
+        return lax.dynamic_slice_in_dim(values, core * width, width, 1)
+
+    def coarse_back(grad_mixture, stored):
+        triple, chances = stored
+        parts = triple.reshape(1, all_patches, 3, D // HEAD_DIM, HEAD_DIM)
+        grads = attend_backward_known(
+            parts[:, :, 0], parts[:, :, 1], parts[:, :, 2], chances[None],
+            grad_mixture.reshape(1, all_patches, D // HEAD_DIM, HEAD_DIM),
+        )
+        return jnp.stack(grads, 2).astype(jnp.bfloat16).reshape(all_patches, 3 * D)
+
     coarse_w = unpack(coarse_full, 0)
-    segment_row = segment_ids[0]
-    all_patches = segment_row.shape[0]
-    places = jnp.arange(all_patches)
-    coarse_allowed = (
-        (places[:, None] >= places[None, :]) & (segment_row[:, None] == segment_row[None, :])
-    )[None]
-
-    def attend(shape, allowed):
-        rows = shape[0] * shape[1]
-
-        def forward(triple):
-            grouped = triple.reshape(shape + (3, D // HEAD_DIM, HEAD_DIM))
-            parts = grouped[:, :, 0], grouped[:, :, 1], grouped[:, :, 2]
-            mixture, log_total = attend_forward(*parts, allowed)
-            return (mixture.reshape(rows, D).astype(jnp.bfloat16), parts + (log_total,))
-
-        def backward(grad_mixture, stored):
-            queries, key_part, value_part, log_total = stored
-            grads = attend_backward(
-                queries, key_part, value_part, allowed, log_total,
-                grad_mixture.reshape(shape + (D // HEAD_DIM, HEAD_DIM)),
-            )
-            return jnp.stack(grads, 2).astype(jnp.bfloat16).reshape(rows, 3 * D)
-
-        return forward, backward
-
-    coarse_attend, coarse_back = attend((1, all_patches), coarse_allowed)
+    coarse_stored = tuple(stored[:2]) + (tuple(stored[2:4]),) + tuple(stored[4:])
     grouped_bytes = all_rows.reshape(all_patches, PATCH * D)
-    embedded = product(grouped_bytes, patch_full)
-    coarse_out, coarse_stored = block_forward_t(embedded, coarse_w, coarse_attend)
     coarse_low = coarse_out.astype(jnp.bfloat16)
     joined = jnp.concatenate([jnp.zeros((1,), bool), segment_row[1:] == segment_row[:-1]]).astype(jnp.float32)[:, None]
     previous = jnp.concatenate([jnp.zeros((1, D), jnp.bfloat16), coarse_low[:-1]]).astype(jnp.float32) * joined
@@ -897,9 +996,9 @@
     ]
     grad_previous = lax.all_gather(grad_previous, "seq", axis=0, tiled=True) * joined
     grad_coarse_out = jnp.concatenate([grad_previous[1:], jnp.zeros((1, D), jnp.float32)])
-    grad_embedded, coarse_grads = block_backward_t(grad_coarse_out, coarse_w, coarse_stored, coarse_back)
+    grad_embedded, coarse_grads = block_backward_t(grad_coarse_out, coarse_w, coarse_stored, coarse_back, mine)
     grad_embed_low = grad_embedded.astype(jnp.bfloat16)
-    grad_patch = left_product(grouped_bytes, grad_embed_low).astype(jnp.bfloat16)
+    grad_patch = left_product(grouped_bytes, mine(grad_embed_low)).astype(jnp.bfloat16)
     grad_here = lax.dynamic_slice_in_dim(grad_embed_low, core * patches, patches)
     grad_grouped = right_product(grad_here, patch_full)
     input_gradient = (grad_fine_in + grad_grouped.reshape(bytes_here, D)).astype(jnp.bfloat16)
@@ -916,37 +1015,45 @@
     return (layer_rows[None], input_gradient[None], shards[0]) + gradients(shards[1:5], 0) + gradients(shards[5:], 4)
 
 
-def block_forward_t(inputs, weights, attend):
-    first_gain, first_bias, project, output_t, second_gain, second_bias, expand, narrow_t = weights
-    normed = layer_norm(inputs, first_gain, first_bias).astype(jnp.bfloat16)
-    triple = product(normed, project).astype(jnp.bfloat16)
-    mixture, attend_stored = attend(triple)
-    middle = inputs + right_product(mixture, output_t)
-    second = layer_norm(middle, second_gain, second_bias).astype(jnp.bfloat16)
-    lifted = product(second, expand)
-    hidden = smooth_gate(lifted).astype(jnp.bfloat16)
-    result = middle + right_product(hidden, narrow_t)
-    stored = (inputs, normed, attend_stored, mixture, middle, second, lifted, hidden)
-    return (result, stored)
-
-
-def block_backward_t(grad_result, weights, stored, attend_back):
+def attend_backward_known(queries, key_part, value_part, chances, grad_mixture):
+    factor = 1.0 / math.sqrt(HEAD_DIM)
+    grad_values = jnp.einsum(
+        "bhqk,bqhd->bkhd", chances.astype(jnp.bfloat16), grad_mixture, preferred_element_type=jnp.float32
+    )
+    grad_chances = jnp.einsum(
+        "bqhd,bkhd->bhqk", grad_mixture, value_part, preferred_element_type=jnp.float32
+    )
+    grad_scores = (
+        chances * (grad_chances - jnp.sum(grad_chances * chances, -1, keepdims=True))
+    ).astype(jnp.bfloat16)
+    grad_queries = (
+        jnp.einsum("bhqk,bkhd->bqhd", grad_scores, key_part, preferred_element_type=jnp.float32)
+        * factor
+    )
+    grad_keys = (
+        jnp.einsum("bhqk,bqhd->bkhd", grad_scores, queries, preferred_element_type=jnp.float32)
+        * factor
+    )
+    return (grad_queries, grad_keys, grad_values)
+
+
+def block_backward_t(grad_result, weights, stored, attend_back, mine):
     first_gain, first_bias, project, output_t, second_gain, second_bias, expand, narrow_t = weights
     inputs, normed, attend_stored, mixture, middle, second, lifted, hidden = stored
     grad_branch = grad_result.astype(jnp.bfloat16)
-    grad_narrow_t = left_product(grad_branch, hidden)
+    grad_narrow_t = left_product(grad_branch, mine(hidden))
     grad_hidden = product(grad_branch, narrow_t)
     grad_lifted = jax.vjp(smooth_gate, lifted)[1](grad_hidden)[0].astype(jnp.bfloat16)
-    grad_expand = left_product(second, grad_lifted)
+    grad_expand = left_product(second, mine(grad_lifted))
     grad_second = right_product(grad_lifted, expand)
     pullback = jax.vjp(layer_norm, middle, second_gain, second_bias)[1]
     grad_middle, grad_gain_two, grad_bias_two = pullback(grad_second)
     grad_middle = grad_middle + grad_result
     grad_attended = grad_middle.astype(jnp.bfloat16)
-    grad_output_t = left_product(grad_attended, mixture)
+    grad_output_t = left_product(grad_attended, mine(mixture))
     grad_mixture = product(grad_attended, output_t).astype(jnp.bfloat16)
     grad_triple = attend_back(grad_mixture, attend_stored)
-    grad_project = left_product(normed, grad_triple)
+    grad_project = left_product(normed, mine(grad_triple))
     grad_normed = right_product(grad_triple, project)
     pullback = jax.vjp(layer_norm, inputs, first_gain, first_bias)[1]
     grad_inputs, grad_gain_one, grad_bias_one = pullback(grad_normed)

time: 577 us -> 562 us (0.974)
  matrix products: 92.2 us -> 76.4 us
  Pallas kernels: 434 us -> 440 us
    dot_general x5 -> x2, matrix products: 22 us -> 10.5 us  [product(): return jnp.dot(left_side, right_side, preferred_element_type=jnp.float32)]
    dot_general x5 -> x3, matrix products: 20.7 us -> 17.3 us  [right_product(): lax.dot_general(left_side, right_side, (((1,), (1,)), ((), ())), preferre...]
where the time goes in v4:
time: 562 us; the launch traced here: 553 us
  Pallas kernels  440 us (78%)
  matrix products  76.4 us (14%)
  local copies, waits for them, and re-layouts  25.3 us (5%)
  other arithmetic  7.55 us (1%)
    pallas_call x1, Pallas kernels, reduce_all(): pl.pallas_call(kernel, out_shape=[jax.ShapeDtypeStruct((g.shape[2], g.sha...  177 us
    pallas_call x1, Pallas kernels, gather_all(): pl.pallas_call(functools.partial(gather_kernel, plan, ahead), out_shape=[...  175 us
    pallas_call x1, Pallas kernels, fine_block(): pl.pallas_call(fine_kernel, grid=(steps,), out_shape=[jax.ShapeDtypeStruc...  87.9 us
    dot_general x9, matrix products, left_product(): lax.dot_general(left_side, right_side, (((0,), (0,)), ((), ())), preferre...  45.5 us
    dot_general x3, matrix products, right_product(): lax.dot_general(left_side, right_side, (((1,), (1,)), ((), ())), preferre...  17.3 us

profile of v4, /device:TPU:0, one launch (start us, length us, event | category | flops | bytes accessed | tf_op | source)
XLA Modules:
  0.0 553.2 jit_solution(17625684871444947342)
XLA Ops:
  1.8 3.6 reshape_squeeze.3.refs_10_
  6.1 174.5 %gather_all.1 = (bf16[4,4,384,768]{3,2,1,0:T(8,128)(2,1)}, bf16[4,4,48,9216]{3,2,1,0:T(8,128)(2,1)}, bf16[4,4,48,9216]{3,2,1,0:T(8,128)(2,1)}, f32[8,768]{1,0:T(...) custom-call(bf16[384,768]{1,0:T(8,128)(2,1)} %refs_0_.1, ...), custom_call_target="tpu_custom_call" | custom-call | tf_op jit(solution)/shard_map/gather_all/pallas_call | solution.py:689
  180.7 1.2 slice.130
  183.0 87.9 %fine_block.1 = (bf16[1024,768]{1,0:T(8,128)(2,1)}, f32[1024,768]{1,0:T(8,128)}, f32[128,768]{1,0:T(8,128)}, f32[8,768]{1,0:T(8,128)}, bf16[1024,768]{1,0:T(8,12...) custom-call(bf16[1024,768]{1,0:T(8,128)(2,1)} %bitcast.110, ...), custom_call_target="tpu_custom_call" | custom-call | tf_op jit(solution)/shard_map/fine_block/pallas_call | solution.py:1226
  270.8 2.8 all_gather.3
  273.9 7.9 %fusion.12 = bf16[256,3072]{1,0:T(8,128)(2,1)} fusion(f32[256,3072]{1,0:T(8,128)} %get-tuple-element.64, bf16[768,9216]{1,0:T(8,128)(2,1)} %bitcast.131, f32[255,768]{1,0:T(8,128)S(1)} %slice_multiply_fusion), kind=kOutput, calls=%fused_computation.21 | convolution fusion | flops 1223688192 | bytes 10220544 | tf_op jit(solution)/shard_map/dot_general | solution.py:38
  283.2 5.0 multiply_reduce_fusion.1
  289.7 2.6 convolution_convert_fusion.9
  293.5 2.4 copy.47
  295.9 1.7 multiply_reduce_fusion
  301.0 3.9 multiply_reduce_fusion.2
  305.7 9.4 %convolution_convert_fusion.2 = bf16[768,3072]{1,0:T(8,128)(2,1)} fusion(bf16[1024,768]{1,0:T(8,128)(2,1)} %get-tuple-element.77, bf16[1024,3072]{1,0:T(8,128)(2,1)} %get-tuple-element.78), kind=kOutput, calls=%fused_computation.2 | convolution fusion | flops 4834197504 | bytes 12582912 | tf_op jit(solution)/shard_map/dot_general | solution.py:42
  315.2 2.5 convolution_convert_fusion.7
  317.6 7.8 %convolution_convert_fusion.3 = bf16[768,2304]{1,0:T(8,128)(2,1)} fusion(bf16[1024,768]{1,0:T(8,128)(2,1)S(1)} %copy-done.28, bf16[1024,2304]{1,0:T(8,128)(2,1)} %get-tuple-element.74), kind=kOutput, calls=%fused_computation.3 | convolution fusion | flops 3625648128 | bytes 9830400 | tf_op jit(solution)/shard_map/dot_general | solution.py:42
  325.4 2.2 convolution_convert_fusion.8
  327.6 3.1 convolution_convert_fusion.6
  331.9 4.0 convolution_convert_fusion
  335.9 3.4 convolution_convert_fusion.5
  339.3 3.4 convolution_convert_fusion.4
  342.7 9.7 %convolution_convert_fusion.1 = bf16[3072,768]{0,1:T(8,128)(2,1)} fusion(bf16[1024,3072]{1,0:T(8,128)(2,1)} %get-tuple-element.79, bf16[1,1024,768]{2,1,0:T(8,128)(2,1)S(1)} %copy-done.11), kind=kOutput, calls=%fused_computation.1 | convolution fusion | flops 4834197504 | bytes 12582912 | tf_op jit(solution)/shard_map/dot_general | solution.py:42
  352.4 177.2 %reduce_all.1 = (f32[384,768]{1,0:T(8,128)}, f32[48,2304]{1,0:T(8,128)}, f32[48,768]{1,0:T(8,128)}, f32[48,3072]{1,0:T(8,128)}, f32[48,3072]{1,0:T(8,128)}, /*in...) custom-call(bf16[4,4,384,384]{3,2,1,0:T(8,128)(2,1)} %bitcast.105, ...), custom_call_target="tpu_custom_call" | custom-call | tf_op jit(solution)/shard_map/reduce_all/pallas_call | solution.py:935
  530.9 8.4 %fusion.35 = f32[128,6144]{1,0:T(8,128)} fusion(bf16[6144,768]{1,0:T(8,128)(2,1)} %bitcast.104, bf16[256,768]{1,0:T(8,128)(2,1)S(1)} %add_convert_fusion.1, s32[]{:T(128)S(6)} %select_n.20), kind=kOutput, calls=%fused_computation.65 | convolution fusion | flops 1207959552 | bytes 12779524 | tf_op jit(solution)/shard_map/dot_general | solution.py:48
  539.3 2.8 reshape.263
  542.1 3.4 fusion.15
  (116 shorter events, 20.9 us)
Async XLA Ops:
  0.7 4.7 copy-start.23
  1.7 4.4 copy-start.22
  5.3 176.5 %copy-start.24 = (s32[1,256]{1,0:T(1,128)S(1)}, s32[1,256]{1,0:T(1,128)}, u32[]{:S(2)}) copy-start(s32[1,256]{1,0:T(1,128)} %refs_11_.1) | copy-start | bytes 3076
  273.9 14.7 %copy-start.7 = (f32[255,768]{1,0:T(8,128)}, f32[255,768]{1,0:T(8,128)S(1)}, u32[]{:S(2)}) copy-start(f32[255,768]{1,0:T(8,128)S(1)} %slice_multiply_fusion) | copy-start | bytes 2350084
  273.9 7.9 %copy-start.3 = (f32[256,768]{1,0:T(8,128)S(1)}, f32[256,768]{1,0:T(8,128)}, u32[]{:S(2)}) copy-start(f32[256,768]{1,0:T(8,128)} %get-tuple-element.66) | copy-start | bytes 2359300
  273.9 8.0 %copy-start.6 = (f32[256,768]{1,0:T(8,128)S(1)}, f32[256,768]{1,0:T(8,128)}, u32[]{:S(2)}) copy-start(f32[256,768]{1,0:T(8,128)} %get-tuple-element.65) | copy-start | bytes 2359300
  289.7 6.2 %copy-start = (f32[12,256,256]{2,1,0:T(8,128)S(1)}, f32[12,256,256]{2,1,0:T(8,128)}, u32[]{:S(2)}) copy-start(f32[12,256,256]{2,1,0:T(8,128)} %get-tuple-element.61) | copy-start | bytes 9437188
  301.0 3.9 copy-start.27
  301.0 4.0 copy-start.26
  301.0 4.0 copy-start.25
  305.7 9.5 %copy-start.29 = (bf16[1024,768]{1,0:T(8,128)(2,1)S(1)}, bf16[1024,768]{1,0:T(8,128)(2,1)}, u32[]{:S(2)}) copy-start(bf16[1024,768]{1,0:T(8,128)(2,1)} %get-tuple-element.76) | copy-start | bytes 4718596
  305.7 9.5 %copy-start.30 = (bf16[1024,768]{1,0:T(8,128)(2,1)S(1)}, bf16[1024,768]{1,0:T(8,128)(2,1)}, u32[]{:S(2)}) copy-start(bf16[1024,768]{1,0:T(8,128)(2,1)} %get-tuple-element.75) | copy-start | bytes 4718596
  317.6 7.8 %copy-start.2 = (f32[256,768]{1,0:T(8,128)S(1)}, f32[256,768]{1,0:T(8,128)}, u32[]{:S(2)}) copy-start(f32[256,768]{1,0:T(8,128)} %copy-done.1) | copy-start | bytes 2359300
  325.4 6.0 %copy-start.5 = (f32[256,768]{1,0:T(8,128)S(1)}, f32[256,768]{1,0:T(8,128)}, u32[]{:S(2)}) copy-start(f32[256,768]{1,0:T(8,128)} %get-tuple-element.66) | copy-start | bytes 2359300
  327.6 4.3 copy-start.9
  331.9 4.0 copy-start.13
  335.9 3.4 copy-start.8
  339.3 3.4 copy-start.11
  542.1 3.5 copy-start.12
  542.1 4.5 copy-start.19
  545.6 4.1 copy-start.18
  545.6 4.9 copy-start.20
  545.6 5.5 copy-start.15
  546.7 5.3 copy-start.14
  (7 other events, 13.4 us)

commit v5 on v4

--- a/solution.py
+++ b/solution.py
@@ -772,6 +772,7 @@
 
     def pair(self, theirs):
         self.send(0, theirs, self.from_partner, self.p.partner())
+        self.paired = self.started.pop()
 
     def fold(self, plane, others):
         def step(z, _):
@@ -845,7 +846,7 @@
 
 def backward_plan(step=1536, patch_rows=96):
     plan = []
-    for array, width in ((8, 3072), (7, 3072), (6, 768), (5, 2304), (4, 3072), (3, 3072), (2, 768), (1, 2304)):
+    for array, width in ((6, 768), (8, 3072), (7, 3072), (5, 2304), (4, 3072), (3, 3072), (2, 768), (1, 2304)):
         for start in range(0, width, step):
             plan.append((array, 0, 48, start, min(step, width - start)))
     for first in range(0, 384, patch_rows):
@@ -859,44 +860,100 @@
 ARRAYS = 9
 
 
-def reduce_kernel(plan, grads, small, outs, small_out, slots, pairs, fars, nears, lines, sends, receives, loads,
-                  value, arriving, small_sends, small_receives):
+def reduce_kernel(plan, patch, lefts, rights, small, outs, small_out, slots, pairs, fars, nears, lines, staging, left_held,
+                  right_held, sends, receives, loads, left_sems, right_sems, value, arriving, small_sends, small_receives):
     place = Place()
     enter(place, MASKS)
     n = len(plan)
     value[0] = small[...]
     total = Total(place, (0, 1, 2, 4, 8), value, arriving, small_sends, small_receives, small_out)
     used = [0, 0]
-    reduces, copies = [], []
+    reduces, copies, staged, steps, order = [], {}, [], [], []
     for k, (array, first, rows, column, width, z_last) in enumerate(plan):
         kind = 0 if array == 0 else 1
         slot = used[kind] % SLOTS
         used[kind] += 1
         half = width // 2
         cut = (lambda ref, half=half: ref if half == ref.shape[-1] else ref.at[..., pl.ds(0, half)])
-        reduces.append(
-            Reduce(place, cut(slots[kind].at[slot]), cut(pairs.at[used[kind] - 1]) if array > 4 else None, cut(fars[kind].at[used[kind] - 1]),
+        r = Reduce(place, cut(slots[kind].at[slot]), cut(pairs.at[used[kind] - 1]) if array > 4 else None, cut(fars[kind].at[used[kind] - 1]),
                    cut(nears[kind].at[used[kind] - 1]), cut(lines[kind].at[used[kind] - 1]), outs[array],
                    pl.ds(first, rows), column, width, z_last, sends.at[k], receives.at[k])
-        )
+        r.staging = cut(staging.at[(used[kind] - 1) % 2])
+        r.paired = None
+        reduces.append(r)
+        if array > 4:
+            steps.append((k, r.theirs))
+        if array:
+            steps.append((k, r.mine))
+            if array not in order:
+                order.append(array)
+
+    def left_view(index):
+        return left_held.at[index % 2, pl.ds(0, lefts[order[index] - 1].shape[0])]
+
+    def left_copy(index):
+        return pltpu.make_async_copy(lefts[order[index] - 1], left_view(index), left_sems.at[index % 2])
+
+    def right_view(index):
+        k = steps[index][0]
+        return right_held.at[index % 3, pl.ds(0, rights[plan[k][0] - 1].shape[0]), pl.ds(0, reduces[k].half)]
+
+    def right_copy(index):
+        k, columns = steps[index]
+        return pltpu.make_async_copy(rights[plan[k][0] - 1].at[:, columns], right_view(index), right_sems.at[index % 3])
+
+    done, begun = [0], [0]
+
+    def make(target, k):
+        index = done[0]
+        if plan[k][0] != order[begun[0] - 1] or begun[0] == 0:
+            left_copy(begun[0]).wait()
+            begun[0] += 1
+            if begun[0] < len(order):
+                left_copy(begun[0]).start()
+        left, right = left_view(begun[0] - 1), right_view(index)
+        right_copy(index).wait()
+        rows = D // 2
+
+        def part(i, _):
+            columns = pl.ds(pl.multiple_of(i * rows, 128), rows)
+            term = left_product(left[:, columns], right[...]).astype(jnp.bfloat16)
+            target[pl.ds(i * 2, 2)] = term.reshape((2,) + target.shape[1:])
+            return 0
+
+        lax.fori_loop(0, 2, part, 0)
+        done[0] += 1
+        if index + 3 < len(steps):
+            right_copy(index + 3).start()
+
+    left_copy(0).start()
+    for index in range(3):
+        right_copy(index).start()
 
     def load(k):
         array = plan[k][0]
         r = reduces[k]
         if k - SLOTS >= 0:
             reduces[k - SLOTS].drain()
-        copy = pltpu.make_async_copy(grads[array].at[:, :, r.rows, r.mine if array > 4 else r.own], r.held, loads.at[k])
-        copy.start()
-        copies.append(copy)
+        if array == 0:
+            copies[k] = pltpu.make_async_copy(patch.at[:, :, r.rows, r.own], r.held, loads.at[k])
+            copies[k].start()
+            return
         if array > 4:
-            r.pair(grads[array].at[:, :, r.rows, r.theirs])
+            if len(staged) > 1:
+                staged[-2].paired.wait_send()
+            make(r.staging, k)
+            r.pair(r.staging)
+            staged.append(r)
+        make(r.held, k)
 
     load(0)
     for t in range(n + LAGS[-1]):
         if t + 1 < n:
             load(t + 1)
         if t < n:
-            copies[t].wait()
+            if t in copies:
+                copies[t].wait()
             reduces[t].one()
         for lag, name in zip(LAGS, ("two", "three", "four", "five")):
             if 0 <= t - lag < n:
@@ -904,45 +961,55 @@
         total.advance()
     for r in reduces:
         r.drain()
-
-
-def reduce_all(grads, small, plan=BACK_PLAN):
+    for r in staged[-2:]:
+        r.paired.wait_send()
+
+
+def reduce_all(patch, terms, small, plan=BACK_PLAN):
     n = len(plan)
     bf = jnp.bfloat16
     counts = [sum(p[0] == 0 for p in plan), sum(p[0] > 0 for p in plan), sum(p[0] > 4 for p in plan)]
     shapes = tuple((max(p[2] for p in plan if c(p[0])), max(p[4] for p in plan if c(p[0])) // 2) for c in (lambda a: a == 0, lambda a: a > 0))
 
+    inputs = 2 * ARRAYS
+
     def kernel(*refs):
-        grads, small, outs, small_out = refs[:ARRAYS], refs[ARRAYS], refs[ARRAYS + 1 : 2 * ARRAYS + 1], refs[2 * ARRAYS + 1]
-        pairs, rest = refs[2 * ARRAYS + 2], refs[2 * ARRAYS + 3 :]
+        patch, lefts, rights, small = refs[0], refs[1:ARRAYS], refs[ARRAYS : inputs - 1], refs[inputs - 1]
+        outs, small_out = refs[inputs : inputs + ARRAYS], refs[inputs + ARRAYS]
+        pairs, rest = refs[inputs + ARRAYS + 1], refs[inputs + ARRAYS + 2 :]
         slots, fars, nears, lines = (rest[2 * i : 2 * i + 2] for i in range(4))
-        reduce_kernel(plan, grads, small, outs, small_out, slots, pairs, fars, nears, lines, *rest[8:])
+        reduce_kernel(plan, patch, lefts, rights, small, outs, small_out, slots, pairs, fars, nears, lines, *rest[8:])
 
     scratch = [pltpu.VMEM((counts[2], 4, 4) + shapes[1], bf)]
     scratch += [pltpu.VMEM((min(SLOTS, counts[i]), 4, 4) + shapes[i], bf) for i in (0, 1)]
     for lead in ((2, 4), (4,), (6,)):
         scratch += [pltpu.VMEM((counts[i],) + lead + shapes[i], bf) for i in (0, 1)]
+    depth = max(left.shape[0] for left, _ in terms)
     scratch += [
+        pltpu.VMEM((2, 4, 4) + shapes[1], bf),
+        pltpu.VMEM((2, depth, D), bf),
+        pltpu.VMEM((3, depth, shapes[1][1]), bf),
         pltpu.SemaphoreType.DMA((n, 11)),
         pltpu.SemaphoreType.DMA((n, 11)),
         pltpu.SemaphoreType.DMA((n,)),
+        pltpu.SemaphoreType.DMA((2,)),
+        pltpu.SemaphoreType.DMA((3,)),
         pltpu.VMEM((6, 8, 768), jnp.float32),
         pltpu.VMEM((5, 8, 768), jnp.float32),
         pltpu.SemaphoreType.DMA((5,)),
         pltpu.SemaphoreType.DMA((5,)),
     ]
-    grads = [g.reshape(4, 4, g.shape[0] // 16, g.shape[1]) for g in grads]
+    patch = patch.reshape(4, 4, patch.shape[0] // 16, patch.shape[1])
+    outs = [(patch.shape[2], 2 * patch.shape[3])] + [(left.shape[1] // 16, right.shape[1]) for left, right in terms] + [(8, 768)]
     return pl.pallas_call(
         kernel,
-        out_shape=[
-            jax.ShapeDtypeStruct((g.shape[2], g.shape[3] if i > 4 else 2 * g.shape[3]), jnp.float32) for i, g in enumerate(grads)
-        ] + [jax.ShapeDtypeStruct((8, 768), jnp.float32)],
-        in_specs=[pl.BlockSpec(memory_space=HBM)] * ARRAYS + [pl.BlockSpec(memory_space=VMEM)],
+        out_shape=[jax.ShapeDtypeStruct(out, jnp.float32) for out in outs],
+        in_specs=[pl.BlockSpec(memory_space=HBM)] * (inputs - 1) + [pl.BlockSpec(memory_space=VMEM)],
         out_specs=[pl.BlockSpec(memory_space=VMEM)] * (ARRAYS + 1),
         scratch_shapes=scratch,
-        compiler_params=pltpu.CompilerParams(collective_id=1, has_side_effects=True, vmem_limit_bytes=66_000_000),
+        compiler_params=pltpu.CompilerParams(collective_id=1, has_side_effects=True, vmem_limit_bytes=67_000_000),
         name="reduce_all",
-    )(*grads, small)
+    )(patch, *[left for left, _ in terms], *[right for _, right in terms], small)
 
 
 def fast_body(byte_inputs, segment_ids, cotangent, patch_weight, *weights):
@@ -990,23 +1057,18 @@
     previous = lax.dynamic_slice_in_dim(previous, core * patches, patches)
     (layer_rows, grad_fine_in, grad_previous, fine_vectors, normed, mixture, second, hidden, grad_middle, grad_lifted,
      grad_triple) = fine_block(byte_rows, previous, cotangent[0], small, fine_full.reshape(D, -1))
-    fine_grads = [
-        left_product(*pair).astype(jnp.bfloat16)
-        for pair in ((normed, grad_triple), (grad_middle, mixture), (second, grad_lifted), (cotangent[0], hidden))
-    ]
+    fine_terms = [(normed, grad_triple), (grad_middle, mixture), (second, grad_lifted), (cotangent[0], hidden)]
     grad_previous = lax.all_gather(grad_previous, "seq", axis=0, tiled=True) * joined
     grad_coarse_out = jnp.concatenate([grad_previous[1:], jnp.zeros((1, D), jnp.float32)])
-    grad_embedded, coarse_grads = block_backward_t(grad_coarse_out, coarse_w, coarse_stored, coarse_back, mine)
+    grad_embedded, coarse_vectors, coarse_terms = block_backward_t(grad_coarse_out, coarse_w, coarse_stored, coarse_back)
     grad_embed_low = grad_embedded.astype(jnp.bfloat16)
     grad_patch = left_product(grouped_bytes, mine(grad_embed_low)).astype(jnp.bfloat16)
     grad_here = lax.dynamic_slice_in_dim(grad_embed_low, core * patches, patches)
     grad_grouped = right_product(grad_here, patch_full)
     input_gradient = (grad_fine_in + grad_grouped.reshape(bytes_here, D)).astype(jnp.bfloat16)
     once = (core == 0).astype(jnp.float32)
-    small = jnp.concatenate([jnp.stack([coarse_grads[i] * once for i in (0, 1, 4, 5)]), fine_vectors[4:]])
-    *shards, small = reduce_all(
-        [grad_patch] + [coarse_grads[i].astype(jnp.bfloat16) for i in (2, 3, 6, 7)] + fine_grads, small
-    )
+    small = jnp.concatenate([jnp.stack(coarse_vectors) * once, fine_vectors[4:]])
+    *shards, small = reduce_all(grad_patch, coarse_terms + fine_terms, small)
     small = lax.dynamic_slice_in_dim(small, at * vectors.shape[1], vectors.shape[1], 1)
 
     def gradients(parts, first):
@@ -1037,30 +1099,27 @@
     return (grad_queries, grad_keys, grad_values)
 
 
-def block_backward_t(grad_result, weights, stored, attend_back, mine):
+def block_backward_t(grad_result, weights, stored, attend_back):
     first_gain, first_bias, project, output_t, second_gain, second_bias, expand, narrow_t = weights
     inputs, normed, attend_stored, mixture, middle, second, lifted, hidden = stored
     grad_branch = grad_result.astype(jnp.bfloat16)
-    grad_narrow_t = left_product(grad_branch, mine(hidden))
     grad_hidden = product(grad_branch, narrow_t)
     grad_lifted = jax.vjp(smooth_gate, lifted)[1](grad_hidden)[0].astype(jnp.bfloat16)
-    grad_expand = left_product(second, mine(grad_lifted))
     grad_second = right_product(grad_lifted, expand)
     pullback = jax.vjp(layer_norm, middle, second_gain, second_bias)[1]
     grad_middle, grad_gain_two, grad_bias_two = pullback(grad_second)
     grad_middle = grad_middle + grad_result
     grad_attended = grad_middle.astype(jnp.bfloat16)
-    grad_output_t = left_product(grad_attended, mine(mixture))
     grad_mixture = product(grad_attended, output_t).astype(jnp.bfloat16)
     grad_triple = attend_back(grad_mixture, attend_stored)
-    grad_project = left_product(normed, mine(grad_triple))
     grad_normed = right_product(grad_triple, project)
     pullback = jax.vjp(layer_norm, inputs, first_gain, first_bias)[1]
     grad_inputs, grad_gain_one, grad_bias_one = pullback(grad_normed)
     grad_inputs = grad_inputs + grad_middle
     return (
         grad_inputs,
-        (grad_gain_one, grad_bias_one, grad_project, grad_output_t, grad_gain_two, grad_bias_two, grad_expand, grad_narrow_t),
+        (grad_gain_one, grad_bias_one, grad_gain_two, grad_bias_two),
+        [(normed, grad_triple), (grad_attended, mixture), (second, grad_lifted), (grad_branch, hidden)],
     )
 
 

time: 562 us -> 544 us (0.968)
  matrix products: 76.4 us -> 36.9 us
  Pallas kernels: 440 us -> 460 us
    dot_general x9 -> x1, matrix products: 45.5 us -> 6 us  [left_product(): lax.dot_general(left_side, right_side, (((0,), (0,)), ((), ())), preferre...]
    pallas_call x1, Pallas kernels: 87.9 us -> 98.5 us  [fine_block(): pl.pallas_call(fine_kernel, grid=(steps,), out_shape=[jax.ShapeDtypeStruc...]
    pallas_call x1, Pallas kernels: 177 us -> 187 us  [reduce_all(): pl.pallas_call(kernel, out_shape=[jax.ShapeDtypeStruct(out, jnp.float32)...]
where the time goes in v5:
time: 544 us; the launch traced here: 540 us
  Pallas kernels  460 us (85%)
  matrix products  36.9 us (7%)
  local copies, waits for them, and re-layouts  28.6 us (5%)
  other arithmetic  10.8 us (2%)
    pallas_call x1, Pallas kernels, reduce_all(): pl.pallas_call(kernel, out_shape=[jax.ShapeDtypeStruct(out, jnp.float32)...  187 us
    pallas_call x1, Pallas kernels, gather_all(): pl.pallas_call(functools.partial(gather_kernel, plan, ahead), out_shape=[...  174 us
    pallas_call x1, Pallas kernels, fine_block(): pl.pallas_call(fine_kernel, grid=(steps,), out_shape=[jax.ShapeDtypeStruc...  98.5 us
    dot_general x3, matrix products, right_product(): lax.dot_general(left_side, right_side, (((1,), (1,)), ((), ())), preferre...  18.4 us

profile of v5, /device:TPU:0, one launch (start us, length us, event | category | flops | bytes accessed | tf_op | source)
XLA Modules:
  0.0 540.3 jit_solution(16284837969635494167)
XLA Ops:
  1.8 3.6 reshape_squeeze.3.refs_10_
  6.1 174.5 %gather_all.1 = (bf16[4,4,384,768]{3,2,1,0:T(8,128)(2,1)}, bf16[4,4,48,9216]{3,2,1,0:T(8,128)(2,1)}, bf16[4,4,48,9216]{3,2,1,0:T(8,128)(2,1)}, f32[8,768]{1,0:T(...) custom-call(bf16[384,768]{1,0:T(8,128)(2,1)} %refs_0_.1, ...), custom_call_target="tpu_custom_call" | custom-call | tf_op jit(solution)/shard_map/gather_all/pallas_call | solution.py:689
  180.6 1.2 slice.130
  182.1 0.8 convert_multiply_fusion.previous_ref
  182.9 98.5 %fine_block.1 = (bf16[1024,768]{1,0:T(8,128)(2,1)}, f32[1024,768]{1,0:T(8,128)}, f32[128,768]{1,0:T(8,128)}, f32[8,768]{1,0:T(8,128)}, bf16[1024,768]{1,0:T(8,12...) custom-call(bf16[1024,768]{1,0:T(8,128)(2,1)} %bitcast.90, ...), custom_call_target="tpu_custom_call" | custom-call | tf_op jit(solution)/shard_map/fine_block/pallas_call | solution.py:1285
  281.5 2.9 all_gather.3
  284.7 6.8 %fusion.12.refs_11_ = bf16[256,3072]{1,0:T(8,128)(2,1)} fusion(f32[256,3072]{1,0:T(8,128)S(1)} %copy-done.31, bf16[256,768]{1,0:T(8,128)(2,1)S(1)} %pad_convert_fusion.refs_4_, bf16[768,9216]{1,0:T(8,128)(2,1)} %bitcast.116), kind=kOutput, calls=%fused_computation.15 | convolution fusion | flops 1223688192 | bytes 9830400 | tf_op jit(solution)/shard_map/dot_general | solution.py:38
  292.1 0.8 slice_reduce_fusion
  293.0 5.0 multiply_reduce_fusion.1
  298.4 0.9 copy-done.7
  300.1 2.6 convolution_convert_fusion.1
  302.8 1.2 copy.49
  304.0 2.8 copy.48
  306.7 1.7 multiply_reduce_fusion
  311.9 4.8 multiply_reduce_fusion.2
  320.1 1.5 fusion.38
  321.6 0.9 add_convert_fusion.1
  322.6 6.0 %convolution_convert_fusion = bf16[6144,384]{1,0:T(8,128)(2,1)} fusion(bf16[256,6144]{1,0:T(8,128)(2,1)} %bitcast.91, bf16[256,768]{1,0:T(8,128)(2,1)S(1)} %add_convert_fusion.1, s32[]{:T(128)S(6)} %select_n.13), kind=kOutput, calls=%fused_computation | convolution fusion | flops 1210318848 | bytes 8060932 | tf_op jit(solution)/shard_map/dot_general | solution.py:42
  328.6 1.5 copy.52.refs_9_
  330.1 186.8 %reduce_all.1 = (f32[384,768]{1,0:T(8,128)}, f32[48,2304]{1,0:T(8,128)}, f32[48,768]{1,0:T(8,128)}, f32[48,3072]{1,0:T(8,128)}, f32[48,3072]{1,0:T(8,128)}, /*in...) custom-call(bf16[4,4,384,384]{3,2,1,0:T(8,128)(2,1)} %bitcast.86, ...), custom_call_target="tpu_custom_call" | custom-call | tf_op jit(solution)/shard_map/reduce_all/pallas_call | solution.py:1004
  518.2 8.5 %fusion.31 = f32[128,6144]{1,0:T(8,128)} fusion(bf16[6144,768]{1,0:T(8,128)(2,1)} %bitcast.85, bf16[256,768]{1,0:T(8,128)(2,1)} %copy-done.12, s32[]{:T(128)S(6)} %select_n.12), kind=kOutput, calls=%fused_computation.53 | convolution fusion | flops 1207959552 | bytes 12779524 | tf_op jit(solution)/shard_map/dot_general | solution.py:48
  526.7 2.8 reshape.219
  529.5 3.4 fusion.15
  533.0 1.0 copy.64
  (109 shorter events, 18.4 us)
Async XLA Ops:
  0.7 4.7 copy-start.23
  1.7 4.4 copy-start.22
  5.3 176.5 %copy-start.24 = (s32[1,256]{1,0:T(1,128)S(1)}, s32[1,256]{1,0:T(1,128)}, u32[]{:S(2)}) copy-start(s32[1,256]{1,0:T(1,128)} %refs_11_.1) | copy-start | bytes 3076
  284.6 13.7 %copy-start.1 = (f32[255,768]{1,0:T(8,128)}, f32[255,768]{1,0:T(8,128)S(1)}, u32[]{:S(2)}) copy-start(f32[255,768]{1,0:T(8,128)S(1)} %slice_multiply_fusion) | copy-start | bytes 2350084
  284.7 6.8 %copy-start.11 = (bf16[256,768]{1,0:T(8,128)(2,1)}, bf16[256,768]{1,0:T(8,128)(2,1)S(1)}, u32[]{:S(2)}) copy-start(bf16[256,768]{1,0:T(8,128)(2,1)S(1)} %pad_convert_fusion.refs_4_) | copy-start | bytes 1179652
  284.7 6.8 %copy-start.3 = (f32[256,768]{1,0:T(8,128)S(1)}, f32[256,768]{1,0:T(8,128)}, u32[]{:S(2)}) copy-start(f32[256,768]{1,0:T(8,128)} %get-tuple-element.66) | copy-start | bytes 2359300
  284.7 6.9 %copy-start.6 = (f32[256,768]{1,0:T(8,128)S(1)}, f32[256,768]{1,0:T(8,128)}, u32[]{:S(2)}) copy-start(f32[256,768]{1,0:T(8,128)} %get-tuple-element.65) | copy-start | bytes 2359300
  291.6 19.7 %copy-start.26 = (f32[256]{0:T(256)}, f32[256]{0:T(256)S(1)}, u32[]{:S(2)}) copy-start(f32[256]{0:T(256)S(1)} %broadcast_multiply_fusion) | copy-start | bytes 3076
  292.1 19.2 %copy-start.27 = (f32[256]{0:T(256)}, f32[256]{0:T(256)S(1)}, u32[]{:S(2)}) copy-start(f32[256]{0:T(256)S(1)} %get-tuple-element.115) | copy-start | bytes 3076
  300.1 6.6 %copy-start = (f32[12,256,256]{2,1,0:T(8,128)S(1)}, f32[12,256,256]{2,1,0:T(8,128)}, u32[]{:S(2)}) copy-start(f32[12,256,256]{2,1,0:T(8,128)} %get-tuple-element.61) | copy-start | bytes 9437188
  311.3 5.4 %copy-start.28 = (f32[256]{0:T(256)}, f32[256]{0:T(256)S(1)}, u32[]{:S(2)}) copy-start(f32[256]{0:T(256)S(1)} %fusion.37) | copy-start | bytes 3076
  311.9 4.9 copy-start.30
  311.9 4.9 copy-start.29
  311.9 8.2 %copy-start.5 = (f32[256,768]{1,0:T(8,128)S(1)}, f32[256,768]{1,0:T(8,128)}, u32[]{:S(2)}) copy-start(f32[256,768]{1,0:T(8,128)} %get-tuple-element.66) | copy-start | bytes 2359300
  311.9 9.7 %copy-start.2 = (f32[255,768]{1,0:T(8,128)S(1)}, f32[255,768]{1,0:T(8,128)}, u32[]{:S(2)}) copy-start(f32[255,768]{1,0:T(8,128)} %copy-done.1) | copy-start | bytes 2350084
  311.9 9.7 %copy-start.8 = (f32[256,768]{1,0:T(8,128)S(1)}, f32[256,768]{1,0:T(8,128)}, u32[]{:S(2)}) copy-start(f32[256,768]{1,0:T(8,128)} %copy-done.7) | copy-start | bytes 2359300
  322.5 6.0 %copy-start.12 = (bf16[256,768]{1,0:T(8,128)(2,1)}, bf16[256,768]{1,0:T(8,128)(2,1)S(1)}, u32[]{:S(2)}) copy-start(bf16[256,768]{1,0:T(8,128)(2,1)S(1)} %add_convert_fusion.1) | copy-start | bytes 1179652
  529.5 3.5 copy-start.13
  529.5 4.5 copy-start.19
  532.9 3.3 copy-start.16
  532.9 4.1 copy-start.18
  533.0 4.9 copy-start.20
  533.0 5.5 %copy-start.15 = (f32[48,3072]{1,0:T(8,128)S(1)}, f32[48,3072]{1,0:T(8,128)}, u32[]{:S(2)}) copy-start(f32[48,3072]{1,0:T(8,128)} %get-tuple-element.153) | copy-start | bytes 1769476
  534.0 5.3 copy-start.14
  (8 other events, 12.6 us)

commit v6 on v5

--- a/solution.py
+++ b/solution.py
@@ -1030,26 +1030,11 @@
     )
     patch_full = patch_full.reshape(-1, D)
 
-    def unpack(full, first):
-        full = full.reshape(D, -1)
-        return (small[first], small[first + 1], full[:, : 3 * D], full[:, 3 * D : 4 * D], small[first + 2], small[first + 3],
-                full[:, 4 * D : 8 * D], full[:, 8 * D :])
-
     def mine(values):
         width = values.shape[1] // 2
         return lax.dynamic_slice_in_dim(values, core * width, width, 1)
 
-    def coarse_back(grad_mixture, stored):
-        triple, chances = stored
-        parts = triple.reshape(1, all_patches, 3, D // HEAD_DIM, HEAD_DIM)
-        grads = attend_backward_known(
-            parts[:, :, 0], parts[:, :, 1], parts[:, :, 2], chances[None],
-            grad_mixture.reshape(1, all_patches, D // HEAD_DIM, HEAD_DIM),
-        )
-        return jnp.stack(grads, 2).astype(jnp.bfloat16).reshape(all_patches, 3 * D)
-
-    coarse_w = unpack(coarse_full, 0)
-    coarse_stored = tuple(stored[:2]) + (tuple(stored[2:4]),) + tuple(stored[4:])
+    embedded, coarse_normed, coarse_triple, chances, coarse_mixture, coarse_middle, coarse_second, lifted, coarse_hidden = stored
     grouped_bytes = all_rows.reshape(all_patches, PATCH * D)
     coarse_low = coarse_out.astype(jnp.bfloat16)
     joined = jnp.concatenate([jnp.zeros((1,), bool), segment_row[1:] == segment_row[:-1]]).astype(jnp.float32)[:, None]
@@ -1060,14 +1045,17 @@
     fine_terms = [(normed, grad_triple), (grad_middle, mixture), (second, grad_lifted), (cotangent[0], hidden)]
     grad_previous = lax.all_gather(grad_previous, "seq", axis=0, tiled=True) * joined
     grad_coarse_out = jnp.concatenate([grad_previous[1:], jnp.zeros((1, D), jnp.float32)])
-    grad_embedded, coarse_vectors, coarse_terms = block_backward_t(grad_coarse_out, coarse_w, coarse_stored, coarse_back)
-    grad_embed_low = grad_embedded.astype(jnp.bfloat16)
+    grad_branch, coarse_grad_lifted, grad_attended, coarse_grad_triple, grad_embed_low, coarse_vectors, input_gradient = coarse_block_back(
+        grad_coarse_out, embedded, coarse_middle, lifted, coarse_triple, chances, small, coarse_full.reshape(D, -1), patch_full,
+        grad_fine_in,
+    )
     grad_patch = left_product(grouped_bytes, mine(grad_embed_low)).astype(jnp.bfloat16)
-    grad_here = lax.dynamic_slice_in_dim(grad_embed_low, core * patches, patches)
-    grad_grouped = right_product(grad_here, patch_full)
-    input_gradient = (grad_fine_in + grad_grouped.reshape(bytes_here, D)).astype(jnp.bfloat16)
+    coarse_terms = [
+        (coarse_normed, coarse_grad_triple), (grad_attended, coarse_mixture), (coarse_second, coarse_grad_lifted),
+        (grad_branch, coarse_hidden),
+    ]
     once = (core == 0).astype(jnp.float32)
-    small = jnp.concatenate([jnp.stack(coarse_vectors) * once, fine_vectors[4:]])
+    small = coarse_vectors * once + fine_vectors
     *shards, small = reduce_all(grad_patch, coarse_terms + fine_terms, small)
     small = lax.dynamic_slice_in_dim(small, at * vectors.shape[1], vectors.shape[1], 1)
 
@@ -1075,52 +1063,6 @@
         return (small[first], small[first + 1], parts[0], parts[1].T, small[first + 2], small[first + 3], parts[2], parts[3].T)
 
     return (layer_rows[None], input_gradient[None], shards[0]) + gradients(shards[1:5], 0) + gradients(shards[5:], 4)
-
-
-def attend_backward_known(queries, key_part, value_part, chances, grad_mixture):
-    factor = 1.0 / math.sqrt(HEAD_DIM)
-    grad_values = jnp.einsum(
-        "bhqk,bqhd->bkhd", chances.astype(jnp.bfloat16), grad_mixture, preferred_element_type=jnp.float32
-    )
-    grad_chances = jnp.einsum(
-        "bqhd,bkhd->bhqk", grad_mixture, value_part, preferred_element_type=jnp.float32
-    )
-    grad_scores = (
-        chances * (grad_chances - jnp.sum(grad_chances * chances, -1, keepdims=True))
-    ).astype(jnp.bfloat16)
-    grad_queries = (
-        jnp.einsum("bhqk,bkhd->bqhd", grad_scores, key_part, preferred_element_type=jnp.float32)
-        * factor
-    )
-    grad_keys = (
-        jnp.einsum("bhqk,bqhd->bkhd", grad_scores, queries, preferred_element_type=jnp.float32)
-        * factor
-    )
-    return (grad_queries, grad_keys, grad_values)
-
-
-def block_backward_t(grad_result, weights, stored, attend_back):
-    first_gain, first_bias, project, output_t, second_gain, second_bias, expand, narrow_t = weights
-    inputs, normed, attend_stored, mixture, middle, second, lifted, hidden = stored
-    grad_branch = grad_result.astype(jnp.bfloat16)
-    grad_hidden = product(grad_branch, narrow_t)
-    grad_lifted = jax.vjp(smooth_gate, lifted)[1](grad_hidden)[0].astype(jnp.bfloat16)
-    grad_second = right_product(grad_lifted, expand)
-    pullback = jax.vjp(layer_norm, middle, second_gain, second_bias)[1]
-    grad_middle, grad_gain_two, grad_bias_two = pullback(grad_second)
-    grad_middle = grad_middle + grad_result
-    grad_attended = grad_middle.astype(jnp.bfloat16)
-    grad_mixture = product(grad_attended, output_t).astype(jnp.bfloat16)
-    grad_triple = attend_back(grad_mixture, attend_stored)
-    grad_normed = right_product(grad_triple, project)
-    pullback = jax.vjp(layer_norm, inputs, first_gain, first_bias)[1]
-    grad_inputs, grad_gain_one, grad_bias_one = pullback(grad_normed)
-    grad_inputs = grad_inputs + grad_middle
-    return (
-        grad_inputs,
-        (grad_gain_one, grad_bias_one, grad_gain_two, grad_bias_two),
-        [(normed, grad_triple), (grad_attended, mixture), (second, grad_lifted), (grad_branch, hidden)],
-    )
 
 
 def normalize(values):
@@ -1301,6 +1243,109 @@
     )(byte_rows, previous, cotangent, small, full)
 
 
+def coarse_kernel(grad_ref, embedded_ref, middle_ref, lifted_ref, triple, chances, small_ref, w_hbm, patch_hbm, bytes_hbm,
+                  branch_ref, lifted_grad_ref, low_ref, triple_grad_ref, embed_ref, vectors_ref, out_ref,
+                  w, patch, byte_grad, spread, mixed_ref, grad_second, sems):
+    bf = jnp.bfloat16
+    core = lax.axis_index("seq")
+    parts = ((8 * D, 4 * D), (4 * D, 4 * D), (3 * D, D), (0, 3 * D))
+    copies = [
+        pltpu.make_async_copy(w_hbm.at[:, pl.ds(*part)], w.at[:, pl.ds(*part)], sems.at[i]) for i, part in enumerate(parts)
+    ]
+    copies.append(pltpu.make_async_copy(patch_hbm, patch, sems.at[4]))
+    copies.append(pltpu.make_async_copy(bytes_hbm, byte_grad, sems.at[5]))
+    for copy in copies:
+        copy.start()
+    first_gain, second_gain = small_ref[0:1], small_ref[2:3]
+    branch = grad_ref[...].astype(bf)
+    branch_ref[...] = branch
+    unit_two, scale_two = normalize(middle_ref[...])
+    copies[0].wait()
+    copies[1].wait()
+    for j in range(4):
+        here = slice(j * D, j * D + D)
+        _, slope = gate_both(lifted_ref[:, here])
+        lifted_grad = (product(branch, w[:, 8 * D + j * D : 9 * D + j * D]) * slope).astype(bf)
+        lifted_grad_ref[:, here] = lifted_grad
+        term = right_product(lifted_grad, w[:, 4 * D + j * D : 5 * D + j * D])
+        if j:
+            grad_second[...] += term
+        else:
+            grad_second[...] = term
+    grad_two = grad_second[...]
+    grad_middle = grad_ref[...] + normalize_back(grad_two, unit_two, scale_two, second_gain)
+    low = grad_middle.astype(bf)
+    low_ref[...] = low
+    copies[2].wait()
+    mixed_ref[...] = product(low, w[:, 3 * D : 4 * D]).astype(bf)
+
+    def attend_back(pair, _):
+        lanes = [pl.ds(pl.multiple_of(i * D + pair * 128, 128), 128) for i in range(3)]
+        factor = 1.0 / math.sqrt(HEAD_DIM)
+        queries = head_lanes(triple[:, lanes[0]])
+        keys = head_lanes(triple[:, lanes[1]])
+        values = triple[:, lanes[2]]
+        mixed = head_lanes(mixed_ref[:, lanes[0]])
+        sums = [None, None, None]
+        for head in range(2):
+            found = chances[pair * 2 + head]
+            grad = right_product(mixed[head], values)
+            scores = (found * (grad - jnp.sum(grad * found, -1, keepdims=True))).astype(bf)
+            terms = (
+                product(scores, keys[head]),
+                left_product(scores, queries[head]),
+                left_product(found.astype(bf), mixed[head]),
+            )
+            sums = [t if s is None else s + t for s, t in zip(sums, terms)]
+        triple_grad_ref[:, lanes[0]] = (sums[0] * factor).astype(bf)
+        triple_grad_ref[:, lanes[1]] = (sums[1] * factor).astype(bf)
+        triple_grad_ref[:, lanes[2]] = sums[2].astype(bf)
+        return 0
+
+    lax.fori_loop(0, PAIRS, attend_back, 0)
+    copies[3].wait()
+    grad_one = right_product(triple_grad_ref[...], w[:, : 3 * D])
+    unit_one, scale_one = normalize(embedded_ref[...])
+    embed_ref[...] = (grad_middle + normalize_back(grad_one, unit_one, scale_one, first_gain)).astype(bf)
+    terms = [grad_one * unit_one, grad_one, grad_two * unit_two, grad_two]
+    vectors_ref[...] = jnp.concatenate([jnp.sum(t, 0, keepdims=True) for t in terms] + [jnp.zeros((4, D), jnp.float32)], 0)
+    patches = byte_grad.shape[0] // PATCH
+    rows = embed_ref[pl.ds(pl.multiple_of(core * patches, 128), patches)]
+    copies[4].wait()
+    copies[5].wait()
+    for i in range(PATCH):
+        term = right_product(rows, patch[i * D : i * D + D])
+        for j in range(D // 128):
+            spread[j, pl.ds(i, patches, stride=PATCH)] = term[:, j * 128 : j * 128 + 128]
+    for j in range(D // 128):
+        here = slice(j * 128, j * 128 + 128)
+        out_ref[:, here] = (byte_grad[:, here] + spread[j]).astype(bf)
+
+
+def coarse_block_back(grad, embedded, middle, lifted, triple, chances, small, full, patch, byte_grad):
+    count = grad.shape[0]
+    bf, f32 = jnp.bfloat16, jnp.float32
+    outs = [((count, D), bf), ((count, 4 * D), bf), ((count, D), bf), ((count, 3 * D), bf), ((count, D), bf), ((8, D), f32),
+            (byte_grad.shape, bf)]
+    return pl.pallas_call(
+        coarse_kernel,
+        out_shape=[jax.ShapeDtypeStruct(*out) for out in outs],
+        in_specs=[pl.BlockSpec(memory_space=VMEM)] * 7 + [pl.BlockSpec(memory_space=HBM)] * 3,
+        out_specs=[pl.BlockSpec(memory_space=VMEM)] * len(outs),
+        scratch_shapes=[
+            pltpu.VMEM(full.shape, bf),
+            pltpu.VMEM(patch.shape, bf),
+            pltpu.VMEM(byte_grad.shape, f32),
+            pltpu.VMEM((D // 128, byte_grad.shape[0], 128), f32),
+            pltpu.VMEM((count, D), bf),
+            pltpu.VMEM((count, D), f32),
+            pltpu.SemaphoreType.DMA((6,)),
+        ],
+        compiler_params=pltpu.CompilerParams(vmem_limit_bytes=64_000_000),
+        name="coarse_block_back",
+    )(grad, embedded, middle, lifted, triple, chances, small, full, patch, byte_grad)
+
+
 def solution(mesh):
     return jax.shard_map(
         fast_body if (mesh.shape["seq"], mesh.shape["fsdp"]) == (2, 16) else body,

time: 544 us -> 512 us (0.941)
  matrix products: 36.9 us -> 5.86 us
  Pallas kernels: 460 us -> 472 us
  local copies, waits for them, and re-layouts: 28.6 us -> 18.9 us
  other arithmetic: 10.8 us -> 2.52 us
    dot_general x9 -> x0, matrix products: 30.9 us -> none  [the longest x3 18.4 us: right_product(): lax.dot_general(left_side, right_side, (((1,), (1,)), ((), ())), preferre...]
    pallas_call x0 -> x1, Pallas kernels: none -> 22.9 us  [coarse_block_back(): pl.pallas_call(coarse_kernel, out_shape=[jax.ShapeDtypeStruct(*out) for o...]
    pallas_call x1, Pallas kernels: 98.5 us -> 87.7 us  [fine_block(): pl.pallas_call(fine_kernel, grid=(steps,), out_shape=[jax.ShapeDtypeStruc...]
where the time goes in v6:
time: 512 us; the launch traced here: 503 us
  Pallas kernels  472 us (92%)
  local copies, waits for them, and re-layouts  18.9 us (4%)
  matrix products  5.86 us (1%)
    pallas_call x1, Pallas kernels, reduce_all(): pl.pallas_call(kernel, out_shape=[jax.ShapeDtypeStruct(out, jnp.float32)...  187 us
    pallas_call x1, Pallas kernels, gather_all(): pl.pallas_call(functools.partial(gather_kernel, plan, ahead), out_shape=[...  175 us
    pallas_call x1, Pallas kernels, fine_block(): pl.pallas_call(fine_kernel, grid=(steps,), out_shape=[jax.ShapeDtypeStruc...  87.7 us
    pallas_call x1, Pallas kernels, coarse_block_back(): pl.pallas_call(coarse_kernel, out_shape=[jax.ShapeDtypeStruct(*out) for o...  22.9 us

profile of v6, /device:TPU:0, one launch (start us, length us, event | category | flops | bytes accessed | tf_op | source)
XLA Modules:
  0.0 502.9 jit_solution(9918463885817375711)
XLA Ops:
  0.7 0.8 stack.35
  1.8 3.6 reshape_squeeze.3.refs_10_
  5.3 0.8 copy.39.refs_12_
  6.1 174.6 %gather_all.1 = (bf16[4,4,384,768]{3,2,1,0:T(8,128)(2,1)}, bf16[4,4,48,9216]{3,2,1,0:T(8,128)(2,1)}, bf16[4,4,48,9216]{3,2,1,0:T(8,128)(2,1)}, f32[8,768]{1,0:T(...) custom-call(bf16[384,768]{1,0:T(8,128)(2,1)} %refs_0_.1, ...), custom_call_target="tpu_custom_call" | custom-call | tf_op jit(solution)/shard_map/gather_all/pallas_call | solution.py:689
  180.8 1.2 slice.65
  182.2 0.8 convert_multiply_fusion.previous_ref
  183.1 87.7 %fine_block.1 = (bf16[1024,768]{1,0:T(8,128)(2,1)}, f32[1024,768]{1,0:T(8,128)}, f32[128,768]{1,0:T(8,128)}, f32[8,768]{1,0:T(8,128)}, bf16[1024,768]{1,0:T(8,12...) custom-call(bf16[1024,768]{1,0:T(8,128)(2,1)} %bitcast.49, ...), custom_call_target="tpu_custom_call" | custom-call | tf_op jit(solution)/shard_map/fine_block/pallas_call | solution.py:1227
  270.8 2.8 all_gather.3
  273.8 1.0 concatenate.15.grad_ref
  274.8 22.9 %coarse_block_back.1 = (bf16[256,768]{1,0:T(8,128)(2,1)}, bf16[256,3072]{1,0:T(8,128)(2,1)}, bf16[256,768]{1,0:T(8,128)(2,1)}, bf16[256,2304]{1,0:T(8,128)(2,1)}...) custom-call(f32[256,768]{1,0:T(8,128)} %concatenate.15.grad_ref, ...), custom_call_target="tpu_custom_call" | custom-call | tf_op jit(solution)/shard_map/coarse_block_back/pallas_call | solution.py:1330
  297.7 1.4 multiply_add_fusion.refs_17_
  299.1 5.9 %convolution_convert_fusion = bf16[6144,384]{1,0:T(8,128)(2,1)} fusion(bf16[256,6144]{1,0:T(8,128)(2,1)} %bitcast.50, bf16[256,768]{1,0:T(8,128)(2,1)} %get-tuple-element.77, s32[]{:T(128)S(6)} %select_n.12), kind=kOutput, calls=%fused_computation | convolution fusion | flops 1210318848 | bytes 8060932 | tf_op jit(solution)/shard_map/dot_general | solution.py:42
  304.9 186.6 %reduce_all.1 = (f32[384,768]{1,0:T(8,128)}, f32[48,2304]{1,0:T(8,128)}, f32[48,768]{1,0:T(8,128)}, f32[48,3072]{1,0:T(8,128)}, f32[48,3072]{1,0:T(8,128)}, /*in...) custom-call(bf16[4,4,384,384]{3,2,1,0:T(8,128)(2,1)} %bitcast.43, ...), custom_call_target="tpu_custom_call" | custom-call | tf_op jit(solution)/shard_map/reduce_all/pallas_call | solution.py:1004
  491.5 0.9 constant_dynamic-slice_fusion
  492.4 0.5 slice_bitcast_fusion
  493.0 2.4 copy.50
  495.4 1.9 copy.51
  497.3 0.7 copy.52
  498.0 0.8 copy.53
  498.8 0.8 copy.54
  499.6 0.8 copy.55
  500.4 0.7 copy.56
  501.0 0.8 copy.57
  501.8 0.8 copy.58
  (30 shorter events, 0.8 us)
Async XLA Ops:
  0.7 4.7 copy-start.9
  1.7 4.4 copy-start.7
  5.3 176.6 %copy-start.10 = (s32[1,256]{1,0:T(1,128)S(1)}, s32[1,256]{1,0:T(1,128)}, u32[]{:S(2)}) copy-start(s32[1,256]{1,0:T(1,128)} %refs_11_.1) | copy-start | bytes 3076
  274.8 22.9 %copy-start.8 = (f32[8,768]{1,0:T(8,128)S(1)}, f32[8,768]{1,0:T(8,128)}, u32[]{:S(2)}) copy-start(f32[8,768]{1,0:T(8,128)} %get-tuple-element.94) | copy-start | bytes 73732
  491.5 5.8 %copy-start.6 = (f32[48,768]{1,0:T(8,128)S(1)}, f32[48,768]{1,0:T(8,128)}, u32[]{:S(2)}) copy-start(f32[48,768]{1,0:T(8,128)} %get-tuple-element.98) | copy-start | bytes 442372
  491.5 6.4 %copy-start.3 = (f32[48,3072]{1,0:T(8,128)S(1)}, f32[48,3072]{1,0:T(8,128)}, u32[]{:S(2)}) copy-start(f32[48,3072]{1,0:T(8,128)} %get-tuple-element.141) | copy-start | bytes 1769476
  491.5 7.3 %copy-start.2 = (f32[48,3072]{1,0:T(8,128)S(1)}, f32[48,3072]{1,0:T(8,128)}, u32[]{:S(2)}) copy-start(f32[48,3072]{1,0:T(8,128)} %get-tuple-element.100) | copy-start | bytes 1769476
  491.5 8.1 %copy-start.4 = (f32[48,2304]{1,0:T(8,128)S(1)}, f32[48,2304]{1,0:T(8,128)}, u32[]{:S(2)}) copy-start(f32[48,2304]{1,0:T(8,128)} %get-tuple-element.145) | copy-start | bytes 1327108
  493.0 7.4 %copy-start.5 = (f32[48,768]{1,0:T(8,128)S(1)}, f32[48,768]{1,0:T(8,128)}, u32[]{:S(2)}) copy-start(f32[48,768]{1,0:T(8,128)} %get-tuple-element.102) | copy-start | bytes 442372
  493.0 8.0 %copy-start.1 = (f32[48,3072]{1,0:T(8,128)S(1)}, f32[48,3072]{1,0:T(8,128)}, u32[]{:S(2)}) copy-start(f32[48,3072]{1,0:T(8,128)} %get-tuple-element.149) | copy-start | bytes 1769476
  495.4 6.4 %copy-start = (f32[48,3072]{1,0:T(8,128)S(1)}, f32[48,3072]{1,0:T(8,128)}, u32[]{:S(2)}) copy-start(f32[48,3072]{1,0:T(8,128)} %get-tuple-element.104) | copy-start | bytes 1769476

commit v7 on v6

--- a/solution.py
+++ b/solution.py
@@ -949,12 +949,12 @@
 
     load(0)
     for t in range(n + LAGS[-1]):
-        if t + 1 < n:
-            load(t + 1)
         if t < n:
             if t in copies:
                 copies[t].wait()
             reduces[t].one()
+        if t + 1 < n:
+            load(t + 1)
         for lag, name in zip(LAGS, ("two", "three", "four", "five")):
             if 0 <= t - lag < n:
                 getattr(reduces[t - lag], name)()

time: 512 us -> 508 us (level)
  no operation moved by 1% of the time
where the time goes in v7:
time: 508 us; the launch traced here: 499 us
  Pallas kernels  468 us (92%)
  local copies, waits for them, and re-layouts  18.9 us (4%)
  matrix products  5.86 us (1%)
    pallas_call x1, Pallas kernels, reduce_all(): pl.pallas_call(kernel, out_shape=[jax.ShapeDtypeStruct(out, jnp.float32)...  183 us
    pallas_call x1, Pallas kernels, gather_all(): pl.pallas_call(functools.partial(gather_kernel, plan, ahead), out_shape=[...  175 us
    pallas_call x1, Pallas kernels, fine_block(): pl.pallas_call(fine_kernel, grid=(steps,), out_shape=[jax.ShapeDtypeStruc...  87.7 us
    pallas_call x1, Pallas kernels, coarse_block_back(): pl.pallas_call(coarse_kernel, out_shape=[jax.ShapeDtypeStruct(*out) for o...  22.9 us

profile of v7, /device:TPU:0, one launch (start us, length us, event | category | flops | bytes accessed | tf_op | source)
XLA Modules:
  0.0 499.3 jit_solution(9684337064836589464)
XLA Ops:
  0.7 0.8 stack.35
  1.8 3.6 reshape_squeeze.3.refs_10_
  5.3 0.8 copy.39.refs_12_
  6.1 174.6 %gather_all.1 = (bf16[4,4,384,768]{3,2,1,0:T(8,128)(2,1)}, bf16[4,4,48,9216]{3,2,1,0:T(8,128)(2,1)}, bf16[4,4,48,9216]{3,2,1,0:T(8,128)(2,1)}, f32[8,768]{1,0:T(...) custom-call(bf16[384,768]{1,0:T(8,128)(2,1)} %refs_0_.1, ...), custom_call_target="tpu_custom_call" | custom-call | tf_op jit(solution)/shard_map/gather_all/pallas_call | solution.py:689
  180.8 1.2 slice.65
  182.2 0.8 convert_multiply_fusion.previous_ref
  183.1 87.7 %fine_block.1 = (bf16[1024,768]{1,0:T(8,128)(2,1)}, f32[1024,768]{1,0:T(8,128)}, f32[128,768]{1,0:T(8,128)}, f32[8,768]{1,0:T(8,128)}, bf16[1024,768]{1,0:T(8,12...) custom-call(bf16[1024,768]{1,0:T(8,128)(2,1)} %bitcast.49, ...), custom_call_target="tpu_custom_call" | custom-call | tf_op jit(solution)/shard_map/fine_block/pallas_call | solution.py:1227
  270.8 2.8 all_gather.3
  273.8 1.0 concatenate.15.grad_ref
  274.8 22.9 %coarse_block_back.1 = (bf16[256,768]{1,0:T(8,128)(2,1)}, bf16[256,3072]{1,0:T(8,128)(2,1)}, bf16[256,768]{1,0:T(8,128)(2,1)}, bf16[256,2304]{1,0:T(8,128)(2,1)}...) custom-call(f32[256,768]{1,0:T(8,128)} %concatenate.15.grad_ref, ...), custom_call_target="tpu_custom_call" | custom-call | tf_op jit(solution)/shard_map/coarse_block_back/pallas_call | solution.py:1330
  297.7 1.4 multiply_add_fusion.refs_17_
  299.1 5.9 %convolution_convert_fusion = bf16[6144,384]{1,0:T(8,128)(2,1)} fusion(bf16[256,6144]{1,0:T(8,128)(2,1)} %bitcast.50, bf16[256,768]{1,0:T(8,128)(2,1)} %get-tuple-element.77, s32[]{:T(128)S(6)} %select_n.12), kind=kOutput, calls=%fused_computation | convolution fusion | flops 1210318848 | bytes 8060932 | tf_op jit(solution)/shard_map/dot_general | solution.py:42
  304.9 183.0 %reduce_all.1 = (f32[384,768]{1,0:T(8,128)}, f32[48,2304]{1,0:T(8,128)}, f32[48,768]{1,0:T(8,128)}, f32[48,3072]{1,0:T(8,128)}, f32[48,3072]{1,0:T(8,128)}, /*in...) custom-call(bf16[4,4,384,384]{3,2,1,0:T(8,128)(2,1)} %bitcast.43, ...), custom_call_target="tpu_custom_call" | custom-call | tf_op jit(solution)/shard_map/reduce_all/pallas_call | solution.py:1004
  488.0 0.9 constant_dynamic-slice_fusion
  488.9 0.5 slice_bitcast_fusion
  489.5 2.4 copy.50
  491.9 1.9 copy.51
  493.8 0.7 copy.52
  494.4 0.8 copy.53
  495.2 0.8 copy.54
  496.1 0.8 copy.55
  496.8 0.7 copy.56
  497.5 0.8 copy.57
  498.3 0.8 copy.58
  (30 shorter events, 0.8 us)
Async XLA Ops:
  0.7 4.7 copy-start.9
  1.7 4.4 copy-start.7
  5.3 176.6 %copy-start.10 = (s32[1,256]{1,0:T(1,128)S(1)}, s32[1,256]{1,0:T(1,128)}, u32[]{:S(2)}) copy-start(s32[1,256]{1,0:T(1,128)} %refs_11_.1) | copy-start | bytes 3076
  274.8 22.9 %copy-start.8 = (f32[8,768]{1,0:T(8,128)S(1)}, f32[8,768]{1,0:T(8,128)}, u32[]{:S(2)}) copy-start(f32[8,768]{1,0:T(8,128)} %get-tuple-element.94) | copy-start | bytes 73732
  488.0 5.8 %copy-start.6 = (f32[48,768]{1,0:T(8,128)S(1)}, f32[48,768]{1,0:T(8,128)}, u32[]{:S(2)}) copy-start(f32[48,768]{1,0:T(8,128)} %get-tuple-element.98) | copy-start | bytes 442372
  488.0 6.4 %copy-start.3 = (f32[48,3072]{1,0:T(8,128)S(1)}, f32[48,3072]{1,0:T(8,128)}, u32[]{:S(2)}) copy-start(f32[48,3072]{1,0:T(8,128)} %get-tuple-element.141) | copy-start | bytes 1769476
  488.0 7.3 %copy-start.2 = (f32[48,3072]{1,0:T(8,128)S(1)}, f32[48,3072]{1,0:T(8,128)}, u32[]{:S(2)}) copy-start(f32[48,3072]{1,0:T(8,128)} %get-tuple-element.100) | copy-start | bytes 1769476
  488.0 8.1 %copy-start.4 = (f32[48,2304]{1,0:T(8,128)S(1)}, f32[48,2304]{1,0:T(8,128)}, u32[]{:S(2)}) copy-start(f32[48,2304]{1,0:T(8,128)} %get-tuple-element.145) | copy-start | bytes 1327108
  489.4 7.4 %copy-start.5 = (f32[48,768]{1,0:T(8,128)S(1)}, f32[48,768]{1,0:T(8,128)}, u32[]{:S(2)}) copy-start(f32[48,768]{1,0:T(8,128)} %get-tuple-element.102) | copy-start | bytes 442372
  489.4 8.0 %copy-start.1 = (f32[48,3072]{1,0:T(8,128)S(1)}, f32[48,3072]{1,0:T(8,128)}, u32[]{:S(2)}) copy-start(f32[48,3072]{1,0:T(8,128)} %get-tuple-element.149) | copy-start | bytes 1769476
  491.9 6.4 %copy-start = (f32[48,3072]{1,0:T(8,128)S(1)}, f32[48,3072]{1,0:T(8,128)}, u32[]{:S(2)}) copy-start(f32[48,3072]{1,0:T(8,128)} %get-tuple-element.104) | copy-start | bytes 1769476
